TPU v7x, 32 devices: a whole 2x2x4 slice. The times are simulated.
32 devices in a mesh: atoms: 16 (over z, y, x), bricks: 2 (over core).
Axes of the slice: x: 2, y: 2, z: 4, core: 2. Of those that a mesh axis runs over, the one named last changes fastest.
Arguments:
- orbitals: bfloat16 [32, 32, 32, 32], P('atoms'), may hold values from -6 to 6
- offsets: int32 [32, 3], P('atoms'), may hold values from 0 to 224, as said below
- kernel: float32 [32, 6], P(('atoms', 'bricks')), may hold values from -3 to 3
- pattern: int32 [32, 6], P(('atoms', 'bricks')), may hold values 0 or 1
- local_potential: float32 [512, 64, 256], P('atoms', None, 'bricks'), may hold values from -1 to 1
Outputs:
- density: float32 [512, 64, 256], P('atoms', None, 'bricks')
- gradient: bfloat16 [32, 32, 32, 32], P(('atoms', 'bricks'))
Inputs may be any that keep to these rules, and one draw needn't show every extreme that they name: offsets[a,0] lies in 0..31, offsets[a,1] in 0..32, offsets[a,2] in 0..224.
All inputs are finite; a program needn't handle non-finite values. No bound on the sum of `pattern` on one device may be relied on, other than what follows from the above.
Results may differ from a plain program's by a relative error of at most 0.0049.
Values may be sent and summed in bfloat16 or wider, within the bound.
No kernel may reach another device: no remote copies, remote signals or barrier semaphores. Data moves between devices by JAX's collectives and lax.ppermute only.
A program may use at most 64 MiB of HBM per device.

v0:
```python
import jax
import jax.numpy as jnp
from jax import lax
from jax.sharding import PartitionSpec as P


def padded_2(x, sides, width):
    for axis, dim in sides:
        devices, length = (lax.axis_size(axis), x.shape[dim])
        up = [(i, (i + 1) % devices) for i in range(devices)]
        down = [(j, i) for i, j in up]
        last = lax.slice_in_dim(x, length - width, length, axis=dim)
        leading = lax.slice_in_dim(x, 0, width, axis=dim)
        before = lax.ppermute(last, axis, up)
        after = lax.ppermute(leading, axis, down)
        x = jnp.concatenate([before, x, after], axis=dim)
    return x


def from_behind(x, axis, by):
    devices = lax.axis_size(axis)
    return lax.ppermute(x, axis, [(i, (i + by) % devices) for i in range(devices)])


def cut_window(padded, move, box_side):
    start = box_side - move
    return lax.dynamic_slice(padded, (start[0], start[1], start[2]), (box_side, box_side, box_side))


def local(orbitals, offsets, kernel, pattern, local_potential):
    orbs_domain = orbitals.shape[0]
    box_side = orbitals.shape[1]
    owned_count = kernel.shape[0]
    pieces = lax.axis_size("bricks")
    core_index = lax.axis_index("bricks")
    nearby, nearby_offsets = (
        padded_2(orbitals, (("atoms", 0),), orbs_domain),
        padded_2(offsets, (("atoms", 0),), orbs_domain),
    )
    own_offsets = lax.dynamic_slice_in_dim(offsets, core_index * owned_count, owned_count, 0)
    own_orbitals = lax.dynamic_slice_in_dim(orbitals, core_index * owned_count, owned_count, 0)
    shell_shift = (jnp.arange(3 * orbs_domain, dtype=jnp.int32) // orbs_domain - 1) * box_side
    displace = nearby_offsets[None, :, :] - own_offsets[:, None, :]
    displace = jnp.concatenate(
        [displace[:, :, :1] + shell_shift[None, :, None], displace[:, :, 1:]], 2
    )
    displace = jnp.clip(displace, -box_side, box_side).astype(jnp.int32)
    weights = kernel * pattern.astype(jnp.float32)
    mixed = jnp.zeros((owned_count, box_side, box_side, box_side), jnp.float32)
    cut_partners = jax.vmap(cut_window, in_axes=(0, 0, None))
    cut_all = jax.vmap(cut_partners, in_axes=(None, 0, None))
    for shell in range(3):
        group = nearby[shell * orbs_domain : (shell + 1) * orbs_domain]
        padded = jnp.pad(
            group, ((0, 0), (box_side, box_side), (box_side, box_side), (box_side, box_side))
        )
        moves = displace[:, shell * orbs_domain : (shell + 1) * orbs_domain, :]
        windows = cut_all(padded, moves, box_side)
        weight = weights[:, shell * orbs_domain : (shell + 1) * orbs_domain]
        mixed = mixed + jnp.sum(weight[:, :, None, None, None] * windows.astype(jnp.float32), 1)
    depth = local_potential.shape[1]
    full_z = pieces * local_potential.shape[2]
    products = own_orbitals.astype(jnp.float32) * mixed
    slab = jnp.zeros((2 * box_side, depth, full_z), jnp.float32)
    item = 0
    corner = own_offsets[item]
    spot = (corner[0], corner[1], corner[2])
    slab = lax.dynamic_update_slice(slab, products[item], spot)
    summed = lax.psum_scatter(slab, "bricks", scatter_dimension=2, tiled=True)
    incoming = from_behind(summed[box_side:].astype(jnp.bfloat16), "atoms", 1).astype(jnp.float32)
    density = summed[:box_side] + incoming
    potential = (local_potential + density * lax.rsqrt(1.0 + density * density)).astype(
        jnp.bfloat16
    )
    following = from_behind(potential, "atoms", -1)
    extended = lax.all_gather(
        jnp.concatenate([potential, following], 0), "bricks", axis=2, tiled=True
    )
    item = 0
    corner = own_offsets[item]
    window = lax.dynamic_slice(
        extended, (corner[0], corner[1], corner[2]), (box_side, box_side, box_side)
    )
    results = [(2.0 * window.astype(jnp.float32) * mixed[item]).astype(jnp.bfloat16)]
    return (density, jnp.stack(results, 0))


def solution(mesh):
    return jax.shard_map(
        local,
        mesh=mesh,
        in_specs=(
            P("atoms", None, None, None),
            P("atoms", None),
            P(("atoms", "bricks"), None),
            P(("atoms", "bricks"), None),
            P("atoms", None, "bricks"),
        ),
        out_specs=(P("atoms", None, "bricks"), P(("atoms", "bricks"), None, None, None)),
        check_vma=False,
    )
```

profile of v0, /device:TPU:0, one launch (start us, length us, event | category | flops | bytes accessed | tf_op | source)
XLA Modules:
  0.0 147.5 jit_solution(9425104326792939022)
XLA Ops:
  7.2 3.0 %collective-permute-start.1 = (s32[2,3]{1,0:T(2,128)}, s32[2,3]{1,0:T(2,128)S(1)}, u32[]{:S(2)}, u32[]{:S(2)}) collective-permute-start(s32[2,3]{1,0:T(2,128)} %param.6), channel_id=1, source_target_pairs={{0,2},{2,4},{4,6},{6,8},{8,10},{10,12},{12,14},{14,16},{16,18},{18... | collective-permute-start | bytes 80 | tf_op jit(solution)/shard_map/ppermute | solution.py:14
  10.2 4.1 %collective-permute-start.2 = (s32[2,3]{1,0:T(2,128)}, s32[2,3]{1,0:T(2,128)S(1)}, u32[]{:S(2)}, u32[]{:S(2)}) collective-permute-start(s32[2,3]{1,0:T(2,128)} %param.6), channel_id=1, source_target_pairs={{2,0},{4,2},{6,4},{8,6},{10,8},{12,10},{14,12},{16,14},{18,16},{20... | collective-permute-start | bytes 80 | tf_op jit(solution)/shard_map/ppermute | solution.py:15
  14.3 2.0 %collective-permute-start.3 = (bf16[2,32,32,32]{3,2,1,0:T(8,128)(2,1)}, bf16[2,32,32,32]{3,2,1,0:T(8,128)(2,1)S(1)}, u32[]{:S(2)}, u32[]{:S(2)}) collective-permute-start(bf16[2,32,32,32]{3,2,1,0:T(8,128)(2,1)} %param.5), channel_id=1, source_target_pairs={{2,0},{4,2},{6,4},{8,6},{10,8},{12,10},{14,12},{16,14},{18,16},{20... | collective-permute-start | bytes 393224 | tf_op jit(solution)/shard_map/ppermute | solution.py:15
  16.3 0.7 fusion.12
  17.0 0.7 constant_dynamic-slice_fusion.3
  17.7 0.6 fusion.11
  20.6 0.8 copy.8
  21.4 0.7 convert_multiply_fusion.3
  22.1 3.9 %pad.11 = bf16[2,96,96,96]{3,2,1,0:T(8,128)(2,1)} pad(bf16[2,32,32,32]{3,2,1,0:T(8,128)(2,1)} %param.5, bf16[]{:T(256)} %constant.18.clone.1), padding=0_0x32_32x32_32x32_32 | pad | bytes 3670018 | tf_op jit(solution)/shard_map/jit(_pad)/pad | solution.py:54
  29.0 0.1 copy.7
  29.1 0.1 copy.9
  29.2 0.1 add_subtract_fusion
  29.4 0.1 copy.12
  29.5 0.1 copy.10
  29.6 0.1 copy.11
  29.8 8.6 %while.4 = (s32[]{:T(128)}, bf16[2,96,96,96]{3,2,1,0:T(8,128)(2,1)}, s32[2,4]{1,0:T(2,128)S(1)}, bf16[2,32,32,32]{3,2,1,0:T(8,128)(2,1)S(1)}, s32[]{:T(128)}) while((s32[]{:T(128)}, bf16[2,96,96,96]{3,2,1,0:T(8,128)(2,1)}, s32[2,4]{1,0:T(2,128)S(1)}, bf16[2,32,32,32]{3,2,1,0:T(8,128)(2,1)S(1)}, s32[]{:T(128)}) %tuple.90), condition=%wide.while_cond.1, body=%wide.while_body.1.sunk | while | flops 2 | bytes 327829 | solution.py:27
  29.8 0.7 fusion.17
  30.5 3.6 %dynamic-slice_dynamic-update-slice_fusion.7 = bf16[2,32,32,32]{3,2,1,0:T(8,128)(2,1)S(1)} fusion(bf16[2,32,32,32]{3,2,1,0:T(8,128)(2,1)S(1)} %get-tuple-element.225, s32[]{:T(128)} %get-tuple-element.222, bf16[2,96,96,96]{3,2,1,0:T(8,128)(2,1)} %get-tuple-element.228, s32[]{:T(128)} %bitcast.62, s32[]{:T(128)} %bitcast.63, s32[]{:T(128)} %bitcast.64, ...), kind=kLoop, calls=%fused_computation.2.clone.1 | loop fusion | bytes 327700 | tf_op jit(solution)/shard_map/vmap(vmap())/gather
  34.1 0.7 fusion.17
  34.8 3.6 %dynamic-slice_dynamic-update-slice_fusion.7 = bf16[2,32,32,32]{3,2,1,0:T(8,128)(2,1)S(1)} fusion(bf16[2,32,32,32]{3,2,1,0:T(8,128)(2,1)S(1)} %get-tuple-element.225, s32[]{:T(128)} %get-tuple-element.222, bf16[2,96,96,96]{3,2,1,0:T(8,128)(2,1)} %get-tuple-element.228, s32[]{:T(128)} %bitcast.62, s32[]{:T(128)} %bitcast.63, s32[]{:T(128)} %bitcast.64, ...), kind=kLoop, calls=%fused_computation.2.clone.1 | loop fusion | bytes 327700 | tf_op jit(solution)/shard_map/vmap(vmap())/gather
  38.4 0.2 fusion.1
  38.6 2.8 %pad.12 = bf16[2,96,96,96]{3,2,1,0:T(8,128)(2,1)} pad(bf16[2,32,32,32]{3,2,1,0:T(8,128)(2,1)S(1)} %collective-permute-done.3, bf16[]{:T(256)} %constant.18.clone.1), padding=0_0x32_32x32_32x32_32 | pad | bytes 3670018 | tf_op jit(solution)/shard_map/jit(_pad)/pad | solution.py:54
  41.5 8.4 %while.5 = (s32[]{:T(128)}, bf16[2,96,96,96]{3,2,1,0:T(8,128)(2,1)}, s32[2,4]{1,0:T(2,128)S(1)}, bf16[2,32,32,32]{3,2,1,0:T(8,128)(2,1)S(1)}, s32[]{:T(128)}) while((s32[]{:T(128)}, bf16[2,96,96,96]{3,2,1,0:T(8,128)(2,1)}, s32[2,4]{1,0:T(2,128)S(1)}, bf16[2,32,32,32]{3,2,1,0:T(8,128)(2,1)S(1)}, s32[]{:T(128)}) %tuple.89), condition=%wide.while_cond.2, body=%wide.while_body.2.sunk | while | flops 2 | bytes 327829 | solution.py:27
  41.6 0.6 fusion.18
  42.2 3.5 %dynamic-slice_dynamic-update-slice_fusion.8 = bf16[2,32,32,32]{3,2,1,0:T(8,128)(2,1)S(1)} fusion(bf16[2,32,32,32]{3,2,1,0:T(8,128)(2,1)S(1)} %get-tuple-element.195, s32[]{:T(128)} %get-tuple-element.192, bf16[2,96,96,96]{3,2,1,0:T(8,128)(2,1)} %get-tuple-element.198, s32[]{:T(128)} %bitcast.66, s32[]{:T(128)} %bitcast.67, s32[]{:T(128)} %bitcast.68, ...), kind=kLoop, calls=%fused_computation.4.clone.1 | loop fusion | bytes 327700 | tf_op jit(solution)/shard_map/vmap(vmap())/gather
  45.8 0.6 fusion.18
  46.4 3.5 %dynamic-slice_dynamic-update-slice_fusion.8 = bf16[2,32,32,32]{3,2,1,0:T(8,128)(2,1)S(1)} fusion(bf16[2,32,32,32]{3,2,1,0:T(8,128)(2,1)S(1)} %get-tuple-element.195, s32[]{:T(128)} %get-tuple-element.192, bf16[2,96,96,96]{3,2,1,0:T(8,128)(2,1)} %get-tuple-element.198, s32[]{:T(128)} %bitcast.66, s32[]{:T(128)} %bitcast.67, s32[]{:T(128)} %bitcast.68, ...), kind=kLoop, calls=%fused_computation.4.clone.1 | loop fusion | bytes 327700 | tf_op jit(solution)/shard_map/vmap(vmap())/gather
  50.0 2.8 %pad.10 = bf16[2,96,96,96]{3,2,1,0:T(8,128)(2,1)} pad(bf16[2,32,32,32]{3,2,1,0:T(8,128)(2,1)S(1)} %collective-permute-done, bf16[]{:T(256)} %constant.18.clone.1), padding=0_0x32_32x32_32x32_32 | pad | bytes 3670018 | tf_op jit(solution)/shard_map/jit(_pad)/pad | solution.py:54
  52.9 8.6 %while.3 = (s32[]{:T(128)}, bf16[2,96,96,96]{3,2,1,0:T(8,128)(2,1)}, s32[2,4]{1,0:T(2,128)S(1)}, bf16[2,32,32,32]{3,2,1,0:T(8,128)(2,1)S(1)}, s32[]{:T(128)}) while((s32[]{:T(128)}, bf16[2,96,96,96]{3,2,1,0:T(8,128)(2,1)}, s32[2,4]{1,0:T(2,128)S(1)}, bf16[2,32,32,32]{3,2,1,0:T(8,128)(2,1)S(1)}, s32[]{:T(128)}) %tuple.88), condition=%wide.while_cond, body=%wide.while_body.sunk | while | flops 2 | bytes 327829 | solution.py:27
  53.0 0.6 fusion.16
  53.6 3.6 %dynamic-slice_dynamic-update-slice_fusion.6 = bf16[2,32,32,32]{3,2,1,0:T(8,128)(2,1)S(1)} fusion(bf16[2,32,32,32]{3,2,1,0:T(8,128)(2,1)S(1)} %get-tuple-element.210, s32[]{:T(128)} %get-tuple-element.207, bf16[2,96,96,96]{3,2,1,0:T(8,128)(2,1)} %get-tuple-element.213, s32[]{:T(128)} %bitcast.58, s32[]{:T(128)} %bitcast.59, s32[]{:T(128)} %bitcast.60, ...), kind=kLoop, calls=%fused_computation.clone.1 | loop fusion | bytes 327700 | tf_op jit(solution)/shard_map/vmap(vmap())/gather
  57.3 0.6 fusion.16
  57.9 3.6 %dynamic-slice_dynamic-update-slice_fusion.6 = bf16[2,32,32,32]{3,2,1,0:T(8,128)(2,1)S(1)} fusion(bf16[2,32,32,32]{3,2,1,0:T(8,128)(2,1)S(1)} %get-tuple-element.210, s32[]{:T(128)} %get-tuple-element.207, bf16[2,96,96,96]{3,2,1,0:T(8,128)(2,1)} %get-tuple-element.213, s32[]{:T(128)} %bitcast.58, s32[]{:T(128)} %bitcast.59, s32[]{:T(128)} %bitcast.60, ...), kind=kLoop, calls=%fused_computation.clone.1 | loop fusion | bytes 327700 | tf_op jit(solution)/shard_map/vmap(vmap())/gather
  61.6 0.2 fusion
  61.8 0.2 fusion.2
  62.0 0.2 fusion.3
  62.2 2.5 %broadcast_in_dim.2 = f32[64,64,256]{2,1,0:T(8,128)} broadcast(f32[]{:T(128)} %constant.14.clone.1), dimensions={} | broadcast | bytes 4194308 | tf_op jit(solution)/shard_map/broadcast_in_dim | solution.py:64
  64.7 13.9 %dynamic_update_slice.3 = f32[64,64,256]{2,1,0:T(8,128)} dynamic-update-slice(f32[64,64,256]{2,1,0:T(8,128)} %broadcast_in_dim.2, f32[32,32,32]{2,1,0:T(8,128)S(1)} %fusion.3, s32[]{:T(128)S(6)} %select_n.93, s32[]{:T(128)S(6)} %select_n.94, s32[]{:T(128)S(6)} %select_n.95) | dynamic-update-slice | bytes 262148 | tf_op jit(solution)/shard_map/dynamic_update_slice | solution.py:68
  78.7 12.6 %reduce-scatter.2.cloned.1.call-done = f32[64,64,128]{2,1,0:T(8,128)} async-done(((f32[64,64,256]{2,1,0:T(8,128)}), f32[64,64,128]{2,1,0:T(8,128)}) %reduce-scatter.2.cloned.1.call-update) | async-done | bytes 2097168 | tf_op jit(solution)/shard_map/reduce_scatter | solution.py:69
  91.3 1.3 slice.183
  92.6 1.9 %collective-permute-start.4 = (bf16[32,64,128]{2,1,0:T(8,128)(2,1)S(1)}, bf16[32,64,128]{2,1,0:T(8,128)(2,1)S(1)}, u32[]{:S(2)}, u32[]{:S(2)}) collective-permute-start(bf16[32,64,128]{2,1,0:T(8,128)(2,1)S(1)} %slice.183), channel_id=1, source_target_pairs={{0,2},{2,4},{4,6},{6,8},{8,10},{10,12},{12,14},{14,16},{16,18},{18... | collective-permute-start | bytes 1572872 | tf_op jit(solution)/shard_map/ppermute | solution.py:22
  94.5 15.9 %collective-permute-done.4 = bf16[32,64,128]{2,1,0:T(8,128)(2,1)S(1)} collective-permute-done((bf16[32,64,128]{2,1,0:T(8,128)(2,1)S(1)}, bf16[32,64,128]{2,1,0:T(8,128)(2,1)S(1)}, u32[]{:S(2)}, u32[]{:S(2)}) %collective-permute-start.4) | collective-permute-done | bytes 524320 | tf_op jit(solution)/shard_map/ppermute | solution.py:22
  110.4 2.5 %add_convert_fusion = (bf16[32,64,128]{2,1,0:T(8,128)(2,1)S(1)}, f32[32,64,128]{2,1,0:T(8,128)}) fusion(f32[32,64,128]{2,1,0:T(8,128)S(1)} %copy-done.1, bf16[32,64,128]{2,1,0:T(8,128)(2,1)S(1)} %collective-permute-done.4, f32[64,64,128]{2,1,0:T(8,128)} %reduce-scatter.2.cloned.1.call-done), kind=kLoop, calls=%fused_computation.15 | loop fusion | flops 1835008 | bytes 4194304 | tf_op jit(solution)/shard_map/convert_element_type | solution.py:72
  112.9 1.7 %collective-permute-start.5 = (bf16[32,64,128]{2,1,0:T(8,128)(2,1)S(1)}, bf16[32,64,128]{2,1,0:T(8,128)(2,1)S(1)}, u32[]{:S(2)}, u32[]{:S(2)}) collective-permute-start(bf16[32,64,128]{2,1,0:T(8,128)(2,1)S(1)} %get-tuple-element.50), channel_id=1, source_target_pairs={{0,30},{2,0},{4,2},{6,4},{8,6},{10,8},{12,10},{14,12},{16,14},{18,... | collective-permute-start | bytes 1572872 | tf_op jit(solution)/shard_map/ppermute | solution.py:22
  114.7 11.6 %collective-permute-done.5 = bf16[32,64,128]{2,1,0:T(8,128)(2,1)S(1)} collective-permute-done((bf16[32,64,128]{2,1,0:T(8,128)(2,1)S(1)}, bf16[32,64,128]{2,1,0:T(8,128)(2,1)S(1)}, u32[]{:S(2)}, u32[]{:S(2)}) %collective-permute-start.5) | collective-permute-done | bytes 524320 | tf_op jit(solution)/shard_map/ppermute | solution.py:22
  126.2 1.1 pad_maximum_fusion
  127.3 11.2 %all-gather.2.cloned.1.call-done = bf16[64,64,256]{2,1,0:T(8,128)(2,1)} async-done(((bf16[64,64,128]{2,1,0:T(8,128)(2,1)}), bf16[64,64,256]{2,1,0:T(8,128)(2,1)}) %all-gather.2.cloned.1.call-update) | async-done | bytes 2097168 | tf_op jit(solution)/shard_map/all_gather | solution.py:76
  138.5 2.2 %fusion.4 = bf16[1,32,32,32]{3,2,1,0:T(8,128)(2,1)} fusion(bf16[64,64,256]{2,1,0:T(8,128)(2,1)} %all-gather.2.cloned.1.call-done, s32[]{:T(128)S(6)} %select_n.93, s32[]{:T(128)S(6)} %select_n.94, s32[]{:T(128)S(6)} %select_n.95, f32[32,32,32]{2,1,0:T(8,128)S(1)} %fusion, f32[32,32,32]{2,1,0:T(8,128)S(1)} %fusion.2, f32[32,32,32]{2,1,0:T(8,128)S(1)} %fusion.1), kind=kLoop, calls=%fused_computation.20 | loop fusion | flops 196608 | bytes 524300 | tf_op jit(solution)/shard_map/stack | solution.py:85
  (31 shorter events, 0.7 us)
Async XLA Ops:
  7.2 84.1 %reduce-scatter.2.cloned.1.call-start = ((), (), s32[]{:S(2)}) async-start(), calls=%async_computation.1 | async-start | bytes 6291456 | tf_op jit(solution)/shard_map/reduce_scatter | solution.py:69
  7.2 21.8 %collective-permute-start.1 = (s32[2,3]{1,0:T(2,128)}, s32[2,3]{1,0:T(2,128)S(1)}, u32[]{:S(2)}, u32[]{:S(2)}) collective-permute-start(s32[2,3]{1,0:T(2,128)} %param.6), channel_id=1, source_target_pairs={{0,2},{2,4},{4,6},{6,8},{8,10},{10,12},{12,14},{14,16},{16,18},{18... | collective-permute-start | bytes 80 | tf_op jit(solution)/shard_map/ppermute | solution.py:14
  10.2 18.9 %collective-permute-start.2 = (s32[2,3]{1,0:T(2,128)}, s32[2,3]{1,0:T(2,128)S(1)}, u32[]{:S(2)}, u32[]{:S(2)}) collective-permute-start(s32[2,3]{1,0:T(2,128)} %param.6), channel_id=1, source_target_pairs={{2,0},{4,2},{6,4},{8,6},{10,8},{12,10},{14,12},{16,14},{18,16},{20... | collective-permute-start | bytes 80 | tf_op jit(solution)/shard_map/ppermute | solution.py:15
  14.3 24.3 %collective-permute-start.3 = (bf16[2,32,32,32]{3,2,1,0:T(8,128)(2,1)}, bf16[2,32,32,32]{3,2,1,0:T(8,128)(2,1)S(1)}, u32[]{:S(2)}, u32[]{:S(2)}) collective-permute-start(bf16[2,32,32,32]{3,2,1,0:T(8,128)(2,1)} %param.5), channel_id=1, source_target_pairs={{2,0},{4,2},{6,4},{8,6},{10,8},{12,10},{14,12},{16,14},{18,16},{20... | collective-permute-start | bytes 393224 | tf_op jit(solution)/shard_map/ppermute | solution.py:15
  16.2 33.8 %collective-permute-start = (bf16[2,32,32,32]{3,2,1,0:T(8,128)(2,1)}, bf16[2,32,32,32]{3,2,1,0:T(8,128)(2,1)S(1)}, u32[]{:S(2)}, u32[]{:S(2)}) collective-permute-start(bf16[2,32,32,32]{3,2,1,0:T(8,128)(2,1)} %param.5), channel_id=1, source_target_pairs={{0,2},{2,4},{4,6},{6,8},{8,10},{10,12},{12,14},{14,16},{16,18},{18... | collective-permute-start | bytes 393224 | tf_op jit(solution)/shard_map/ppermute | solution.py:14
  50.0 12.0 %copy-start = (bf16[2,32,32,32]{3,2,1,0:T(8,128)(2,1)S(1)}, bf16[2,32,32,32]{3,2,1,0:T(8,128)(2,1)}, u32[]{:S(2)}) copy-start(bf16[2,32,32,32]{3,2,1,0:T(8,128)(2,1)} %param.5) | copy-start | bytes 393220
  62.2 48.2 %copy-start.1 = (f32[32,64,128]{2,1,0:T(8,128)S(1)}, f32[32,64,128]{2,1,0:T(8,128)}, u32[]{:S(2)}) copy-start(f32[32,64,128]{2,1,0:T(8,128)} %param.9) | copy-start | bytes 3145732
  78.6 59.9 %all-gather.2.cloned.1.call-start = ((), (), s32[]{:S(2)}) async-start(), calls=%async_computation.2 | async-start | bytes 3145728 | tf_op jit(solution)/shard_map/all_gather | solution.py:76
  92.6 17.8 %collective-permute-start.4 = (bf16[32,64,128]{2,1,0:T(8,128)(2,1)S(1)}, bf16[32,64,128]{2,1,0:T(8,128)(2,1)S(1)}, u32[]{:S(2)}, u32[]{:S(2)}) collective-permute-start(bf16[32,64,128]{2,1,0:T(8,128)(2,1)S(1)} %slice.183), channel_id=1, source_target_pairs={{0,2},{2,4},{4,6},{6,8},{8,10},{10,12},{12,14},{14,16},{16,18},{18... | collective-permute-start | bytes 1572872 | tf_op jit(solution)/shard_map/ppermute | solution.py:22
  112.9 13.3 %collective-permute-start.5 = (bf16[32,64,128]{2,1,0:T(8,128)(2,1)S(1)}, bf16[32,64,128]{2,1,0:T(8,128)(2,1)S(1)}, u32[]{:S(2)}, u32[]{:S(2)}) collective-permute-start(bf16[32,64,128]{2,1,0:T(8,128)(2,1)S(1)} %get-tuple-element.50), channel_id=1, source_target_pairs={{0,30},{2,0},{4,2},{6,4},{8,6},{10,8},{12,10},{14,12},{16,14},{18,... | collective-permute-start | bytes 1572872 | tf_op jit(solution)/shard_map/ppermute | solution.py:22
Sparse Core Ops, SparseCore 0:
  78.7 12.5 reduce-scatter.1
  127.4 11.0 all-gather.1
where the time goes:
time: 149 us; the launch traced here: 148 us
  local copies, waits for them, and re-layouts  56.3 us (38%)
  waiting for transfers between devices  51.4 us (34%)
  between operations  19.4 us (13%)
  starting transfers between devices  12.8 us (9%)
  other arithmetic  7.42 us (5%)
    ppermute x2, waiting for transfers between devices, from_behind(): lax.ppermute(x, axis, [(i, (i + by) % devices) for i in range(devices)])  27.5 us
    gather x18, local copies, waits for them, and re-layouts  25.5 us
    dynamic_update_slice x1, local copies, waits for them, and re-layouts, local(): slab = lax.dynamic_update_slice(slab, products[item], spot)  13.9 us
    reduce_scatter x1, waiting for transfers between devices, local(): summed = lax.psum_scatter(slab, 'bricks', scatter_dimension=2, tiled=True)  12.6 us
    all_gather x1, waiting for transfers between devices, local(): lax.all_gather(jnp.concatenate([potential, following], 0), 'bricks', axis...  11.2 us
    pad x3, local copies, waits for them, and re-layouts, local(): jnp.pad(group, ((0, 0), (box_side, box_side), (box_side, box_side), (box_...  9.57 us
    ppermute x2, starting transfers between devices, padded_2(): after = lax.ppermute(leading, axis, down)  6.02 us
    ppermute x2, starting transfers between devices, from_behind(): lax.ppermute(x, axis, [(i, (i + by) % devices) for i in range(devices)])  3.62 us
  transfers between devices with their start and end apart: 8, of which 4 were waited for; matrix products, arithmetic and copies ran while one was open for 19% of the time, Pallas kernels for 0%

commit v1 on v0

v1 whole, which is shorter than its diff:
```python
import jax
import jax.numpy as jnp
from jax import lax
from jax.experimental import pallas as pl
from jax.experimental.pallas import tpu as pltpu
from jax.sharding import PartitionSpec as P

LANES = 128
SUB = 8
F32 = jnp.float32
BF16 = jnp.bfloat16
I32 = jnp.int32
VMEM = pl.BlockSpec(memory_space=pltpu.VMEM)
SMEM = pl.BlockSpec(memory_space=pltpu.SMEM)


def iota(shape, dim):
    return lax.broadcasted_iota(I32, shape, dim)


def rows_splat(values, count):
    tiles = []
    for start in range(0, count, SUB):
        tile = jnp.zeros((SUB, LANES), F32)
        row = iota((SUB, LANES), 0)
        for r in range(SUB):
            if start + r < len(values) and values[start + r] is not None:
                tile = jnp.where(row == r, values[start + r], tile)
        tiles.append(tile)
    return jnp.concatenate(tiles, 0)


def pack_kernel(offs, kern, pat, kern_other, pat_other, orbs, out):
    core = lax.axis_index("bricks")
    count, side = orbs.shape[0], orbs.shape[1]
    groups = LANES // side
    per = side // groups
    k_at, lane = iota((side, LANES), 0), iota((side, LANES), 1)
    metas = []
    for rel in range(count):
        orb = jnp.bitwise_xor(core, rel)
        o0, o1, o2 = offs[orb, 0], offs[orb, 1], offs[orb, 2]
        metas += [o0, o1, o2]
        turned = (lane & (side - 1)) == ((k_at + o2) & (side - 1))
        total = jnp.zeros((per * side, LANES), F32)
        for g in range(groups):
            spread = jnp.where(turned & ((lane // side) == g), 1.0, 0.0).astype(BF16)
            planes = [orbs[orb, (g * per + i - o0) & (side - 1)] for i in range(per)]
            total = total + jnp.dot(
                jnp.concatenate(planes, 0), spread, preferred_element_type=F32
            )
        for i in range(per):
            plane = pltpu.roll(total[i * side : (i + 1) * side], o1 & (side - 1), 0)
            out[rel * per + i] = plane.astype(BF16)
    values = [jnp.full((1, LANES), m, I32).astype(F32) for m in metas] + [None] * 2
    for rel in range(count):
        kr, pr = (kern, pat) if rel == 0 else (kern_other, pat_other)
        for c in range(3 * count):
            at = (c // count) * count + jnp.bitwise_xor(core, c % count)
            w = jnp.full((1, LANES), kr[0, at] * pr[0, at].astype(F32), F32)
            high = w.astype(BF16).astype(F32)
            values += [high, w - high]
    out[count * per] = rows_splat(values, side).astype(BF16)


def cut_kernel(offs, offs_prev, v_own, v_other, cut_own, cut_prev):
    core = lax.axis_index("bricks")
    side, depth = v_own.shape[0], v_own.shape[1]
    groups = LANES // side
    per = side // groups
    at = iota((2 * LANES, LANES), 0)
    lane = iota((2 * LANES, LANES), 1)
    z_at = jnp.where(at < LANES, core * LANES + at, (1 - core) * LANES + at - LANES)
    picks = []
    for table in (offs, offs_prev):
        o2 = table[core, 2]
        picks.append(
            jnp.where(z_at == o2 + (((lane & (side - 1)) - o2) & (side - 1)), 1.0, 0.0)
        )
    pick = jnp.concatenate(picks, 1)
    group = (iota((1, 2 * LANES), 1) & (LANES - 1)) // side
    total = jnp.zeros((per * depth, 2 * LANES), F32)
    for g in range(groups):
        here = jnp.where(group == g, 1.0, 0.0)
        left = v_own[g * per : (g + 1) * per].reshape(per * depth, LANES)
        right = v_other[g * per : (g + 1) * per].reshape(per * depth, LANES)
        both = jnp.concatenate([left.astype(BF16), right.astype(BF16)], 1)
        total = total + jnp.dot(both, (pick * here).astype(BF16), preferred_element_type=F32)
    row = iota((side, LANES), 0)
    for t, (table, cut) in enumerate(((offs, cut_own), (offs_prev, cut_prev))):
        o1 = table[core, 1]
        for i in range(per):
            low = total[i * depth : i * depth + side, t * LANES : (t + 1) * LANES]
            high = total[i * depth + depth - side : (i + 1) * depth, t * LANES : (t + 1) * LANES]
            cut[i] = jnp.where(row >= o1, low, high).astype(BF16)


def quadratic(fields, weights):
    total = None
    for a in range(len(fields)):
        inner = None
        for b in range(a, len(fields)):
            if (a, b) in weights:
                term = weights[a, b] * fields[b]
                inner = term if inner is None else inner + term
        total = fields[a] * inner if total is None else total + fields[a] * inner
    return total


def density_kernel(prev, own, following, dens, mixed, bend, placed):
    core = lax.axis_index("bricks")
    side = dens.shape[0]
    groups = LANES // side
    per = side // groups
    packets = (prev, own, following)
    count = (prev.shape[0] - 1) // per
    metas = [packet[count * per].astype(F32) for packet in packets]
    orbs = [(d, o) for d in range(3) for o in range(count)]
    corner = {}
    for d, o in orbs:
        corner[d, o] = [
            metas[d][3 * o + axis : 3 * o + axis + 1].astype(I32) for axis in range(3)
        ]

    def weight(a, b):
        at = SUB + 2 * (orbs[a][1] * 3 * count + (orbs[b][0] - orbs[a][0] + 1) * count + orbs[b][1])
        return metas[orbs[a][0]][at : at + 1] + metas[orbs[a][0]][at + 1 : at + 2]

    pair = {}
    for a in range(len(orbs)):
        for b in range(a, len(orbs)):
            if orbs[b][0] - orbs[a][0] <= 1:
                w = weight(a, b) if a == b else weight(a, b) + weight(b, a)
                pair[a, b] = jnp.broadcast_to(w, (side, LANES))
    wide = groups * LANES
    from_lane, to = iota((LANES, wide), 0), iota((LANES, wide), 1)
    replicate = jnp.where(from_lane == (to // LANES) * side + (to & (side - 1)), 1.0, 0.0).astype(BF16)
    lane = iota((1, LANES), 1)
    to_row = iota((1, wide), 1)
    here = range(2 * count)
    for b in here:
        d, o = orbs[b]
        o0, o1, o2 = corner[d, o]
        z_own = core * LANES + (to_row & (LANES - 1))
        o2w = jnp.concatenate([o2] * groups, 1)
        z_orb = o2w + (((to_row & (side - 1)) - o2w) & (side - 1))
        spread = replicate * jnp.where(z_own == z_orb, 1.0, 0.0).astype(BF16)
        planes = []
        for i in range(per):
            x = (lane // side) * per + i
            keep = (x < o0) if d == 0 else (x >= o0)
            planes.append(packets[d][o * per + i] * jnp.where(keep, 1.0, 0.0).astype(BF16))
        placed[b] = jnp.dot(jnp.concatenate(planes, 0), spread, preferred_element_type=F32)
    row = iota((side, LANES), 0)
    for i in range(per):
        for g in range(groups):
            fields = [placed[b, i * side : (i + 1) * side, g * LANES : (g + 1) * LANES] for b in here]
            halves = []
            for half in range(2):
                cut = []
                for b in here:
                    low = row >= corner[orbs[b]][1]
                    cut.append(jnp.where(low if half == 0 else ~low, fields[b], 0.0))
                halves.append(quadratic(cut, pair))
            x = g * per + i
            dens[x, 0:side] = halves[0]
            dens[x, side : 2 * side] = halves[1]
    me = count
    a0, a1, a2 = corner[orbs[me]]
    z_me = a2 + (((lane & (side - 1)) - a2) & (side - 1))
    for i in range(per):
        x = (lane // side) * per + i
        slab_me = jnp.where(x < a0, 1, 0)
        fields = []
        for b in range(len(orbs)):
            d, o = orbs[b]
            field = packets[d][o * per + i].astype(F32)
            if b != me:
                o0, o1, o2 = corner[d, o]
                slab = jnp.where(x < o0, 1, 0) + (d - 1)
                same = (slab == slab_me) & (o2 + (((lane & (side - 1)) - o2) & (side - 1)) == z_me)
                field = field * jnp.where(same, 1.0, 0.0)
                field = jnp.where((row < o1) == (row < a1), field, 0.0)
            fields.append(field)
        mix = None
        for b in range(len(orbs)):
            term = jnp.broadcast_to(weight(me, b), (side, LANES)) * fields[b]
            mix = term if mix is None else mix + term
        mixed[i] = mix
        rho = quadratic(fields, pair)
        bend[i] = rho * lax.rsqrt(1.0 + rho * rho)


def gradient_kernel(offs, cut_own, cut_next, mixed, bend, out):
    core = lax.axis_index("bricks")
    side = out.shape[1]
    groups = LANES // side
    per = side // groups
    o0, o1, o2 = offs[core, 0], offs[core, 1], offs[core, 2]
    lane = iota((1, LANES), 1)
    planes = []
    for i in range(per):
        x = (lane // side) * per + i
        outer = jnp.where(x < o0, cut_next[i].astype(F32), cut_own[i].astype(F32))
        potential = (outer + bend[i]).astype(BF16).astype(F32)
        grad = 2.0 * potential * mixed[i]
        planes.append(pltpu.roll(grad, (side - o1) & (side - 1), 0).astype(BF16))
    stacked = jnp.concatenate(planes, 0)
    from_lane, k_at = iota((LANES, side), 0), iota((LANES, side), 1)
    turned = (from_lane & (side - 1)) == ((k_at + o2) & (side - 1))
    for g in range(groups):
        gather = jnp.where(turned & ((from_lane // side) == g), 1.0, 0.0).astype(BF16)
        part = jnp.dot(stacked, gather, preferred_element_type=F32).astype(BF16)
        for i in range(per):
            out[0, (g * per + i - o0) & (side - 1)] = part[i * side : (i + 1) * side]


def call(kernel, name, outs, ins, args, scratch=()):
    return pl.pallas_call(
        kernel,
        name=name,
        out_shape=outs,
        in_specs=ins,
        out_specs=jax.tree.map(lambda _: VMEM, outs),
        scratch_shapes=scratch,
        cost_estimate=pl.CostEstimate(flops=1000000, bytes_accessed=2000000, transcendentals=0),
    )(*args)


def local(orbitals, offsets, kernel, pattern, local_potential):
    devices = lax.axis_size("atoms")
    up = [(i, (i + 1) % devices) for i in range(devices)]
    down = [(j, i) for i, j in up]
    swap = [(0, 1), (1, 0)]
    count, side = orbitals.shape[0], orbitals.shape[1]
    depth, width = local_potential.shape[1], local_potential.shape[2]
    per = side * side // LANES
    shape = jax.ShapeDtypeStruct
    offsets_prev = lax.ppermute(offsets, "atoms", up)
    other = lax.ppermute(local_potential, "bricks", swap)
    kernel_other = lax.ppermute(kernel, "bricks", swap)
    pattern_other = lax.ppermute(pattern, "bricks", swap)
    packet = call(
        pack_kernel,
        "pack",
        shape((count * per + 1, side, LANES), BF16),
        [SMEM] * 5 + [VMEM],
        (offsets, kernel, pattern, kernel_other, pattern_other, orbitals),
    )
    prev = lax.ppermute(packet, "atoms", up)
    following = lax.ppermute(packet, "atoms", down)
    cut_own, cut_prev = call(
        cut_kernel,
        "cut",
        (shape((per, side, LANES), BF16),) * 2,
        [SMEM] * 2 + [VMEM] * 2,
        (offsets, offsets_prev, local_potential, other),
    )
    cut_next = lax.ppermute(cut_prev, "atoms", down)
    density, mixed, bend = call(
        density_kernel,
        "density",
        (
            shape((side, depth, width), F32),
            shape((per, side, LANES), F32),
            shape((per, side, LANES), F32),
        ),
        [VMEM] * 3,
        (prev, packet, following),
        [pltpu.VMEM((2 * count, per * side, LANES // side * LANES), F32)],
    )
    gradient = call(
        gradient_kernel,
        "gradient",
        shape((1, side, side, side), BF16),
        [SMEM] + [VMEM] * 4,
        (offsets, cut_own, cut_next, mixed, bend),
    )
    return density, gradient


def solution(mesh):
    return jax.shard_map(
        local,
        mesh=mesh,
        in_specs=(
            P("atoms", None, None, None),
            P("atoms", None),
            P(("atoms", "bricks"), None),
            P(("atoms", "bricks"), None),
            P("atoms", None, "bricks"),
        ),
        out_specs=(P("atoms", None, "bricks"), P(("atoms", "bricks"), None, None, None)),
        check_vma=False,
    )
```

time: 149 us -> 34.9 us (0.23)
  local copies, waits for them, and re-layouts: 56.3 us -> 4.45 us
  waiting for transfers between devices: 51.4 us -> 11.3 us
  between operations: 19.4 us -> 0.67 us
  Pallas kernels: 0 us -> 10.4 us
  other arithmetic: 7.42 us -> 0 us
  starting transfers between devices: 12.8 us -> 7.92 us
    gather x21 -> x0, local copies, waits for them, and re-layouts: 25.8 us -> none
    ppermute x6 -> x7, waiting for transfers between devices: 27.5 us -> 11.3 us  [the longest x1 9.29 us: local(): offsets_prev = lax.ppermute(offsets, 'atoms', up)]
    dynamic_update_slice x1 -> x0, local copies, waits for them, and re-layouts: 13.9 us -> none  [local(): slab = lax.dynamic_update_slice(slab, products[item], spot)]
    reduce_scatter x1 -> x0, waiting for transfers between devices: 12.6 us -> none  [local(): summed = lax.psum_scatter(slab, 'bricks', scatter_dimension=2, tiled=True)]
    all_gather x1 -> x0, waiting for transfers between devices: 11.2 us -> none  [local(): lax.all_gather(jnp.concatenate([potential, following], 0), 'bricks', axis...]
    pallas_call x0 -> x4, Pallas kernels: none -> 10.4 us  [call(): pl.pallas_call(kernel, name=name, out_shape=outs, in_specs=ins, out_specs...]
    pad x3 -> x0, local copies, waits for them, and re-layouts: 9.57 us -> none  [local(): jnp.pad(group, ((0, 0), (box_side, box_side), (box_side, box_side), (box_...]
    ppermute x6 -> x7, starting transfers between devices: 12.7 us -> 7.92 us  [the longest x1 6.84 us: local(): following = lax.ppermute(packet, 'atoms', down)]
  transfers between devices with their start and end apart: 8 -> 7, of which waited for: 4 -> 2; matrix products, arithmetic and copies ran while one was open for 19% -> 0% of each run, Pallas kernels for 0% -> 24%
where the time goes in v1:
time: 34.9 us; the launch traced here: 34.7 us
  waiting for transfers between devices  11.3 us (32%)
  Pallas kernels  10.4 us (30%)
  starting transfers between devices  7.92 us (23%)
  local copies, waits for them, and re-layouts  4.45 us (13%)
  between operations  0.67 us (2%)
    pallas_call x4, Pallas kernels, call(): pl.pallas_call(kernel, name=name, out_shape=outs, in_specs=ins, out_specs...  10.4 us
    ppermute x1, waiting for transfers between devices, local(): offsets_prev = lax.ppermute(offsets, 'atoms', up)  9.29 us
    ppermute x1, starting transfers between devices, local(): following = lax.ppermute(packet, 'atoms', down)  6.84 us
    unnamed x16, local copies, waits for them, and re-layouts  4.45 us
    ppermute x1, waiting for transfers between devices, local(): kernel_other = lax.ppermute(kernel, 'bricks', swap)  1.99 us
  transfers between devices with their start and end apart: 7, of which 2 were waited for; matrix products, arithmetic and copies ran while one was open for 0% of the time, Pallas kernels for 24%

profile of v1, /device:TPU:0, one launch (start us, length us, event | category | flops | bytes accessed | tf_op | source)
XLA Modules:
  0.0 34.7 jit_solution(11402370486369297018)
XLA Ops:
  0.6 0.0 copy-start.4
  0.6 0.6 %collective-permute-start.5 = (f32[32,64,128]{2,1,0:T(8,128)}, f32[32,64,128]{2,1,0:T(8,128)S(1)}, u32[]{:S(2)}, u32[]{:S(2)}) collective-permute-start(f32[32,64,128]{2,1,0:T(8,128)} %v_own.1), channel_id=1, source_target_pairs={{0,1},{1,0},{2,3},{3,2},{4,5},{5,4},{6,7},{7,6},{8,9},{9,8},{10,11... | collective-permute-start | bytes 3145736 | tf_op jit(solution)/shard_map/ppermute | solution.py:240
  1.2 0.1 collective-permute-start
  1.3 0.4 %collective-permute-start.1 = (s32[1,6]{1,0:T(1,128)}, s32[1,6]{1,0:T(1,128)S(1)}, u32[]{:S(2)}, u32[]{:S(2)}) collective-permute-start(s32[1,6]{1,0:T(1,128)} %pat.1), channel_id=1, source_target_pairs={{0,1},{1,0},{2,3},{3,2},{4,5},{5,4},{6,7},{7,6},{8,9},{9,8},{10,11... | collective-permute-start | bytes 80 | tf_op jit(solution)/shard_map/ppermute | solution.py:242
  1.7 2.0 %collective-permute-done.kern_other = f32[1,6]{1,0:T(1,128)S(1)} collective-permute-done((f32[1,6]{1,0:T(1,128)}, f32[1,6]{1,0:T(1,128)S(1)}, u32[]{:S(2)}, u32[]{:S(2)}) %collective-permute-start) | collective-permute-done | bytes 56 | tf_op jit(solution)/shard_map/ppermute | solution.py:241
  3.7 0.0 copy-start.6
  3.7 0.0 collective-permute-done.1.pat_other
  3.7 0.5 %copy-done.6 = f32[1,6]{1,0:T(1,128)} copy-done((f32[1,6]{1,0:T(1,128)}, f32[1,6]{1,0:T(1,128)S(1)}, u32[]{:S(2)}) %copy-start.6) | copy-done | bytes 48
  4.2 0.0 copy-start.7
  4.2 0.5 %copy-done.7 = s32[1,6]{1,0:T(1,128)} copy-done((s32[1,6]{1,0:T(1,128)}, s32[1,6]{1,0:T(1,128)S(1)}, u32[]{:S(2)}) %copy-start.7) | copy-done | bytes 48
  4.7 2.0 %pack.1.own = bf16[17,32,128]{2,1,0:T(8,128)(2,1)} custom-call(s32[2,3]{1,0:T(2,128)} %offs.5, f32[1,6]{1,0:T(1,128)} %kern.1, s32[1,6]{1,0:T(1,128)} %pat.1, f32[1,6]{1,0:T(1,128)} %copy-done.6, s32[1,6]{1,0:T(1,128)} %copy-done.7, bf16[2,32,32,32]{3,2,1,0:T(8,128)(2,1)} %orbs.1), custom_call_target="tpu_custom_call" | custom-call | flops 1000000 | bytes 2000000 | tf_op jit(solution)/shard_map/pack/pallas_call | solution.py:219
  6.8 6.8 %collective-permute-start.3 = (bf16[17,32,128]{2,1,0:T(8,128)(2,1)}, bf16[17,32,128]{2,1,0:T(8,128)(2,1)S(1)}, u32[]{:S(2)}, u32[]{:S(2)}) collective-permute-start(bf16[17,32,128]{2,1,0:T(8,128)(2,1)} %pack.1.own), channel_id=1, source_target_pairs={{2,0},{4,2},{6,4},{8,6},{10,8},{12,10},{14,12},{16,14},{18,16},{20... | collective-permute-start | bytes 417800 | tf_op jit(solution)/shard_map/ppermute | solution.py:251
  13.6 0.0 collective-permute-start.2
  13.6 0.0 copy-done.4
  13.6 0.0 collective-permute-start.4
  13.6 9.3 %collective-permute-done.4.offs_prev = s32[2,3]{1,0:T(2,128)S(1)} collective-permute-done((s32[2,3]{1,0:T(2,128)S(1)}, s32[2,3]{1,0:T(2,128)S(1)}, u32[]{:S(2)}, u32[]{:S(2)}) %collective-permute-start.4) | collective-permute-done | bytes 56 | tf_op jit(solution)/shard_map/ppermute | solution.py:239
  22.9 0.0 copy-start.5
  22.9 0.0 collective-permute-done.5.v_other
  22.9 0.5 %copy-done.5 = s32[2,3]{1,0:T(2,128)} copy-done((s32[2,3]{1,0:T(2,128)}, s32[2,3]{1,0:T(2,128)S(1)}, u32[]{:S(2)}) %copy-start.5) | copy-done | bytes 48
  23.4 0.0 copy-start
  23.5 1.0 %copy-done = f32[32,64,128]{2,1,0:T(8,128)} copy-done((f32[32,64,128]{2,1,0:T(8,128)}, f32[32,64,128]{2,1,0:T(8,128)S(1)}, u32[]{:S(2)}) %copy-start) | copy-done | bytes 1048600
  24.4 2.7 %cut.1 = (bf16[8,32,128]{2,1,0:T(8,128)(2,1)}, bf16[8,32,128]{2,1,0:T(8,128)(2,1)}) custom-call(s32[2,3]{1,0:T(2,128)} %offs.5, s32[2,3]{1,0:T(2,128)} %copy-done.5, f32[32,64,128]{2,1,0:T(8,128)} %v_own.1, f32[32,64,128]{2,1,0:T(8,128)} %copy-done), custom_call_target="tpu_custom_call" | custom-call | flops 1000000 | bytes 2000000 | tf_op jit(solution)/shard_map/cut/pallas_call | solution.py:219
  27.1 0.0 collective-permute-start.6
  27.1 0.0 collective-permute-done.3.following
  27.1 0.0 copy-start.1
  27.1 0.0 collective-permute-done.2.prev
  27.1 0.6 %copy-done.1 = bf16[17,32,128]{2,1,0:T(8,128)(2,1)} copy-done((bf16[17,32,128]{2,1,0:T(8,128)(2,1)}, bf16[17,32,128]{2,1,0:T(8,128)(2,1)S(1)}, u32[]{:S(2)}) %copy-start.1) | copy-done | bytes 139288
  27.8 0.0 copy-start.2
  27.8 0.7 %copy-done.2 = bf16[17,32,128]{2,1,0:T(8,128)(2,1)} copy-done((bf16[17,32,128]{2,1,0:T(8,128)(2,1)}, bf16[17,32,128]{2,1,0:T(8,128)(2,1)S(1)}, u32[]{:S(2)}) %copy-start.2) | copy-done | bytes 139288
  28.4 3.7 %density.1 = (f32[32,64,128]{2,1,0:T(8,128)}, f32[8,32,128]{2,1,0:T(8,128)}, f32[8,32,128]{2,1,0:T(8,128)}) custom-call(bf16[17,32,128]{2,1,0:T(8,128)(2,1)} %copy-done.2, bf16[17,32,128]{2,1,0:T(8,128)(2,1)} %pack.1.own, bf16[17,32,128]{2,1,0:T(8,128)(2,1)} %copy-done.1), custom_call_target="tpu_custom_call" | custom-call | flops 1000000 | bytes 2000000 | tf_op jit(solution)/shard_map/density/pallas_call | solution.py:219
  32.1 0.0 collective-permute-done.6.cut_next
  32.1 0.0 copy-start.3
  32.1 0.6 %copy-done.3 = bf16[8,32,128]{2,1,0:T(8,128)(2,1)} copy-done((bf16[8,32,128]{2,1,0:T(8,128)(2,1)}, bf16[8,32,128]{2,1,0:T(8,128)(2,1)S(1)}, u32[]{:S(2)}) %copy-start.3) | copy-done | bytes 65560
  32.7 2.0 %gradient.1 = bf16[1,32,32,32]{3,2,1,0:T(8,128)(2,1)} custom-call(s32[2,3]{1,0:T(2,128)} %offs.5, bf16[8,32,128]{2,1,0:T(8,128)(2,1)} %get-tuple-element.8.cut_own, bf16[8,32,128]{2,1,0:T(8,128)(2,1)} %copy-done.3, f32[8,32,128]{2,1,0:T(8,128)} %get-tuple-element.10.mixed, f32[8,32,128]{2,1,0:T(8,128)} %get-tuple-element.11.bend), custom_call_target="tpu_custom_call" | custom-call | flops 1000000 | bytes 2000000 | tf_op jit(solution)/shard_map/gradient/pallas_call | solution.py:219
Async XLA Ops:
  0.6 13.0 %copy-start.4 = (s32[2,3]{1,0:T(2,128)S(1)}, s32[2,3]{1,0:T(2,128)}, u32[]{:S(2)}) copy-start(s32[2,3]{1,0:T(2,128)} %offs.5) | copy-start | bytes 76
  0.6 22.3 %collective-permute-start.5 = (f32[32,64,128]{2,1,0:T(8,128)}, f32[32,64,128]{2,1,0:T(8,128)S(1)}, u32[]{:S(2)}, u32[]{:S(2)}) collective-permute-start(f32[32,64,128]{2,1,0:T(8,128)} %v_own.1), channel_id=1, source_target_pairs={{0,1},{1,0},{2,3},{3,2},{4,5},{5,4},{6,7},{7,6},{8,9},{9,8},{10,11... | collective-permute-start | bytes 3145736 | tf_op jit(solution)/shard_map/ppermute | solution.py:240
  1.2 2.5 %collective-permute-start = (f32[1,6]{1,0:T(1,128)}, f32[1,6]{1,0:T(1,128)S(1)}, u32[]{:S(2)}, u32[]{:S(2)}) collective-permute-start(f32[1,6]{1,0:T(1,128)} %kern.1), channel_id=1, source_target_pairs={{0,1},{1,0},{2,3},{3,2},{4,5},{5,4},{6,7},{7,6},{8,9},{9,8},{10,11... | collective-permute-start | bytes 80 | tf_op jit(solution)/shard_map/ppermute | solution.py:241
  1.3 2.4 %collective-permute-start.1 = (s32[1,6]{1,0:T(1,128)}, s32[1,6]{1,0:T(1,128)S(1)}, u32[]{:S(2)}, u32[]{:S(2)}) collective-permute-start(s32[1,6]{1,0:T(1,128)} %pat.1), channel_id=1, source_target_pairs={{0,1},{1,0},{2,3},{3,2},{4,5},{5,4},{6,7},{7,6},{8,9},{9,8},{10,11... | collective-permute-start | bytes 80 | tf_op jit(solution)/shard_map/ppermute | solution.py:242
  3.7 0.5 %copy-start.6 = (f32[1,6]{1,0:T(1,128)}, f32[1,6]{1,0:T(1,128)S(1)}, u32[]{:S(2)}) copy-start(f32[1,6]{1,0:T(1,128)S(1)} %collective-permute-done.kern_other) | copy-start | bytes 76
  4.2 0.5 %copy-start.7 = (s32[1,6]{1,0:T(1,128)}, s32[1,6]{1,0:T(1,128)S(1)}, u32[]{:S(2)}) copy-start(s32[1,6]{1,0:T(1,128)S(1)} %collective-permute-done.1.pat_other) | copy-start | bytes 76
  6.8 20.3 %collective-permute-start.3 = (bf16[17,32,128]{2,1,0:T(8,128)(2,1)}, bf16[17,32,128]{2,1,0:T(8,128)(2,1)S(1)}, u32[]{:S(2)}, u32[]{:S(2)}) collective-permute-start(bf16[17,32,128]{2,1,0:T(8,128)(2,1)} %pack.1.own), channel_id=1, source_target_pairs={{2,0},{4,2},{6,4},{8,6},{10,8},{12,10},{14,12},{16,14},{18,16},{20... | collective-permute-start | bytes 417800 | tf_op jit(solution)/shard_map/ppermute | solution.py:251
  13.6 13.5 %collective-permute-start.2 = (bf16[17,32,128]{2,1,0:T(8,128)(2,1)}, bf16[17,32,128]{2,1,0:T(8,128)(2,1)S(1)}, u32[]{:S(2)}, u32[]{:S(2)}) collective-permute-start(bf16[17,32,128]{2,1,0:T(8,128)(2,1)} %pack.1.own), channel_id=1, source_target_pairs={{0,2},{2,4},{4,6},{6,8},{8,10},{10,12},{12,14},{14,16},{16,18},{18... | collective-permute-start | bytes 417800 | tf_op jit(solution)/shard_map/ppermute | solution.py:250
  13.6 9.3 %collective-permute-start.4 = (s32[2,3]{1,0:T(2,128)S(1)}, s32[2,3]{1,0:T(2,128)S(1)}, u32[]{:S(2)}, u32[]{:S(2)}) collective-permute-start(s32[2,3]{1,0:T(2,128)S(1)} %copy-done.4), channel_id=1, source_target_pairs={{0,2},{2,4},{4,6},{6,8},{8,10},{10,12},{12,14},{14,16},{16,18},{18... | collective-permute-start | bytes 80 | tf_op jit(solution)/shard_map/ppermute | solution.py:239
  22.9 0.5 %copy-start.5 = (s32[2,3]{1,0:T(2,128)}, s32[2,3]{1,0:T(2,128)S(1)}, u32[]{:S(2)}) copy-start(s32[2,3]{1,0:T(2,128)S(1)} %collective-permute-done.4.offs_prev) | copy-start | bytes 76
  23.4 1.0 %copy-start = (f32[32,64,128]{2,1,0:T(8,128)}, f32[32,64,128]{2,1,0:T(8,128)S(1)}, u32[]{:S(2)}) copy-start(f32[32,64,128]{2,1,0:T(8,128)S(1)} %collective-permute-done.5.v_other) | copy-start | bytes 3145732
  27.1 5.0 %collective-permute-start.6 = (bf16[8,32,128]{2,1,0:T(8,128)(2,1)}, bf16[8,32,128]{2,1,0:T(8,128)(2,1)S(1)}, u32[]{:S(2)}, u32[]{:S(2)}) collective-permute-start(bf16[8,32,128]{2,1,0:T(8,128)(2,1)} %get-tuple-element.9), channel_id=1, source_target_pairs={{2,0},{4,2},{6,4},{8,6},{10,8},{12,10},{14,12},{16,14},{18,16},{20... | collective-permute-start | bytes 196616 | tf_op jit(solution)/shard_map/ppermute | solution.py:259
  27.1 0.7 %copy-start.1 = (bf16[17,32,128]{2,1,0:T(8,128)(2,1)}, bf16[17,32,128]{2,1,0:T(8,128)(2,1)S(1)}, u32[]{:S(2)}) copy-start(bf16[17,32,128]{2,1,0:T(8,128)(2,1)S(1)} %collective-permute-done.3.following) | copy-start | bytes 417796
  27.8 0.7 %copy-start.2 = (bf16[17,32,128]{2,1,0:T(8,128)(2,1)}, bf16[17,32,128]{2,1,0:T(8,128)(2,1)S(1)}, u32[]{:S(2)}) copy-start(bf16[17,32,128]{2,1,0:T(8,128)(2,1)S(1)} %collective-permute-done.2.prev) | copy-start | bytes 417796
  32.1 0.6 %copy-start.3 = (bf16[8,32,128]{2,1,0:T(8,128)(2,1)}, bf16[8,32,128]{2,1,0:T(8,128)(2,1)S(1)}, u32[]{:S(2)}) copy-start(bf16[8,32,128]{2,1,0:T(8,128)(2,1)S(1)} %collective-permute-done.6.cut_next) | copy-start | bytes 196612

commit v2 on v1

v2 whole, which is shorter than its diff:
```python
import jax
import jax.numpy as jnp
from jax import lax
from jax.experimental import pallas as pl
from jax.experimental.pallas import tpu as pltpu
from jax.sharding import PartitionSpec as P

LANES = 128
SUB = 8
F32 = jnp.float32
BF16 = jnp.bfloat16
I32 = jnp.int32
VMEM = pl.BlockSpec(memory_space=pltpu.VMEM)
HBM = pl.BlockSpec(memory_space=pltpu.HBM)
GRANT = 16 * 2**20


def iota(shape, dim):
    return lax.broadcasted_iota(I32, shape, dim)


def rows_splat(values, count):
    tiles = []
    for start in range(0, count, SUB):
        tile = jnp.zeros((SUB, LANES), F32)
        row = iota((SUB, LANES), 0)
        for r in range(SUB):
            if start + r < len(values) and values[start + r] is not None:
                tile = jnp.where(row == r, values[start + r], tile)
        tiles.append(tile)
    return jnp.concatenate(tiles, 0)


def pack_kernel(offs_hbm, kern_hbm, pat_hbm, kern_other, pat_other, orbs_hbm, out, offs, kern, pat, orbs, sems):
    copies = [
        pltpu.make_async_copy(src, dst, sems.at[n])
        for n, (src, dst) in enumerate(
            ((offs_hbm, offs), (kern_hbm, kern), (pat_hbm, pat), (orbs_hbm, orbs))
        )
    ]
    for copy in copies:
        copy.start()
    core = lax.axis_index("bricks")
    count, side = orbs.shape[0], orbs.shape[1]
    groups = LANES // side
    per = side // groups
    k_at, lane = iota((side, LANES), 0), iota((side, LANES), 1)
    for copy in copies:
        copy.wait()
    metas = []
    for rel in range(count):
        orb = jnp.bitwise_xor(core, rel)
        o0, o1, o2 = offs[orb, 0], offs[orb, 1], offs[orb, 2]
        metas += [o0, o1, o2]
        turned = (lane & (side - 1)) == ((k_at + o2) & (side - 1))
        total = jnp.zeros((per * side, LANES), F32)
        for g in range(groups):
            spread = jnp.where(turned & ((lane // side) == g), 1.0, 0.0).astype(BF16)
            planes = [orbs[orb, (g * per + i - o0) & (side - 1)] for i in range(per)]
            total = total + jnp.dot(
                jnp.concatenate(planes, 0), spread, preferred_element_type=F32
            )
        for i in range(per):
            plane = pltpu.roll(total[i * side : (i + 1) * side], o1 & (side - 1), 0)
            out[rel * per + i] = plane.astype(BF16)
    values = [jnp.full((1, LANES), m, I32).astype(F32) for m in metas] + [None] * 2
    for rel in range(count):
        kr, pr = (kern, pat) if rel == 0 else (kern_other, pat_other)
        line = kr[...] * pr[...].astype(F32)
        spread = [jnp.broadcast_to(line[:, c : c + 1], (1, LANES)) for c in range(3 * count)]
        for c in range(3 * count):
            w = jnp.where(core == 0, spread[c], spread[c ^ 1])
            high = w.astype(BF16).astype(F32)
            values += [high, w - high]
    out[count * per] = rows_splat(values, side).astype(BF16)


def cut_kernel(packet, offs_prev, v_hbm, v_other, cut_own, cut_prev, v_own, sems):
    side, depth = v_own.shape[0], v_own.shape[1]
    groups = LANES // side
    per = side // groups
    copies = [
        pltpu.make_async_copy(
            v_hbm.at[pl.ds(g * per, per)], v_own.at[pl.ds(g * per, per)], sems.at[g]
        )
        for g in range(groups)
    ]
    for copy in copies:
        copy.start()
    core = lax.axis_index("bricks")
    meta = packet[packet.shape[0] - 1].astype(F32)
    line = jnp.where(core == 0, offs_prev[0:1, :], offs_prev[1:2, :])
    corners = [
        [meta[axis : axis + 1].astype(I32) for axis in range(3)],
        [jnp.broadcast_to(line[:, axis : axis + 1], (1, LANES)) for axis in range(3)],
    ]
    at = iota((2 * LANES, LANES), 0)
    lane = iota((1, LANES), 1)
    z_at = jnp.where(at < LANES, core * LANES + at, (1 - core) * LANES + at - LANES)
    picks = []
    for _, _, o2 in corners:
        picks.append(jnp.where(z_at == o2 + ((lane - o2) & (side - 1)), 1.0, 0.0))
    pick = jnp.concatenate(picks, 1)
    group = (iota((1, 2 * LANES), 1) & (LANES - 1)) // side
    total = jnp.zeros((per * depth, 2 * LANES), F32)
    for g in range(groups):
        here = jnp.where(group == g, 1.0, 0.0)
        copies[g].wait()
        left = v_own[g * per : (g + 1) * per].reshape(per * depth, LANES)
        right = v_other[g * per : (g + 1) * per].reshape(per * depth, LANES)
        both = jnp.concatenate([left.astype(BF16), right.astype(BF16)], 1)
        total = total + jnp.dot(both, (pick * here).astype(BF16), preferred_element_type=F32)
    row = iota((side, LANES), 0)
    for t, cut in enumerate((cut_own, cut_prev)):
        o1 = corners[t][1]
        for i in range(per):
            low = total[i * depth : i * depth + side, t * LANES : (t + 1) * LANES]
            high = total[i * depth + depth - side : (i + 1) * depth, t * LANES : (t + 1) * LANES]
            cut[i] = jnp.where(row >= o1, low, high).astype(BF16)


def quadratic(fields, weights):
    total = None
    for a in range(len(fields)):
        inner = None
        for b in range(a, len(fields)):
            if (a, b) in weights:
                term = weights[a, b] * fields[b]
                inner = term if inner is None else inner + term
        total = fields[a] * inner if total is None else total + fields[a] * inner
    return total


class Tables:
    def __init__(self, packets, per):
        self.count = (packets[0].shape[0] - 1) // per
        self.metas = [packet[self.count * per].astype(F32) for packet in packets]
        self.orbs = [(d, o) for d in range(len(packets)) for o in range(self.count)]
        self.corner = [
            [self.metas[d][3 * o + axis : 3 * o + axis + 1].astype(I32) for axis in range(3)]
            for d, o in self.orbs
        ]

    def weight(self, a, b):
        (da, oa), (db, ob) = self.orbs[a], self.orbs[b]
        at = SUB + 2 * (oa * 3 * self.count + (db - da + 1) * self.count + ob)
        return self.metas[da][at : at + 1] + self.metas[da][at + 1 : at + 2]

    def pairs(self, side):
        pair = {}
        for a in range(len(self.orbs)):
            for b in range(a, len(self.orbs)):
                if self.orbs[b][0] - self.orbs[a][0] <= 1:
                    w = self.weight(a, b)
                    if a != b:
                        w = w + self.weight(b, a)
                    pair[a, b] = jnp.broadcast_to(w, (side, LANES))
        return pair


def brick_kernel(prev, own, dens_hbm, dens, placed, sems):
    core = lax.axis_index("bricks")
    side = dens.shape[0]
    groups = LANES // side
    per = side // groups
    packets = (prev, own)
    tables = Tables(packets, per)
    pair = tables.pairs(side)
    wide = groups * LANES
    from_lane, to = iota((LANES, wide), 0), iota((LANES, wide), 1)
    replicate = jnp.where(from_lane == (to // LANES) * side + (to & (side - 1)), 1.0, 0.0).astype(BF16)
    lane = iota((1, LANES), 1)
    to_row = iota((1, wide), 1)
    z_own = core * LANES + (to_row & (LANES - 1))
    here = range(len(tables.orbs))
    for b in here:
        d, o = tables.orbs[b]
        o0, _, o2 = tables.corner[b]
        o2w = jnp.concatenate([o2] * groups, 1)
        z_orb = o2w + ((to_row - o2w) & (side - 1))
        spread = replicate * jnp.where(z_own == z_orb, 1.0, 0.0).astype(BF16)
        planes = []
        for i in range(per):
            x = (lane // side) * per + i
            keep = (x < o0) if d == 0 else (x >= o0)
            planes.append(packets[d][o * per + i] * jnp.where(keep, 1.0, 0.0).astype(BF16))
        placed[b] = jnp.dot(jnp.concatenate(planes, 0), spread, preferred_element_type=F32)
    row = iota((side, LANES), 0)
    copies = []
    for g in range(groups):
        for i in range(per):
            fields = [placed[b, i * side : (i + 1) * side, g * LANES : (g + 1) * LANES] for b in here]
            x = g * per + i
            for half in range(2):
                cut = []
                for b in here:
                    low = row >= tables.corner[b][1]
                    cut.append(jnp.where(low if half == 0 else ~low, fields[b], 0.0))
                dens[x, half * side : (half + 1) * side] = quadratic(cut, pair)
        copies.append(
            pltpu.make_async_copy(
                dens.at[pl.ds(g * per, per)], dens_hbm.at[pl.ds(g * per, per)], sems.at[g]
            )
        )
        copies[-1].start()
    for copy in copies:
        copy.wait()


def box_kernel(offs_hbm, prev, own, following, cut_own, cut_next, out, offs, sem):
    copy = pltpu.make_async_copy(offs_hbm, offs, sem)
    copy.start()
    core = lax.axis_index("bricks")
    side = out.shape[1]
    groups = LANES // side
    per = side // groups
    packets = (prev, own, following)
    tables = Tables(packets, per)
    me = tables.count
    pair = tables.pairs(side)
    mine = [jnp.broadcast_to(tables.weight(me, b), (side, LANES)) for b in range(len(tables.orbs))]
    lane = iota((1, LANES), 1)
    row = iota((side, LANES), 0)
    a0, a1, a2 = tables.corner[me]
    z_me = a2 + ((lane - a2) & (side - 1))
    copy.wait()
    s0, s1, s2 = offs[core, 0], offs[core, 1], offs[core, 2]
    planes = []
    for i in range(per):
        x = (lane // side) * per + i
        slab_me = jnp.where(x < a0, 1, 0)
        fields = []
        for b, (d, o) in enumerate(tables.orbs):
            field = packets[d][o * per + i].astype(F32)
            if b != me:
                o0, o1, o2 = tables.corner[b]
                slab = jnp.where(x < o0, 1, 0) + (d - 1)
                same = (slab == slab_me) & (o2 + ((lane - o2) & (side - 1)) == z_me)
                field = field * jnp.where(same, 1.0, 0.0)
                field = jnp.where((row < o1) == (row < a1), field, 0.0)
            fields.append(field)
        mix = None
        for b in range(len(fields)):
            term = mine[b] * fields[b]
            mix = term if mix is None else mix + term
        rho = quadratic(fields, pair)
        bend = rho * lax.rsqrt(1.0 + rho * rho)
        outer = jnp.where(x < a0, cut_next[i].astype(F32), cut_own[i].astype(F32))
        potential = (outer + bend).astype(BF16).astype(F32)
        grad = 2.0 * potential * mix
        planes.append(pltpu.roll(grad, (side - s1) & (side - 1), 0).astype(BF16))
    stacked = jnp.concatenate(planes, 0)
    from_lane, k_at = iota((LANES, side), 0), iota((LANES, side), 1)
    turned = (from_lane & (side - 1)) == ((k_at + s2) & (side - 1))
    for g in range(groups):
        gather = jnp.where(turned & ((from_lane // side) == g), 1.0, 0.0).astype(BF16)
        part = jnp.dot(stacked, gather, preferred_element_type=F32).astype(BF16)
        for i in range(per):
            out[0, (g * per + i - s0) & (side - 1)] = part[i * side : (i + 1) * side]


def call(kernel, outs, out_specs, ins, args, scratch):
    return pl.pallas_call(
        kernel,
        out_shape=outs,
        in_specs=ins,
        out_specs=out_specs,
        scratch_shapes=scratch,
        compiler_params=pltpu.CompilerParams(vmem_limit_bytes=GRANT),
        cost_estimate=pl.CostEstimate(
            flops=1000000, bytes_accessed=2000000, transcendentals=0
        ),
    )(*[
        pltpu.with_memory_space_constraint(x, pltpu.HBM) if spec is HBM else x
        for x, spec in zip(args, ins)
    ])


def step(orbitals, offsets, kernel, pattern, local_potential):
    devices = lax.axis_size("atoms")
    up = [(i, (i + 1) % devices) for i in range(devices)]
    down = [(j, i) for i, j in up]
    swap = [(0, 1), (1, 0)]
    count, side = orbitals.shape[0], orbitals.shape[1]
    depth, width = local_potential.shape[1], local_potential.shape[2]
    groups = LANES // side
    per = side // groups
    shape = jax.ShapeDtypeStruct
    dma = pltpu.SemaphoreType.DMA
    offsets_prev = lax.ppermute(offsets, "atoms", up)
    kernel_other = lax.ppermute(kernel, "bricks", swap)
    pattern_other = lax.ppermute(pattern, "bricks", swap)
    other = lax.ppermute(local_potential, "bricks", swap)
    packet = call(
        pack_kernel,
        shape((count * per + 1, side, LANES), BF16),
        VMEM,
        [HBM] * 3 + [VMEM] * 2 + [HBM],
        (offsets, kernel, pattern, kernel_other, pattern_other, orbitals),
        [
            pltpu.SMEM(offsets.shape, I32),
            pltpu.VMEM(kernel.shape, F32),
            pltpu.VMEM(pattern.shape, I32),
            pltpu.VMEM(orbitals.shape, BF16),
            dma((4,)),
        ],
    )
    prev = lax.ppermute(packet, "atoms", up)
    following = lax.ppermute(packet, "atoms", down)
    cut_own, cut_prev = call(
        cut_kernel,
        (shape((per, side, LANES), BF16),) * 2,
        (VMEM,) * 2,
        [VMEM] * 2 + [HBM] + [VMEM],
        (packet, offsets_prev, local_potential, other),
        [pltpu.VMEM(local_potential.shape, F32), dma((groups,))],
    )
    cut_next = lax.ppermute(cut_prev, "atoms", down)
    density = call(
        brick_kernel,
        shape((side, depth, width), F32),
        HBM,
        [VMEM] * 2,
        (prev, packet),
        [
            pltpu.VMEM((side, depth, width), F32),
            pltpu.VMEM((2 * count, per * side, groups * LANES), F32),
            dma((groups,)),
        ],
    )
    gradient = call(
        box_kernel,
        shape((1, side, side, side), BF16),
        VMEM,
        [HBM] + [VMEM] * 5,
        (offsets, prev, packet, following, cut_own, cut_next),
        [pltpu.SMEM(offsets.shape, I32), dma(())],
    )
    return density, gradient


def solution(mesh):
    return jax.shard_map(
        step,
        mesh=mesh,
        in_specs=(
            P("atoms", None, None, None),
            P("atoms", None),
            P(("atoms", "bricks"), None),
            P(("atoms", "bricks"), None),
            P("atoms", None, "bricks"),
        ),
        out_specs=(P("atoms", None, "bricks"), P(("atoms", "bricks"), None, None, None)),
        check_vma=False,
    )
```

time: 34.9 us -> 27.7 us (0.79)
  local copies, waits for them, and re-layouts: 4.45 us -> 0.01 us
  Pallas kernels: 10.4 us -> 7.72 us
  waiting for transfers between devices: 11.3 us -> 9.55 us
  starting transfers between devices: 7.92 us -> 9.57 us
    unnamed x16 -> x2, local copies, waits for them, and re-layouts: 4.45 us -> 0.01 us
    pallas_call x4, Pallas kernels: 10.4 us -> 7.72 us  [call(): pl.pallas_call(kernel, out_shape=outs, in_specs=ins, out_specs=out_specs,...]
    ppermute x7, waiting for transfers between devices: 11.3 us -> 9.55 us  [the longest x1 7.17 us: step(): offsets_prev = lax.ppermute(offsets, 'atoms', up)]
    ppermute x7, starting transfers between devices: 7.92 us -> 9.57 us  [the longest x1 4.06 us: step(): following = lax.ppermute(packet, 'atoms', down)]
  transfers between devices with their start and end apart: 7 -> 7, of which waited for: 2 -> 3; matrix products, arithmetic and copies ran while one was open for 0% -> 0% of each run, Pallas kernels for 24% -> 21%
where the time goes in v2:
time: 27.7 us; the launch traced here: 27.5 us
  starting transfers between devices  9.57 us (35%)
  waiting for transfers between devices  9.55 us (34%)
  Pallas kernels  7.72 us (28%)
  between operations  0.68 us (2%)
    pallas_call x4, Pallas kernels, call(): pl.pallas_call(kernel, out_shape=outs, in_specs=ins, out_specs=out_specs,...  7.72 us
    ppermute x1, waiting for transfers between devices, step(): offsets_prev = lax.ppermute(offsets, 'atoms', up)  7.17 us
    ppermute x1, starting transfers between devices, step(): following = lax.ppermute(packet, 'atoms', down)  4.06 us
    ppermute x1, starting transfers between devices, step(): prev = lax.ppermute(packet, 'atoms', up)  2.9 us
    ppermute x1, waiting for transfers between devices, step(): kernel_other = lax.ppermute(kernel, 'bricks', swap)  1.99 us
    ppermute x1, starting transfers between devices, step(): cut_next = lax.ppermute(cut_prev, 'atoms', down)  1.54 us
    ppermute x1, starting transfers between devices, step(): other = lax.ppermute(local_potential, 'bricks', swap)  0.56 us
  transfers between devices with their start and end apart: 7, of which 3 were waited for; matrix products, arithmetic and copies ran while one was open for 0% of the time, Pallas kernels for 21%

profile of v2, /device:TPU:0, one launch (start us, length us, event | category | flops | bytes accessed | tf_op | source)
XLA Modules:
  0.0 27.5 jit_solution(2921133464061621452)
XLA Ops:
  0.6 0.0 copy-start
  0.6 0.6 %collective-permute-start.5 = (f32[32,64,128]{2,1,0:T(8,128)}, f32[32,64,128]{2,1,0:T(8,128)S(1)}, u32[]{:S(2)}, u32[]{:S(2)}) collective-permute-start(f32[32,64,128]{2,1,0:T(8,128)} %v_hbm.1), channel_id=1, source_target_pairs={{0,1},{1,0},{2,3},{3,2},{4,5},{5,4},{6,7},{7,6},{8,9},{9,8},{10,11... | collective-permute-start | bytes 3145736 | tf_op jit(solution)/shard_map/ppermute | solution.py:293
  1.2 0.1 collective-permute-start
  1.3 0.4 %collective-permute-start.1 = (s32[1,6]{1,0:T(1,128)}, s32[1,6]{1,0:T(1,128)S(1)}, u32[]{:S(2)}, u32[]{:S(2)}) collective-permute-start(s32[1,6]{1,0:T(1,128)} %pat_hbm.1), channel_id=1, source_target_pairs={{0,1},{1,0},{2,3},{3,2},{4,5},{5,4},{6,7},{7,6},{8,9},{9,8},{10,11... | collective-permute-start | bytes 80 | tf_op jit(solution)/shard_map/ppermute | solution.py:292
  1.7 2.0 %collective-permute-done.kern_other = f32[1,6]{1,0:T(1,128)S(1)} collective-permute-done((f32[1,6]{1,0:T(1,128)}, f32[1,6]{1,0:T(1,128)S(1)}, u32[]{:S(2)}, u32[]{:S(2)}) %collective-permute-start) | collective-permute-done | bytes 56 | tf_op jit(solution)/shard_map/ppermute | solution.py:291
  3.7 0.0 collective-permute-done.1.pat_other
  3.7 1.4 %shard_map.68.own.packet = bf16[17,32,128]{2,1,0:T(8,128)(2,1)S(1)} custom-call(s32[2,3]{1,0:T(2,128)} %offs_hbm.3, f32[1,6]{1,0:T(1,128)} %kern_hbm.1, s32[1,6]{1,0:T(1,128)} %pat_hbm.1, f32[1,6]{1,0:T(1,128)S(1)} %collective-permute-done.kern_other, s32[1,6]{1,0:T(1,128)S(1)} %collective-permute-done.1.pat_other, bf16[2,32,32,32]{3,2,1,0:T(8,128)(2,1)} %orbs_hbm.1), custom_call_target="tpu_custom_call" | custom-call | flops 1000000 | bytes 2000000 | tf_op jit(solution)/shard_map/pallas_call | solution.py:263
  5.1 2.9 %collective-permute-start.2 = (bf16[17,32,128]{2,1,0:T(8,128)(2,1)S(1)}, bf16[17,32,128]{2,1,0:T(8,128)(2,1)S(1)}, u32[]{:S(2)}, u32[]{:S(2)}) collective-permute-start(bf16[17,32,128]{2,1,0:T(8,128)(2,1)S(1)} %shard_map.68.own.packet), channel_id=1, source_target_pairs={{0,2},{2,4},{4,6},{6,8},{8,10},{10,12},{12,14},{14,16},{16,18},{18... | collective-permute-start | bytes 417800 | tf_op jit(solution)/shard_map/ppermute | solution.py:308
  8.0 4.1 %collective-permute-start.3 = (bf16[17,32,128]{2,1,0:T(8,128)(2,1)S(1)}, bf16[17,32,128]{2,1,0:T(8,128)(2,1)S(1)}, u32[]{:S(2)}, u32[]{:S(2)}) collective-permute-start(bf16[17,32,128]{2,1,0:T(8,128)(2,1)S(1)} %shard_map.68.own.packet), channel_id=1, source_target_pairs={{2,0},{4,2},{6,4},{8,6},{10,8},{12,10},{14,12},{16,14},{18,16},{20... | collective-permute-start | bytes 417800 | tf_op jit(solution)/shard_map/ppermute | solution.py:309
  12.1 0.0 copy-done
  12.1 0.0 collective-permute-start.4
  12.1 7.2 %collective-permute-done.4.offs_prev = s32[2,3]{1,0:T(2,128)S(1)} collective-permute-done((s32[2,3]{1,0:T(2,128)S(1)}, s32[2,3]{1,0:T(2,128)S(1)}, u32[]{:S(2)}, u32[]{:S(2)}) %collective-permute-start.4) | collective-permute-done | bytes 56 | tf_op jit(solution)/shard_map/ppermute | solution.py:290
  19.2 0.0 collective-permute-done.5.v_other
  19.2 2.0 %shard_map.70 = (bf16[8,32,128]{2,1,0:T(8,128)(2,1)S(1)}, bf16[8,32,128]{2,1,0:T(8,128)(2,1)S(1)}) custom-call(bf16[17,32,128]{2,1,0:T(8,128)(2,1)S(1)} %shard_map.68.own.packet, s32[2,3]{1,0:T(2,128)S(1)} %collective-permute-done.4.offs_prev, f32[32,64,128]{2,1,0:T(8,128)} %v_hbm.1, f32[32,64,128]{2,1,0:T(8,128)S(1)} %collective-permute-done.5.v_other), custom_call_target="tpu_custom_call" | custom-call | flops 1000000 | bytes 2000000 | tf_op jit(solution)/shard_map/pallas_call | solution.py:263
  21.2 1.5 %collective-permute-start.6 = (bf16[8,32,128]{2,1,0:T(8,128)(2,1)S(1)}, bf16[8,32,128]{2,1,0:T(8,128)(2,1)S(1)}, u32[]{:S(2)}, u32[]{:S(2)}) collective-permute-start(bf16[8,32,128]{2,1,0:T(8,128)(2,1)S(1)} %get-tuple-element.5), channel_id=1, source_target_pairs={{2,0},{4,2},{6,4},{8,6},{10,8},{12,10},{14,12},{16,14},{18,16},{20... | collective-permute-start | bytes 196616 | tf_op jit(solution)/shard_map/ppermute | solution.py:318
  22.7 0.0 collective-permute-done.2.prev
  22.7 2.4 %shard_map.69 = f32[32,64,128]{2,1,0:T(8,128)} custom-call(bf16[17,32,128]{2,1,0:T(8,128)(2,1)S(1)} %collective-permute-done.2.prev, bf16[17,32,128]{2,1,0:T(8,128)(2,1)S(1)} %shard_map.68.own.packet), custom_call_target="tpu_custom_call" | custom-call | flops 1000000 | bytes 2000000 | tf_op jit(solution)/shard_map/pallas_call | solution.py:263
  25.1 0.0 collective-permute-done.3.following
  25.1 0.4 %collective-permute-done.6.cut_next = bf16[8,32,128]{2,1,0:T(8,128)(2,1)S(1)} collective-permute-done((bf16[8,32,128]{2,1,0:T(8,128)(2,1)S(1)}, bf16[8,32,128]{2,1,0:T(8,128)(2,1)S(1)}, u32[]{:S(2)}, u32[]{:S(2)}) %collective-permute-start.6) | collective-permute-done | bytes 65568 | tf_op jit(solution)/shard_map/ppermute | solution.py:318
  25.5 2.0 %shard_map.71 = bf16[1,32,32,32]{3,2,1,0:T(8,128)(2,1)} custom-call(s32[2,3]{1,0:T(2,128)} %offs_hbm.3, bf16[17,32,128]{2,1,0:T(8,128)(2,1)S(1)} %collective-permute-done.2.prev, bf16[17,32,128]{2,1,0:T(8,128)(2,1)S(1)} %shard_map.68.own.packet, bf16[17,32,128]{2,1,0:T(8,128)(2,1)S(1)} %collective-permute-done.3.following, ...), custom_call_target="tpu_custom_call" | custom-call | flops 1000000 | bytes 2000000 | tf_op jit(solution)/shard_map/pallas_call | solution.py:263
Async XLA Ops:
  0.6 11.4 %copy-start = (s32[2,3]{1,0:T(2,128)S(1)}, s32[2,3]{1,0:T(2,128)}, u32[]{:S(2)}) copy-start(s32[2,3]{1,0:T(2,128)} %offs_hbm.3) | copy-start | bytes 76
  0.6 18.6 %collective-permute-start.5 = (f32[32,64,128]{2,1,0:T(8,128)}, f32[32,64,128]{2,1,0:T(8,128)S(1)}, u32[]{:S(2)}, u32[]{:S(2)}) collective-permute-start(f32[32,64,128]{2,1,0:T(8,128)} %v_hbm.1), channel_id=1, source_target_pairs={{0,1},{1,0},{2,3},{3,2},{4,5},{5,4},{6,7},{7,6},{8,9},{9,8},{10,11... | collective-permute-start | bytes 3145736 | tf_op jit(solution)/shard_map/ppermute | solution.py:293
  1.2 2.5 %collective-permute-start = (f32[1,6]{1,0:T(1,128)}, f32[1,6]{1,0:T(1,128)S(1)}, u32[]{:S(2)}, u32[]{:S(2)}) collective-permute-start(f32[1,6]{1,0:T(1,128)} %kern_hbm.1), channel_id=1, source_target_pairs={{0,1},{1,0},{2,3},{3,2},{4,5},{5,4},{6,7},{7,6},{8,9},{9,8},{10,11... | collective-permute-start | bytes 80 | tf_op jit(solution)/shard_map/ppermute | solution.py:291
  1.3 2.4 %collective-permute-start.1 = (s32[1,6]{1,0:T(1,128)}, s32[1,6]{1,0:T(1,128)S(1)}, u32[]{:S(2)}, u32[]{:S(2)}) collective-permute-start(s32[1,6]{1,0:T(1,128)} %pat_hbm.1), channel_id=1, source_target_pairs={{0,1},{1,0},{2,3},{3,2},{4,5},{5,4},{6,7},{7,6},{8,9},{9,8},{10,11... | collective-permute-start | bytes 80 | tf_op jit(solution)/shard_map/ppermute | solution.py:292
  5.1 17.6 %collective-permute-start.2 = (bf16[17,32,128]{2,1,0:T(8,128)(2,1)S(1)}, bf16[17,32,128]{2,1,0:T(8,128)(2,1)S(1)}, u32[]{:S(2)}, u32[]{:S(2)}) collective-permute-start(bf16[17,32,128]{2,1,0:T(8,128)(2,1)S(1)} %shard_map.68.own.packet), channel_id=1, source_target_pairs={{0,2},{2,4},{4,6},{6,8},{8,10},{10,12},{12,14},{14,16},{16,18},{18... | collective-permute-start | bytes 417800 | tf_op jit(solution)/shard_map/ppermute | solution.py:308
  8.0 17.1 %collective-permute-start.3 = (bf16[17,32,128]{2,1,0:T(8,128)(2,1)S(1)}, bf16[17,32,128]{2,1,0:T(8,128)(2,1)S(1)}, u32[]{:S(2)}, u32[]{:S(2)}) collective-permute-start(bf16[17,32,128]{2,1,0:T(8,128)(2,1)S(1)} %shard_map.68.own.packet), channel_id=1, source_target_pairs={{2,0},{4,2},{6,4},{8,6},{10,8},{12,10},{14,12},{16,14},{18,16},{20... | collective-permute-start | bytes 417800 | tf_op jit(solution)/shard_map/ppermute | solution.py:309
  12.1 7.2 %collective-permute-start.4 = (s32[2,3]{1,0:T(2,128)S(1)}, s32[2,3]{1,0:T(2,128)S(1)}, u32[]{:S(2)}, u32[]{:S(2)}) collective-permute-start(s32[2,3]{1,0:T(2,128)S(1)} %copy-done), channel_id=1, source_target_pairs={{0,2},{2,4},{4,6},{6,8},{8,10},{10,12},{12,14},{14,16},{16,18},{18... | collective-permute-start | bytes 80 | tf_op jit(solution)/shard_map/ppermute | solution.py:290
  21.2 4.3 %collective-permute-start.6 = (bf16[8,32,128]{2,1,0:T(8,128)(2,1)S(1)}, bf16[8,32,128]{2,1,0:T(8,128)(2,1)S(1)}, u32[]{:S(2)}, u32[]{:S(2)}) collective-permute-start(bf16[8,32,128]{2,1,0:T(8,128)(2,1)S(1)} %get-tuple-element.5), channel_id=1, source_target_pairs={{2,0},{4,2},{6,4},{8,6},{10,8},{12,10},{14,12},{16,14},{18,16},{20... | collective-permute-start | bytes 196616 | tf_op jit(solution)/shard_map/ppermute | solution.py:318

commit v3 on v2

v3 whole, which is shorter than its diff:
```python
import jax
import jax.numpy as jnp
from jax import lax
from jax.experimental import pallas as pl
from jax.experimental.pallas import tpu as pltpu
from jax.sharding import PartitionSpec as P

LANES = 128
SUB = 8
F32 = jnp.float32
BF16 = jnp.bfloat16
I32 = jnp.int32
VMEM = pl.BlockSpec(memory_space=pltpu.VMEM)
HBM = pl.BlockSpec(memory_space=pltpu.HBM)
GRANT = 16 * 2**20


def iota(shape, dim):
    return lax.broadcasted_iota(I32, shape, dim)


def rows_splat(values, count):
    tiles = []
    for start in range(0, count, SUB):
        tile = jnp.zeros((SUB, LANES), F32)
        row = iota((SUB, LANES), 0)
        for r in range(SUB):
            if start + r < len(values) and values[start + r] is not None:
                tile = jnp.where(row == r, values[start + r], tile)
        tiles.append(tile)
    return jnp.concatenate(tiles, 0)


def pack_kernel(offs_hbm, kern_hbm, pat_hbm, orbs_hbm, out, offs, kern, pat, orb, sems):
    core = lax.axis_index("bricks")
    copies = [
        pltpu.make_async_copy(src, dst, sems.at[n])
        for n, (src, dst) in enumerate(
            ((offs_hbm, offs), (kern_hbm, kern), (pat_hbm, pat), (orbs_hbm.at[core], orb))
        )
    ]
    for copy in copies:
        copy.start()
    count, side = orbs_hbm.shape[0], orb.shape[0]
    groups = LANES // side
    per = side // groups
    k_at, lane = iota((side, LANES), 0), iota((side, LANES), 1)
    for copy in copies:
        copy.wait()
    corner = [offs[core, axis] for axis in range(3)]
    o0, o1, o2 = corner
    turned = (lane & (side - 1)) == ((k_at + o2) & (side - 1))
    total = jnp.zeros((per * side, LANES), F32)
    for g in range(groups):
        spread = jnp.where(turned & ((lane // side) == g), 1.0, 0.0).astype(BF16)
        planes = [orb[(g * per + i - o0) & (side - 1)] for i in range(per)]
        total = total + jnp.dot(jnp.concatenate(planes, 0), spread, preferred_element_type=F32)
    for i in range(per):
        plane = pltpu.roll(total[i * side : (i + 1) * side], o1 & (side - 1), 0)
        out[i] = plane.astype(BF16)
    values = [jnp.full((1, LANES), m, I32).astype(F32) for m in corner] + [None] * (SUB - 3)
    line = kern[...] * pat[...].astype(F32)
    spread = [jnp.broadcast_to(line[:, c : c + 1], (1, LANES)) for c in range(3 * count)]
    for c in range(3 * count):
        w = jnp.where(core == 0, spread[c], spread[c ^ 1])
        high = w.astype(BF16).astype(F32)
        values += [high, w - high]
    out[per] = rows_splat(values, side).astype(BF16)


def cut_kernel(packet, offs_prev, v_hbm, v_other, cut_own, cut_prev, v_own, sems):
    side, depth = v_own.shape[0], v_own.shape[1]
    groups = LANES // side
    per = side // groups
    copies = [
        pltpu.make_async_copy(
            v_hbm.at[pl.ds(g * per, per)], v_own.at[pl.ds(g * per, per)], sems.at[g]
        )
        for g in range(groups)
    ]
    for copy in copies:
        copy.start()
    core = lax.axis_index("bricks")
    meta = packet[packet.shape[0] - 1].astype(F32)
    line = jnp.where(core == 0, offs_prev[0:1, :], offs_prev[1:2, :])
    corners = [
        [meta[axis : axis + 1].astype(I32) for axis in range(3)],
        [jnp.broadcast_to(line[:, axis : axis + 1], (1, LANES)) for axis in range(3)],
    ]
    at = iota((2 * LANES, LANES), 0)
    lane = iota((1, LANES), 1)
    z_at = jnp.where(at < LANES, core * LANES + at, (1 - core) * LANES + at - LANES)
    picks = []
    for _, _, o2 in corners:
        picks.append(jnp.where(z_at == o2 + ((lane - o2) & (side - 1)), 1.0, 0.0))
    pick = jnp.concatenate(picks, 1)
    group = (iota((1, 2 * LANES), 1) & (LANES - 1)) // side
    total = jnp.zeros((per * depth, 2 * LANES), F32)
    for g in range(groups):
        here = jnp.where(group == g, 1.0, 0.0)
        copies[g].wait()
        left = v_own[g * per : (g + 1) * per].reshape(per * depth, LANES)
        right = v_other[g * per : (g + 1) * per].reshape(per * depth, LANES)
        both = jnp.concatenate([left.astype(BF16), right.astype(BF16)], 1)
        total = total + jnp.dot(both, (pick * here).astype(BF16), preferred_element_type=F32)
    row = iota((side, LANES), 0)
    for t, cut in enumerate((cut_own, cut_prev)):
        o1 = corners[t][1]
        for i in range(per):
            low = total[i * depth : i * depth + side, t * LANES : (t + 1) * LANES]
            high = total[i * depth + depth - side : (i + 1) * depth, t * LANES : (t + 1) * LANES]
            cut[i] = jnp.where(row >= o1, low, high).astype(BF16)


class Tables:
    def __init__(self, packets, places):
        self.places = places
        self.metas = [packet[packet.shape[0] - 1].astype(F32) for packet in packets]
        self.corner = [
            [meta[axis : axis + 1].astype(I32) for axis in range(3)] for meta in self.metas
        ]

    def weight(self, a, b):
        (da, oa), (db, ob) = self.places[a], self.places[b]
        at = SUB + 2 * ((db - da + 1) * 2 + (oa ^ ob))
        return self.metas[a][at : at + 1] + self.metas[a][at + 1 : at + 2]

    def pair(self, a, b):
        return self.weight(a, b) if a == b else self.weight(a, b) + self.weight(b, a)


def brick_kernel(prev0, prev1, own0, own1, dens_hbm, dens, ready, placed, sems):
    core = lax.axis_index("bricks")
    side = dens.shape[0]
    groups = LANES // side
    per = side // groups
    packets = (prev0, prev1, own0, own1)
    many = len(packets)
    tables = Tables(packets, ((0, 0), (0, 1), (1, 0), (1, 1)))
    lane = iota((1, LANES), 1)
    k_at = lane & (side - 1)
    row = iota((side, LANES), 0)
    uppers = [row < tables.corner[b][1] for b in range(many)]
    z_at = [o2 + ((k_at - o2) & (side - 1)) for _, _, o2 in tables.corner]
    links = {}
    for a in range(many):
        for b in range(a, many):
            w = tables.pair(a, b)
            if a != b:
                w = jnp.where(uppers[a] == uppers[b], jnp.where(z_at[a] == z_at[b], w, 0.0), 0.0)
            links[a, b] = jnp.broadcast_to(w, (side, LANES))
    for i in range(per):
        x = (lane // side) * per + i
        fields = []
        for b in range(many):
            o0 = tables.corner[b][0]
            keep = (x < o0) if b < 2 else (x >= o0)
            kept = packets[b][i] * jnp.where(keep, 1.0, 0.0).astype(BF16)
            fields.append(kept.astype(F32))
        for a in range(many):
            inner = links[a, a] * fields[a]
            for b in range(a + 1, many):
                inner = inner + links[a, b] * fields[b]
            product = fields[a] * inner
            high = product.astype(BF16)
            ready[a, i * side : (i + 1) * side, 0:LANES] = high
            ready[a, i * side : (i + 1) * side, LANES:] = (product - high.astype(F32)).astype(BF16)
    wide = groups * LANES
    to = iota((LANES, wide), 1)
    from_lane = iota((LANES, wide), 0)
    spread = jnp.where(from_lane == (to // LANES) * side + (to & (side - 1)), 1.0, 0.0).astype(BF16)
    for a in range(many):
        inside = jnp.where(z_at[a] == core * LANES + lane, 1.0, 0.0).astype(BF16)
        place = spread * jnp.concatenate([inside] * groups, 1)
        out = jnp.dot(ready[a], jnp.concatenate([place] * 2, 0), preferred_element_type=F32)
        placed[a] = out
    copies = []
    for g in range(groups):
        for i in range(per):
            x = g * per + i
            parts = [placed[a, i * side : (i + 1) * side, g * LANES : (g + 1) * LANES] for a in range(many)]
            low, high = None, None
            for a in range(many):
                down = jnp.where(uppers[a], 0.0, parts[a])
                up = jnp.where(uppers[a], parts[a], 0.0)
                low = down if low is None else low + down
                high = up if high is None else high + up
            dens[x, 0:side] = low
            dens[x, side : 2 * side] = high
        copies.append(
            pltpu.make_async_copy(
                dens.at[pl.ds(g * per, per)], dens_hbm.at[pl.ds(g * per, per)], sems.at[g]
            )
        )
        copies[-1].start()
    for copy in copies:
        copy.wait()


def box_kernel(
    offs_hbm, prev0, prev1, own0, own1, next0, next1, cut_own, cut_next, out, offs, grads, sem
):
    copy = pltpu.make_async_copy(offs_hbm, offs, sem)
    copy.start()
    core = lax.axis_index("bricks")
    side = out.shape[1]
    groups = LANES // side
    per = side // groups
    packets = (prev0, prev1, own0, own1, next0, next1)
    tables = Tables(packets, ((0, 0), (0, 1), (1, 0), (1, 1), (2, 0), (2, 1)))
    me, mate = 2, 3
    lane = iota((1, LANES), 1)
    k_at = lane & (side - 1)
    row = iota((side, LANES), 0)
    a0, a1, a2 = tables.corner[me]
    z_me = a2 + ((k_at - a2) & (side - 1))
    upper = row < a1

    def same_yz(b):
        _, o1, o2 = tables.corner[b]
        z = jnp.where(o2 + ((k_at - o2) & (side - 1)) == z_me, 1.0, 0.0)
        return jnp.where((row < o1) == upper, z, 0.0)

    overlap = [None if b == me else same_yz(b) for b in range(6)]
    inner_ids, last_ids = (0, 1, me, mate), (4, 5, me, mate)
    pair = {}
    for a in range(4):
        for b in range(a, 4):
            pair[a, b] = (
                tables.pair(inner_ids[a], inner_ids[b]), tables.pair(last_ids[a], last_ids[b])
            )
    mine = [(tables.weight(me, inner_ids[b]), tables.weight(me, last_ids[b])) for b in range(4)]
    for i in range(per):
        x = (lane // side) * per + i
        spill = x < a0

        def pick(both, a, b):
            return both[0] if a >= 2 and b >= 2 else jnp.where(spill, both[1], both[0])

        fields = []
        for o in (0, 1):
            before = jnp.where((x < tables.corner[o][0]) & ~spill, 1.0, 0.0).astype(BF16)
            after = jnp.where((x >= tables.corner[4 + o][0]) & spill, 1.0, 0.0).astype(BF16)
            fields.append(
                (packets[o][i] * before).astype(F32) * overlap[o]
                + (packets[4 + o][i] * after).astype(F32) * overlap[4 + o]
            )
        fields.append(packets[me][i].astype(F32))
        also = jnp.where((x < tables.corner[mate][0]) == spill, 1.0, 0.0).astype(BF16)
        fields.append((packets[mate][i] * also).astype(F32) * overlap[mate])
        rho = None
        for a in range(4):
            inner = None
            for b in range(a, 4):
                term = pick(pair[a, b], a, b) * fields[b]
                inner = term if inner is None else inner + term
            rho = fields[a] * inner if rho is None else rho + fields[a] * inner
        mix = None
        for b in range(4):
            term = pick(mine[b], b, me) * fields[b]
            mix = term if mix is None else mix + term
        bend = rho * lax.rsqrt(1.0 + rho * rho)
        outer = jnp.where(spill, cut_next[i].astype(F32), cut_own[i].astype(F32))
        potential = (outer + bend).astype(BF16).astype(F32)
        grads[i] = 2.0 * potential * mix
    copy.wait()
    s0, s1, s2 = offs[core, 0], offs[core, 1], offs[core, 2]
    planes = [pltpu.roll(grads[i], (side - s1) & (side - 1), 0).astype(BF16) for i in range(per)]
    stacked = jnp.concatenate(planes, 0)
    from_lane, to = iota((LANES, side), 0), iota((LANES, side), 1)
    turned = (from_lane & (side - 1)) == ((to + s2) & (side - 1))
    for g in range(groups):
        gather = jnp.where(turned & ((from_lane // side) == g), 1.0, 0.0).astype(BF16)
        part = jnp.dot(stacked, gather, preferred_element_type=F32).astype(BF16)
        for i in range(per):
            out[0, (g * per + i - s0) & (side - 1)] = part[i * side : (i + 1) * side]


def call(kernel, outs, out_specs, ins, args, scratch):
    return pl.pallas_call(
        kernel,
        out_shape=outs,
        in_specs=ins,
        out_specs=out_specs,
        scratch_shapes=scratch,
        compiler_params=pltpu.CompilerParams(vmem_limit_bytes=GRANT),
        cost_estimate=pl.CostEstimate(
            flops=1000000, bytes_accessed=2000000, transcendentals=0
        ),
    )(*[
        pltpu.with_memory_space_constraint(x, pltpu.HBM) if spec is HBM else x
        for x, spec in zip(args, ins)
    ])


def step(orbitals, offsets, kernel, pattern, local_potential):
    devices = lax.axis_size("atoms")
    up = [(i, (i + 1) % devices) for i in range(devices)]
    down = [(j, i) for i, j in up]
    swap = [(0, 1), (1, 0)]
    count, side = orbitals.shape[0], orbitals.shape[1]
    depth, width = local_potential.shape[1], local_potential.shape[2]
    groups = LANES // side
    per = side // groups
    shape = jax.ShapeDtypeStruct
    dma = pltpu.SemaphoreType.DMA
    offsets_prev = lax.ppermute(offsets, "atoms", up)
    own = call(
        pack_kernel,
        shape((per + 1, side, LANES), BF16),
        VMEM,
        [HBM] * 4,
        (offsets, kernel, pattern, orbitals),
        [
            pltpu.SMEM(offsets.shape, I32),
            pltpu.VMEM(kernel.shape, F32),
            pltpu.VMEM(pattern.shape, I32),
            pltpu.VMEM(orbitals.shape[1:], BF16),
            dma((4,)),
        ],
    )
    prev = lax.ppermute(own, "atoms", up)
    following = lax.ppermute(own, "atoms", down)
    other = lax.ppermute(local_potential, "bricks", swap)
    own_mate = lax.ppermute(own, "bricks", swap)
    cut_own, cut_prev = call(
        cut_kernel,
        (shape((per, side, LANES), BF16),) * 2,
        (VMEM,) * 2,
        [VMEM] * 2 + [HBM] + [VMEM],
        (own, offsets_prev, local_potential, other),
        [pltpu.VMEM(local_potential.shape, F32), dma((groups,))],
    )
    cut_next = lax.ppermute(cut_prev, "atoms", down)
    prev_mate = lax.ppermute(prev, "bricks", swap)
    following_mate = lax.ppermute(following, "bricks", swap)
    density = call(
        brick_kernel,
        shape((side, depth, width), F32),
        HBM,
        [VMEM] * 4,
        (prev, prev_mate, own, own_mate),
        [
            pltpu.VMEM((side, depth, width), F32),
            pltpu.VMEM((2 * count, per * side, 2 * LANES), BF16),
            pltpu.VMEM((2 * count, per * side, groups * LANES), F32),
            dma((groups,)),
        ],
    )
    gradient = call(
        box_kernel,
        shape((1, side, side, side), BF16),
        VMEM,
        [HBM] + [VMEM] * 8,
        (
            offsets,
            prev,
            prev_mate,
            own,
            own_mate,
            following,
            following_mate,
            cut_own,
            cut_next,
        ),
        [pltpu.SMEM(offsets.shape, I32), pltpu.VMEM((per, side, LANES), F32), dma(())],
    )
    return density, gradient


def solution(mesh):
    return jax.shard_map(
        step,
        mesh=mesh,
        in_specs=(
            P("atoms", None, None, None),
            P("atoms", None),
            P(("atoms", "bricks"), None),
            P(("atoms", "bricks"), None),
            P("atoms", None, "bricks"),
        ),
        out_specs=(P("atoms", None, "bricks"), P(("atoms", "bricks"), None, None, None)),
        check_vma=False,
    )
```

time: 27.7 us -> 27.7 us (level)
  waiting for transfers between devices: 9.55 us -> 11.1 us
  Pallas kernels: 7.72 us -> 6.48 us
  starting transfers between devices: 9.57 us -> 9.24 us
    pallas_call x4, Pallas kernels: 7.72 us -> 6.48 us  [call(): pl.pallas_call(kernel, out_shape=outs, in_specs=ins, out_specs=out_specs,...]
    ppermute x1, waiting for transfers between devices: 0.38 us -> 1.26 us  [step(): cut_next = lax.ppermute(cut_prev, 'atoms', down)]
    ppermute x4 -> x5, waiting for transfers between devices: 1.99 us -> 2.66 us  [the longest x1 2.65 us: step(): prev = lax.ppermute(own, 'atoms', up)]
    ppermute x4 -> x5, starting transfers between devices: 7.47 us -> 7.33 us  [the longest x1 4.06 us: step(): following = lax.ppermute(own, 'atoms', down)]
  transfers between devices with their start and end apart: 7 -> 8, of which waited for: 3 -> 3; matrix products, arithmetic and copies ran while one was open for 0% -> 0% of each run, Pallas kernels for 21% -> 18%
where the time goes in v3:
time: 27.7 us; the launch traced here: 27.5 us
  waiting for transfers between devices  11.1 us (40%)
  starting transfers between devices  9.24 us (33%)
  Pallas kernels  6.48 us (23%)
  between operations  0.68 us (2%)
    ppermute x1, waiting for transfers between devices, step(): offsets_prev = lax.ppermute(offsets, 'atoms', up)  7.17 us
    pallas_call x4, Pallas kernels, call(): pl.pallas_call(kernel, out_shape=outs, in_specs=ins, out_specs=out_specs,...  6.48 us
    ppermute x1, starting transfers between devices, step(): following = lax.ppermute(own, 'atoms', down)  4.06 us
    ppermute x1, waiting for transfers between devices, step(): prev = lax.ppermute(own, 'atoms', up)  2.65 us
    ppermute x1, starting transfers between devices, step(): prev = lax.ppermute(own, 'atoms', up)  2.55 us
    ppermute x1, starting transfers between devices, step(): cut_next = lax.ppermute(cut_prev, 'atoms', down)  1.34 us
    ppermute x1, waiting for transfers between devices, step(): cut_next = lax.ppermute(cut_prev, 'atoms', down)  1.26 us
    ppermute x1, starting transfers between devices, step(): other = lax.ppermute(local_potential, 'bricks', swap)  0.56 us
  transfers between devices with their start and end apart: 8, of which 3 were waited for; matrix products, arithmetic and copies ran while one was open for 0% of the time, Pallas kernels for 18%

profile of v3, /device:TPU:0, one launch (start us, length us, event | category | flops | bytes accessed | tf_op | source)
XLA Modules:
  0.0 27.5 jit_solution(16446468768198990048)
XLA Ops:
  0.6 0.0 copy-start
  0.6 0.6 %collective-permute-start.6 = (f32[32,64,128]{2,1,0:T(8,128)}, f32[32,64,128]{2,1,0:T(8,128)S(1)}, u32[]{:S(2)}, u32[]{:S(2)}) collective-permute-start(f32[32,64,128]{2,1,0:T(8,128)} %v_hbm.1), channel_id=1, source_target_pairs={{0,1},{1,0},{2,3},{3,2},{4,5},{5,4},{6,7},{7,6},{8,9},{9,8},{10,11... | collective-permute-start | bytes 3145736 | tf_op jit(solution)/shard_map/ppermute | solution.py:324
  1.2 1.2 %shard_map.68.own0.packet = bf16[9,32,128]{2,1,0:T(8,128)(2,1)S(1)} custom-call(s32[2,3]{1,0:T(2,128)} %offs_hbm.3, f32[1,6]{1,0:T(1,128)} %kern_hbm.1, s32[1,6]{1,0:T(1,128)} %pat_hbm.1, bf16[2,32,32,32]{3,2,1,0:T(8,128)(2,1)} %orbs_hbm.1), custom_call_target="tpu_custom_call" | custom-call | flops 1000000 | bytes 2000000 | tf_op jit(solution)/shard_map/pallas_call | solution.py:280
  2.4 2.5 %collective-permute-start = (bf16[9,32,128]{2,1,0:T(8,128)(2,1)S(1)}, bf16[9,32,128]{2,1,0:T(8,128)(2,1)S(1)}, u32[]{:S(2)}, u32[]{:S(2)}) collective-permute-start(bf16[9,32,128]{2,1,0:T(8,128)(2,1)S(1)} %shard_map.68.own0.packet), channel_id=1, source_target_pairs={{0,2},{2,4},{4,6},{6,8},{8,10},{10,12},{12,14},{14,16},{16,18},{18... | collective-permute-start | bytes 221192 | tf_op jit(solution)/shard_map/ppermute | solution.py:322
  5.0 4.1 %collective-permute-start.3 = (bf16[9,32,128]{2,1,0:T(8,128)(2,1)S(1)}, bf16[9,32,128]{2,1,0:T(8,128)(2,1)S(1)}, u32[]{:S(2)}, u32[]{:S(2)}) collective-permute-start(bf16[9,32,128]{2,1,0:T(8,128)(2,1)S(1)} %shard_map.68.own0.packet), channel_id=1, source_target_pairs={{2,0},{4,2},{6,4},{8,6},{10,8},{12,10},{14,12},{16,14},{18,16},{20... | collective-permute-start | bytes 221192 | tf_op jit(solution)/shard_map/ppermute | solution.py:323
  9.0 0.2 collective-permute-start.2
  9.3 2.6 %collective-permute-done.prev0 = bf16[9,32,128]{2,1,0:T(8,128)(2,1)S(1)} collective-permute-done((bf16[9,32,128]{2,1,0:T(8,128)(2,1)S(1)}, bf16[9,32,128]{2,1,0:T(8,128)(2,1)S(1)}, u32[]{:S(2)}, u32[]{:S(2)}) %collective-permute-start) | collective-permute-done | bytes 73760 | tf_op jit(solution)/shard_map/ppermute | solution.py:322
  11.9 0.0 collective-permute-start.1
  11.9 0.0 collective-permute-done.3.next0
  11.9 0.5 %collective-permute-start.4 = (bf16[9,32,128]{2,1,0:T(8,128)(2,1)S(1)}, bf16[9,32,128]{2,1,0:T(8,128)(2,1)S(1)}, u32[]{:S(2)}, u32[]{:S(2)}) collective-permute-start(bf16[9,32,128]{2,1,0:T(8,128)(2,1)S(1)} %collective-permute-done.3.next0), channel_id=1, source_target_pairs={{0,1},{1,0},{2,3},{3,2},{4,5},{5,4},{6,7},{7,6},{8,9},{9,8},{10,11... | collective-permute-start | bytes 221192 | tf_op jit(solution)/shard_map/ppermute | solution.py:336
  12.4 0.0 copy-done
  12.4 0.0 collective-permute-start.5
  12.4 7.2 %collective-permute-done.5.offs_prev = s32[2,3]{1,0:T(2,128)S(1)} collective-permute-done((s32[2,3]{1,0:T(2,128)S(1)}, s32[2,3]{1,0:T(2,128)S(1)}, u32[]{:S(2)}, u32[]{:S(2)}) %collective-permute-start.5) | collective-permute-done | bytes 56 | tf_op jit(solution)/shard_map/ppermute | solution.py:307
  19.6 0.0 collective-permute-done.6.v_other
  19.6 2.0 %shard_map.70 = (bf16[8,32,128]{2,1,0:T(8,128)(2,1)S(1)}, bf16[8,32,128]{2,1,0:T(8,128)(2,1)S(1)}) custom-call(bf16[9,32,128]{2,1,0:T(8,128)(2,1)S(1)} %shard_map.68.own0.packet, s32[2,3]{1,0:T(2,128)S(1)} %collective-permute-done.5.offs_prev, f32[32,64,128]{2,1,0:T(8,128)} %v_hbm.1, f32[32,64,128]{2,1,0:T(8,128)S(1)} %collective-permute-done.6.v_other), custom_call_target="tpu_custom_call" | custom-call | flops 1000000 | bytes 2000000 | tf_op jit(solution)/shard_map/pallas_call | solution.py:280
  21.6 1.3 %collective-permute-start.7 = (bf16[8,32,128]{2,1,0:T(8,128)(2,1)S(1)}, bf16[8,32,128]{2,1,0:T(8,128)(2,1)S(1)}, u32[]{:S(2)}, u32[]{:S(2)}) collective-permute-start(bf16[8,32,128]{2,1,0:T(8,128)(2,1)S(1)} %get-tuple-element.5), channel_id=1, source_target_pairs={{2,0},{4,2},{6,4},{8,6},{10,8},{12,10},{14,12},{16,14},{18,16},{20... | collective-permute-start | bytes 196616 | tf_op jit(solution)/shard_map/ppermute | solution.py:334
  22.9 0.0 collective-permute-done.2.own1
  22.9 0.0 collective-permute-done.1.prev1
  22.9 1.7 %shard_map.69 = f32[32,64,128]{2,1,0:T(8,128)} custom-call(bf16[9,32,128]{2,1,0:T(8,128)(2,1)S(1)} %collective-permute-done.prev0, bf16[9,32,128]{2,1,0:T(8,128)(2,1)S(1)} %collective-permute-done.1.prev1, bf16[9,32,128]{2,1,0:T(8,128)(2,1)S(1)} %shard_map.68.own0.packet, bf16[9,32,128]{2,1,0:T(8,128)(2,1)S(1)} %collective-permute-done.2.own1), custom_call_target="tpu_custom_call" | custom-call | flops 1000000 | bytes 2000000 | tf_op jit(solution)/shard_map/pallas_call | solution.py:280
  24.6 0.0 collective-permute-done.4.next1
  24.6 1.3 %collective-permute-done.7.cut_next = bf16[8,32,128]{2,1,0:T(8,128)(2,1)S(1)} collective-permute-done((bf16[8,32,128]{2,1,0:T(8,128)(2,1)S(1)}, bf16[8,32,128]{2,1,0:T(8,128)(2,1)S(1)}, u32[]{:S(2)}, u32[]{:S(2)}) %collective-permute-start.7) | collective-permute-done | bytes 65568 | tf_op jit(solution)/shard_map/ppermute | solution.py:334
  25.9 1.6 %shard_map.71 = bf16[1,32,32,32]{3,2,1,0:T(8,128)(2,1)} custom-call(s32[2,3]{1,0:T(2,128)} %offs_hbm.3, bf16[9,32,128]{2,1,0:T(8,128)(2,1)S(1)} %collective-permute-done.prev0, bf16[9,32,128]{2,1,0:T(8,128)(2,1)S(1)} %collective-permute-done.1.prev1, bf16[9,32,128]{2,1,0:T(8,128)(2,1)S(1)} %shard_map.68.own0.packet, ...), custom_call_target="tpu_custom_call" | custom-call | flops 1000000 | bytes 2000000 | tf_op jit(solution)/shard_map/pallas_call | solution.py:280
Async XLA Ops:
  0.6 11.8 %copy-start = (s32[2,3]{1,0:T(2,128)S(1)}, s32[2,3]{1,0:T(2,128)}, u32[]{:S(2)}) copy-start(s32[2,3]{1,0:T(2,128)} %offs_hbm.3) | copy-start | bytes 76
  0.6 19.0 %collective-permute-start.6 = (f32[32,64,128]{2,1,0:T(8,128)}, f32[32,64,128]{2,1,0:T(8,128)S(1)}, u32[]{:S(2)}, u32[]{:S(2)}) collective-permute-start(f32[32,64,128]{2,1,0:T(8,128)} %v_hbm.1), channel_id=1, source_target_pairs={{0,1},{1,0},{2,3},{3,2},{4,5},{5,4},{6,7},{7,6},{8,9},{9,8},{10,11... | collective-permute-start | bytes 3145736 | tf_op jit(solution)/shard_map/ppermute | solution.py:324
  2.4 9.5 %collective-permute-start = (bf16[9,32,128]{2,1,0:T(8,128)(2,1)S(1)}, bf16[9,32,128]{2,1,0:T(8,128)(2,1)S(1)}, u32[]{:S(2)}, u32[]{:S(2)}) collective-permute-start(bf16[9,32,128]{2,1,0:T(8,128)(2,1)S(1)} %shard_map.68.own0.packet), channel_id=1, source_target_pairs={{0,2},{2,4},{4,6},{6,8},{8,10},{10,12},{12,14},{14,16},{16,18},{18... | collective-permute-start | bytes 221192 | tf_op jit(solution)/shard_map/ppermute | solution.py:322
  5.0 6.9 %collective-permute-start.3 = (bf16[9,32,128]{2,1,0:T(8,128)(2,1)S(1)}, bf16[9,32,128]{2,1,0:T(8,128)(2,1)S(1)}, u32[]{:S(2)}, u32[]{:S(2)}) collective-permute-start(bf16[9,32,128]{2,1,0:T(8,128)(2,1)S(1)} %shard_map.68.own0.packet), channel_id=1, source_target_pairs={{2,0},{4,2},{6,4},{8,6},{10,8},{12,10},{14,12},{16,14},{18,16},{20... | collective-permute-start | bytes 221192 | tf_op jit(solution)/shard_map/ppermute | solution.py:323
  9.0 13.9 %collective-permute-start.2 = (bf16[9,32,128]{2,1,0:T(8,128)(2,1)S(1)}, bf16[9,32,128]{2,1,0:T(8,128)(2,1)S(1)}, u32[]{:S(2)}, u32[]{:S(2)}) collective-permute-start(bf16[9,32,128]{2,1,0:T(8,128)(2,1)S(1)} %shard_map.68.own0.packet), channel_id=1, source_target_pairs={{0,1},{1,0},{2,3},{3,2},{4,5},{5,4},{6,7},{7,6},{8,9},{9,8},{10,11... | collective-permute-start | bytes 221192 | tf_op jit(solution)/shard_map/ppermute | solution.py:325
  11.9 11.0 %collective-permute-start.1 = (bf16[9,32,128]{2,1,0:T(8,128)(2,1)S(1)}, bf16[9,32,128]{2,1,0:T(8,128)(2,1)S(1)}, u32[]{:S(2)}, u32[]{:S(2)}) collective-permute-start(bf16[9,32,128]{2,1,0:T(8,128)(2,1)S(1)} %collective-permute-done.prev0), channel_id=1, source_target_pairs={{0,1},{1,0},{2,3},{3,2},{4,5},{5,4},{6,7},{7,6},{8,9},{9,8},{10,11... | collective-permute-start | bytes 221192 | tf_op jit(solution)/shard_map/ppermute | solution.py:335
  11.9 12.7 %collective-permute-start.4 = (bf16[9,32,128]{2,1,0:T(8,128)(2,1)S(1)}, bf16[9,32,128]{2,1,0:T(8,128)(2,1)S(1)}, u32[]{:S(2)}, u32[]{:S(2)}) collective-permute-start(bf16[9,32,128]{2,1,0:T(8,128)(2,1)S(1)} %collective-permute-done.3.next0), channel_id=1, source_target_pairs={{0,1},{1,0},{2,3},{3,2},{4,5},{5,4},{6,7},{7,6},{8,9},{9,8},{10,11... | collective-permute-start | bytes 221192 | tf_op jit(solution)/shard_map/ppermute | solution.py:336
  12.4 7.2 %collective-permute-start.5 = (s32[2,3]{1,0:T(2,128)S(1)}, s32[2,3]{1,0:T(2,128)S(1)}, u32[]{:S(2)}, u32[]{:S(2)}) collective-permute-start(s32[2,3]{1,0:T(2,128)S(1)} %copy-done), channel_id=1, source_target_pairs={{0,2},{2,4},{4,6},{6,8},{8,10},{10,12},{12,14},{14,16},{16,18},{18... | collective-permute-start | bytes 80 | tf_op jit(solution)/shard_map/ppermute | solution.py:307
  21.6 4.3 %collective-permute-start.7 = (bf16[8,32,128]{2,1,0:T(8,128)(2,1)S(1)}, bf16[8,32,128]{2,1,0:T(8,128)(2,1)S(1)}, u32[]{:S(2)}, u32[]{:S(2)}) collective-permute-start(bf16[8,32,128]{2,1,0:T(8,128)(2,1)S(1)} %get-tuple-element.5), channel_id=1, source_target_pairs={{2,0},{4,2},{6,4},{8,6},{10,8},{12,10},{14,12},{16,14},{18,16},{20... | collective-permute-start | bytes 196616 | tf_op jit(solution)/shard_map/ppermute | solution.py:334

commit v4 on v3

--- a/solution.py
+++ b/solution.py
@@ -31,12 +31,20 @@
     return jnp.concatenate(tiles, 0)
 
 
-def pack_kernel(offs_hbm, kern_hbm, pat_hbm, orbs_hbm, out, offs, kern, pat, orb, sems):
+def pack_kernel(
+    offs_hbm, kern_hbm, pat_hbm, orbs_hbm, v_hbm, out, v_out, offs, kern, pat, orb, sems
+):
     core = lax.axis_index("bricks")
     copies = [
         pltpu.make_async_copy(src, dst, sems.at[n])
         for n, (src, dst) in enumerate(
-            ((offs_hbm, offs), (kern_hbm, kern), (pat_hbm, pat), (orbs_hbm.at[core], orb))
+            (
+                (offs_hbm, offs),
+                (kern_hbm, kern),
+                (pat_hbm, pat),
+                (orbs_hbm.at[core], orb),
+                (v_hbm, v_out),
+            )
         )
     ]
     for copy in copies:
@@ -45,7 +53,7 @@
     groups = LANES // side
     per = side // groups
     k_at, lane = iota((side, LANES), 0), iota((side, LANES), 1)
-    for copy in copies:
+    for copy in copies[:-1]:
         copy.wait()
     corner = [offs[core, axis] for axis in range(3)]
     o0, o1, o2 = corner
@@ -66,20 +74,13 @@
         high = w.astype(BF16).astype(F32)
         values += [high, w - high]
     out[per] = rows_splat(values, side).astype(BF16)
-
-
-def cut_kernel(packet, offs_prev, v_hbm, v_other, cut_own, cut_prev, v_own, sems):
+    copies[-1].wait()
+
+
+def cut_kernel(packet, offs_prev, v_own, v_other, cut_own, cut_prev):
     side, depth = v_own.shape[0], v_own.shape[1]
     groups = LANES // side
     per = side // groups
-    copies = [
-        pltpu.make_async_copy(
-            v_hbm.at[pl.ds(g * per, per)], v_own.at[pl.ds(g * per, per)], sems.at[g]
-        )
-        for g in range(groups)
-    ]
-    for copy in copies:
-        copy.start()
     core = lax.axis_index("bricks")
     meta = packet[packet.shape[0] - 1].astype(F32)
     line = jnp.where(core == 0, offs_prev[0:1, :], offs_prev[1:2, :])
@@ -87,29 +88,39 @@
         [meta[axis : axis + 1].astype(I32) for axis in range(3)],
         [jnp.broadcast_to(line[:, axis : axis + 1], (1, LANES)) for axis in range(3)],
     ]
-    at = iota((2 * LANES, LANES), 0)
-    lane = iota((1, LANES), 1)
-    z_at = jnp.where(at < LANES, core * LANES + at, (1 - core) * LANES + at - LANES)
-    picks = []
-    for _, _, o2 in corners:
-        picks.append(jnp.where(z_at == o2 + ((lane - o2) & (side - 1)), 1.0, 0.0))
-    pick = jnp.concatenate(picks, 1)
-    group = (iota((1, 2 * LANES), 1) & (LANES - 1)) // side
-    total = jnp.zeros((per * depth, 2 * LANES), F32)
+    lane = iota((side, LANES), 1)
+    row = iota((side, LANES), 0)
+    fold = jnp.where((lane & (side - 1)) == row, 1.0, 0.0).astype(BF16)
+    folds = []
     for g in range(groups):
-        here = jnp.where(group == g, 1.0, 0.0)
-        copies[g].wait()
-        left = v_own[g * per : (g + 1) * per].reshape(per * depth, LANES)
-        right = v_other[g * per : (g + 1) * per].reshape(per * depth, LANES)
-        both = jnp.concatenate([left.astype(BF16), right.astype(BF16)], 1)
-        total = total + jnp.dot(both, (pick * here).astype(BF16), preferred_element_type=F32)
-    row = iota((side, LANES), 0)
-    for t, cut in enumerate((cut_own, cut_prev)):
-        o1 = corners[t][1]
-        for i in range(per):
-            low = total[i * depth : i * depth + side, t * LANES : (t + 1) * LANES]
-            high = total[i * depth + depth - side : (i + 1) * depth, t * LANES : (t + 1) * LANES]
-            cut[i] = jnp.where(row >= o1, low, high).astype(BF16)
+        block = fold * jnp.where((lane // side) == g, 1.0, 0.0).astype(BF16)
+        folds += [block] * groups
+    folds = jnp.concatenate(folds, 0)
+    for (_, o1, o2), cut in zip(corners, (cut_own, cut_prev)):
+        upper = row < o1
+        mine = ((lane - o2) & (LANES - 1)) < side
+        start = o2 + ((lane - o2) & (LANES - 1))
+        own = mine & ((start // LANES) == core)
+        other = mine & ((start // LANES) != core)
+        masks = [
+            jnp.where(a & b, 1.0, 0.0).astype(BF16)
+            for a in (own, other)
+            for b in (~upper, upper)
+        ]
+        parts = []
+        for g in range(groups):
+            planes = []
+            for x in range(g * per, (g + 1) * per):
+                plane = None
+                for n, (v, at) in enumerate(
+                    ((v_own, 0), (v_own, depth - side), (v_other, 0), (v_other, depth - side))
+                ):
+                    term = v[x, at : at + side].astype(BF16) * masks[n]
+                    plane = term if plane is None else plane + term
+                planes.append(plane)
+            parts.append(jnp.concatenate(planes, 0))
+        out = jnp.dot(jnp.concatenate(parts, 1), folds, preferred_element_type=F32)
+        cut[...] = out.astype(BF16).reshape(per, side, LANES)
 
 
 class Tables:
@@ -129,7 +140,7 @@
         return self.weight(a, b) if a == b else self.weight(a, b) + self.weight(b, a)
 
 
-def brick_kernel(prev0, prev1, own0, own1, dens_hbm, dens, ready, placed, sems):
+def brick_kernel(prev0, prev1, own0, own1, dens, ready, placed):
     core = lax.axis_index("bricks")
     side = dens.shape[0]
     groups = LANES // side
@@ -174,7 +185,6 @@
         place = spread * jnp.concatenate([inside] * groups, 1)
         out = jnp.dot(ready[a], jnp.concatenate([place] * 2, 0), preferred_element_type=F32)
         placed[a] = out
-    copies = []
     for g in range(groups):
         for i in range(per):
             x = g * per + i
@@ -187,21 +197,29 @@
                 high = up if high is None else high + up
             dens[x, 0:side] = low
             dens[x, side : 2 * side] = high
-        copies.append(
-            pltpu.make_async_copy(
-                dens.at[pl.ds(g * per, per)], dens_hbm.at[pl.ds(g * per, per)], sems.at[g]
-            )
-        )
-        copies[-1].start()
-    for copy in copies:
-        copy.wait()
 
 
 def box_kernel(
-    offs_hbm, prev0, prev1, own0, own1, next0, next1, cut_own, cut_next, out, offs, grads, sem
+    offs_hbm,
+    prev0,
+    prev1,
+    own0,
+    own1,
+    next0,
+    next1,
+    cut_own,
+    cut_next,
+    dens,
+    dens_hbm,
+    out,
+    offs,
+    grads,
+    sems,
 ):
-    copy = pltpu.make_async_copy(offs_hbm, offs, sem)
+    copy = pltpu.make_async_copy(offs_hbm, offs, sems.at[0])
     copy.start()
+    whole = pltpu.make_async_copy(dens, dens_hbm, sems.at[1])
+    whole.start()
     core = lax.axis_index("bricks")
     side = out.shape[1]
     groups = LANES // side
@@ -274,9 +292,10 @@
         part = jnp.dot(stacked, gather, preferred_element_type=F32).astype(BF16)
         for i in range(per):
             out[0, (g * per + i - s0) & (side - 1)] = part[i * side : (i + 1) * side]
-
-
-def call(kernel, outs, out_specs, ins, args, scratch):
+    whole.wait()
+
+
+def call(kernel, outs, out_specs, ins, args, scratch, moved=2000000):
     return pl.pallas_call(
         kernel,
         out_shape=outs,
@@ -285,7 +304,7 @@
         scratch_shapes=scratch,
         compiler_params=pltpu.CompilerParams(vmem_limit_bytes=GRANT),
         cost_estimate=pl.CostEstimate(
-            flops=1000000, bytes_accessed=2000000, transcendentals=0
+            flops=1000000, bytes_accessed=moved, transcendentals=0
         ),
     )(*[
         pltpu.with_memory_space_constraint(x, pltpu.HBM) if spec is HBM else x
@@ -305,18 +324,18 @@
     shape = jax.ShapeDtypeStruct
     dma = pltpu.SemaphoreType.DMA
     offsets_prev = lax.ppermute(offsets, "atoms", up)
-    own = call(
+    own, mine = call(
         pack_kernel,
-        shape((per + 1, side, LANES), BF16),
-        VMEM,
-        [HBM] * 4,
-        (offsets, kernel, pattern, orbitals),
+        (shape((per + 1, side, LANES), BF16), shape(local_potential.shape, F32)),
+        (VMEM,) * 2,
+        [HBM] * 5,
+        (offsets, kernel, pattern, orbitals, local_potential),
         [
             pltpu.SMEM(offsets.shape, I32),
             pltpu.VMEM(kernel.shape, F32),
             pltpu.VMEM(pattern.shape, I32),
             pltpu.VMEM(orbitals.shape[1:], BF16),
-            dma((4,)),
+            dma((5,)),
         ],
     )
     prev = lax.ppermute(own, "atoms", up)
@@ -327,31 +346,29 @@
         cut_kernel,
         (shape((per, side, LANES), BF16),) * 2,
         (VMEM,) * 2,
-        [VMEM] * 2 + [HBM] + [VMEM],
-        (own, offsets_prev, local_potential, other),
-        [pltpu.VMEM(local_potential.shape, F32), dma((groups,))],
+        [VMEM] * 4,
+        (own, offsets_prev, mine, other),
+        [],
     )
     cut_next = lax.ppermute(cut_prev, "atoms", down)
     prev_mate = lax.ppermute(prev, "bricks", swap)
     following_mate = lax.ppermute(following, "bricks", swap)
-    density = call(
+    dens = call(
         brick_kernel,
         shape((side, depth, width), F32),
-        HBM,
+        VMEM,
         [VMEM] * 4,
         (prev, prev_mate, own, own_mate),
         [
-            pltpu.VMEM((side, depth, width), F32),
             pltpu.VMEM((2 * count, per * side, 2 * LANES), BF16),
             pltpu.VMEM((2 * count, per * side, groups * LANES), F32),
-            dma((groups,)),
         ],
     )
-    gradient = call(
+    density, gradient = call(
         box_kernel,
-        shape((1, side, side, side), BF16),
-        VMEM,
-        [HBM] + [VMEM] * 8,
+        (shape((side, depth, width), F32), shape((1, side, side, side), BF16)),
+        (HBM, VMEM),
+        [HBM] + [VMEM] * 9,
         (
             offsets,
             prev,
@@ -362,8 +379,9 @@
             following_mate,
             cut_own,
             cut_next,
+            dens,
         ),
-        [pltpu.SMEM(offsets.shape, I32), pltpu.VMEM((per, side, LANES), F32), dma(())],
+        [pltpu.SMEM(offsets.shape, I32), pltpu.VMEM((per, side, LANES), F32), dma((2,))],
     )
     return density, gradient
 

time: 27.7 us -> 26.4 us (0.953)
  Pallas kernels: 6.48 us -> 4.23 us
  waiting for transfers between devices: 11.1 us -> 12.1 us
    pallas_call x4, Pallas kernels: 6.48 us -> 4.23 us  [call(): pl.pallas_call(kernel, out_shape=outs, in_specs=ins, out_specs=out_specs,...]
    ppermute x1, waiting for transfers between devices: 1.26 us -> 2.23 us  [step(): cut_next = lax.ppermute(cut_prev, 'atoms', down)]
  transfers between devices with their start and end apart: 8 -> 8, of which waited for: 3 -> 3; matrix products, arithmetic and copies ran while one was open for 0% -> 0% of each run, Pallas kernels for 18% -> 10%
where the time goes in v4:
time: 26.4 us; the launch traced here: 26.2 us
  waiting for transfers between devices  12.1 us (46%)
  starting transfers between devices  9.23 us (35%)
  Pallas kernels  4.23 us (16%)
  between operations  0.67 us (3%)
    ppermute x1, waiting for transfers between devices, step(): offsets_prev = lax.ppermute(offsets, 'atoms', up)  7.17 us
    pallas_call x4, Pallas kernels, call(): pl.pallas_call(kernel, out_shape=outs, in_specs=ins, out_specs=out_specs,...  4.23 us
    ppermute x1, starting transfers between devices, step(): following = lax.ppermute(own, 'atoms', down)  4.06 us
    ppermute x1, waiting for transfers between devices, step(): prev = lax.ppermute(own, 'atoms', up)  2.65 us
    ppermute x1, starting transfers between devices, step(): prev = lax.ppermute(own, 'atoms', up)  2.55 us
    ppermute x1, waiting for transfers between devices, step(): cut_next = lax.ppermute(cut_prev, 'atoms', down)  2.23 us
    ppermute x1, starting transfers between devices, step(): cut_next = lax.ppermute(cut_prev, 'atoms', down)  1.34 us
    ppermute x1, starting transfers between devices, step(): other = lax.ppermute(local_potential, 'bricks', swap)  0.56 us
  transfers between devices with their start and end apart: 8, of which 3 were waited for; matrix products, arithmetic and copies ran while one was open for 0% of the time, Pallas kernels for 10%

profile of v4, /device:TPU:0, one launch (start us, length us, event | category | flops | bytes accessed | tf_op | source)
XLA Modules:
  0.0 26.2 jit_solution(15245761816368421478)
XLA Ops:
  0.6 0.6 %collective-permute-start.6 = (f32[32,64,128]{2,1,0:T(8,128)}, f32[32,64,128]{2,1,0:T(8,128)S(1)}, u32[]{:S(2)}, u32[]{:S(2)}) collective-permute-start(f32[32,64,128]{2,1,0:T(8,128)} %v_hbm.1), channel_id=1, source_target_pairs={{0,1},{1,0},{2,3},{3,2},{4,5},{5,4},{6,7},{7,6},{8,9},{9,8},{10,11... | collective-permute-start | bytes 3145736 | tf_op jit(solution)/shard_map/ppermute | solution.py:343
  1.2 1.4 %shard_map.68 = (bf16[9,32,128]{2,1,0:T(8,128)(2,1)S(1)}, f32[32,64,128]{2,1,0:T(8,128)S(1)}) custom-call(s32[2,3]{1,0:T(2,128)} %offs_hbm.3, f32[1,6]{1,0:T(1,128)} %kern_hbm.1, s32[1,6]{1,0:T(1,128)} %pat_hbm.1, bf16[2,32,32,32]{3,2,1,0:T(8,128)(2,1)} %orbs_hbm.1, f32[32,64,128]{2,1,0:T(8,128)} %v_hbm.1), custom_call_target="tpu_custom_call" | custom-call | flops 1000000 | bytes 2000000 | tf_op jit(solution)/shard_map/pallas_call | solution.py:299
  2.6 0.0 copy-start
  2.6 2.5 %collective-permute-start = (bf16[9,32,128]{2,1,0:T(8,128)(2,1)S(1)}, bf16[9,32,128]{2,1,0:T(8,128)(2,1)S(1)}, u32[]{:S(2)}, u32[]{:S(2)}) collective-permute-start(bf16[9,32,128]{2,1,0:T(8,128)(2,1)S(1)} %get-tuple-element.6.packet.own0), channel_id=1, source_target_pairs={{0,2},{2,4},{4,6},{6,8},{8,10},{10,12},{12,14},{14,16},{16,18},{18... | collective-permute-start | bytes 221192 | tf_op jit(solution)/shard_map/ppermute | solution.py:341
  5.1 4.1 %collective-permute-start.3 = (bf16[9,32,128]{2,1,0:T(8,128)(2,1)S(1)}, bf16[9,32,128]{2,1,0:T(8,128)(2,1)S(1)}, u32[]{:S(2)}, u32[]{:S(2)}) collective-permute-start(bf16[9,32,128]{2,1,0:T(8,128)(2,1)S(1)} %get-tuple-element.6.packet.own0), channel_id=1, source_target_pairs={{2,0},{4,2},{6,4},{8,6},{10,8},{12,10},{14,12},{16,14},{18,16},{20... | collective-permute-start | bytes 221192 | tf_op jit(solution)/shard_map/ppermute | solution.py:342
  9.2 0.2 collective-permute-start.2
  9.4 2.6 %collective-permute-done.prev0 = bf16[9,32,128]{2,1,0:T(8,128)(2,1)S(1)} collective-permute-done((bf16[9,32,128]{2,1,0:T(8,128)(2,1)S(1)}, bf16[9,32,128]{2,1,0:T(8,128)(2,1)S(1)}, u32[]{:S(2)}, u32[]{:S(2)}) %collective-permute-start) | collective-permute-done | bytes 73760 | tf_op jit(solution)/shard_map/ppermute | solution.py:341
  12.1 0.0 collective-permute-start.1
  12.1 0.0 collective-permute-done.3.next0
  12.1 0.5 %collective-permute-start.4 = (bf16[9,32,128]{2,1,0:T(8,128)(2,1)S(1)}, bf16[9,32,128]{2,1,0:T(8,128)(2,1)S(1)}, u32[]{:S(2)}, u32[]{:S(2)}) collective-permute-start(bf16[9,32,128]{2,1,0:T(8,128)(2,1)S(1)} %collective-permute-done.3.next0), channel_id=1, source_target_pairs={{0,1},{1,0},{2,3},{3,2},{4,5},{5,4},{6,7},{7,6},{8,9},{9,8},{10,11... | collective-permute-start | bytes 221192 | tf_op jit(solution)/shard_map/ppermute | solution.py:355
  12.6 0.0 copy-done
  12.6 0.0 collective-permute-start.5
  12.6 7.2 %collective-permute-done.5.offs_prev = s32[2,3]{1,0:T(2,128)S(1)} collective-permute-done((s32[2,3]{1,0:T(2,128)S(1)}, s32[2,3]{1,0:T(2,128)S(1)}, u32[]{:S(2)}, u32[]{:S(2)}) %collective-permute-start.5) | collective-permute-done | bytes 56 | tf_op jit(solution)/shard_map/ppermute | solution.py:326
  19.7 0.0 collective-permute-done.6.v_other
  19.8 0.4 %shard_map.69 = (bf16[8,32,128]{2,1,0:T(8,128)(2,1)S(1)}, bf16[8,32,128]{2,1,0:T(8,128)(2,1)S(1)}) custom-call(bf16[9,32,128]{2,1,0:T(8,128)(2,1)S(1)} %get-tuple-element.6.packet.own0, s32[2,3]{1,0:T(2,128)S(1)} %collective-permute-done.5.offs_prev, f32[32,64,128]{2,1,0:T(8,128)S(1)} %get-tuple-element.7.v_own, ...), custom_call_target="tpu_custom_call" | custom-call | flops 1000000 | bytes 2000000 | tf_op jit(solution)/shard_map/pallas_call | solution.py:299
  20.2 1.3 %collective-permute-start.7 = (bf16[8,32,128]{2,1,0:T(8,128)(2,1)S(1)}, bf16[8,32,128]{2,1,0:T(8,128)(2,1)S(1)}, u32[]{:S(2)}, u32[]{:S(2)}) collective-permute-start(bf16[8,32,128]{2,1,0:T(8,128)(2,1)S(1)} %get-tuple-element.9), channel_id=1, source_target_pairs={{2,0},{4,2},{6,4},{8,6},{10,8},{12,10},{14,12},{16,14},{18,16},{20... | collective-permute-start | bytes 196616 | tf_op jit(solution)/shard_map/ppermute | solution.py:353
  21.5 0.0 collective-permute-done.2.own1
  21.5 0.0 collective-permute-done.1.prev1
  21.5 0.7 %shard_map.70.dens = f32[32,64,128]{2,1,0:T(8,128)S(1)} custom-call(bf16[9,32,128]{2,1,0:T(8,128)(2,1)S(1)} %collective-permute-done.prev0, bf16[9,32,128]{2,1,0:T(8,128)(2,1)S(1)} %collective-permute-done.1.prev1, bf16[9,32,128]{2,1,0:T(8,128)(2,1)S(1)} %get-tuple-element.6.packet.own0, bf16[9,32,128]{2,1,0:T(8,128)(2,1)S(1)} %collective-permute-done.2.own1), custom_call_target="tpu_custom_call" | custom-call | flops 1000000 | bytes 2000000 | tf_op jit(solution)/shard_map/pallas_call | solution.py:299
  22.3 0.0 collective-permute-done.4.next1
  22.3 2.2 %collective-permute-done.7.cut_next = bf16[8,32,128]{2,1,0:T(8,128)(2,1)S(1)} collective-permute-done((bf16[8,32,128]{2,1,0:T(8,128)(2,1)S(1)}, bf16[8,32,128]{2,1,0:T(8,128)(2,1)S(1)}, u32[]{:S(2)}, u32[]{:S(2)}) %collective-permute-start.7) | collective-permute-done | bytes 65568 | tf_op jit(solution)/shard_map/ppermute | solution.py:353
  24.5 1.7 %shard_map.71 = (f32[32,64,128]{2,1,0:T(8,128)}, bf16[1,32,32,32]{3,2,1,0:T(8,128)(2,1)}) custom-call(s32[2,3]{1,0:T(2,128)} %offs_hbm.3, bf16[9,32,128]{2,1,0:T(8,128)(2,1)S(1)} %collective-permute-done.prev0, bf16[9,32,128]{2,1,0:T(8,128)(2,1)S(1)} %collective-permute-done.1.prev1, bf16[9,32,128]{2,1,0:T(8,128)(2,1)S(1)} %get-tuple-element.6.packet.own0, ...), custom_call_target="tpu_custom_call" | custom-call | flops 1000000 | bytes 2000000 | tf_op jit(solution)/shard_map/pallas_call | solution.py:299
Async XLA Ops:
  0.6 19.1 %collective-permute-start.6 = (f32[32,64,128]{2,1,0:T(8,128)}, f32[32,64,128]{2,1,0:T(8,128)S(1)}, u32[]{:S(2)}, u32[]{:S(2)}) collective-permute-start(f32[32,64,128]{2,1,0:T(8,128)} %v_hbm.1), channel_id=1, source_target_pairs={{0,1},{1,0},{2,3},{3,2},{4,5},{5,4},{6,7},{7,6},{8,9},{9,8},{10,11... | collective-permute-start | bytes 3145736 | tf_op jit(solution)/shard_map/ppermute | solution.py:343
  2.6 10.0 %copy-start = (s32[2,3]{1,0:T(2,128)S(1)}, s32[2,3]{1,0:T(2,128)}, u32[]{:S(2)}) copy-start(s32[2,3]{1,0:T(2,128)} %offs_hbm.3) | copy-start | bytes 76
  2.6 9.5 %collective-permute-start = (bf16[9,32,128]{2,1,0:T(8,128)(2,1)S(1)}, bf16[9,32,128]{2,1,0:T(8,128)(2,1)S(1)}, u32[]{:S(2)}, u32[]{:S(2)}) collective-permute-start(bf16[9,32,128]{2,1,0:T(8,128)(2,1)S(1)} %get-tuple-element.6.packet.own0), channel_id=1, source_target_pairs={{0,2},{2,4},{4,6},{6,8},{8,10},{10,12},{12,14},{14,16},{16,18},{18... | collective-permute-start | bytes 221192 | tf_op jit(solution)/shard_map/ppermute | solution.py:341
  5.1 6.9 %collective-permute-start.3 = (bf16[9,32,128]{2,1,0:T(8,128)(2,1)S(1)}, bf16[9,32,128]{2,1,0:T(8,128)(2,1)S(1)}, u32[]{:S(2)}, u32[]{:S(2)}) collective-permute-start(bf16[9,32,128]{2,1,0:T(8,128)(2,1)S(1)} %get-tuple-element.6.packet.own0), channel_id=1, source_target_pairs={{2,0},{4,2},{6,4},{8,6},{10,8},{12,10},{14,12},{16,14},{18,16},{20... | collective-permute-start | bytes 221192 | tf_op jit(solution)/shard_map/ppermute | solution.py:342
  9.2 12.3 %collective-permute-start.2 = (bf16[9,32,128]{2,1,0:T(8,128)(2,1)S(1)}, bf16[9,32,128]{2,1,0:T(8,128)(2,1)S(1)}, u32[]{:S(2)}, u32[]{:S(2)}) collective-permute-start(bf16[9,32,128]{2,1,0:T(8,128)(2,1)S(1)} %get-tuple-element.6.packet.own0), channel_id=1, source_target_pairs={{0,1},{1,0},{2,3},{3,2},{4,5},{5,4},{6,7},{7,6},{8,9},{9,8},{10,11... | collective-permute-start | bytes 221192 | tf_op jit(solution)/shard_map/ppermute | solution.py:344
  12.1 9.5 %collective-permute-start.1 = (bf16[9,32,128]{2,1,0:T(8,128)(2,1)S(1)}, bf16[9,32,128]{2,1,0:T(8,128)(2,1)S(1)}, u32[]{:S(2)}, u32[]{:S(2)}) collective-permute-start(bf16[9,32,128]{2,1,0:T(8,128)(2,1)S(1)} %collective-permute-done.prev0), channel_id=1, source_target_pairs={{0,1},{1,0},{2,3},{3,2},{4,5},{5,4},{6,7},{7,6},{8,9},{9,8},{10,11... | collective-permute-start | bytes 221192 | tf_op jit(solution)/shard_map/ppermute | solution.py:354
  12.1 10.2 %collective-permute-start.4 = (bf16[9,32,128]{2,1,0:T(8,128)(2,1)S(1)}, bf16[9,32,128]{2,1,0:T(8,128)(2,1)S(1)}, u32[]{:S(2)}, u32[]{:S(2)}) collective-permute-start(bf16[9,32,128]{2,1,0:T(8,128)(2,1)S(1)} %collective-permute-done.3.next0), channel_id=1, source_target_pairs={{0,1},{1,0},{2,3},{3,2},{4,5},{5,4},{6,7},{7,6},{8,9},{9,8},{10,11... | collective-permute-start | bytes 221192 | tf_op jit(solution)/shard_map/ppermute | solution.py:355
  12.6 7.2 %collective-permute-start.5 = (s32[2,3]{1,0:T(2,128)S(1)}, s32[2,3]{1,0:T(2,128)S(1)}, u32[]{:S(2)}, u32[]{:S(2)}) collective-permute-start(s32[2,3]{1,0:T(2,128)S(1)} %copy-done), channel_id=1, source_target_pairs={{0,2},{2,4},{4,6},{6,8},{8,10},{10,12},{12,14},{14,16},{16,18},{18... | collective-permute-start | bytes 80 | tf_op jit(solution)/shard_map/ppermute | solution.py:326
  20.2 4.3 %collective-permute-start.7 = (bf16[8,32,128]{2,1,0:T(8,128)(2,1)S(1)}, bf16[8,32,128]{2,1,0:T(8,128)(2,1)S(1)}, u32[]{:S(2)}, u32[]{:S(2)}) collective-permute-start(bf16[8,32,128]{2,1,0:T(8,128)(2,1)S(1)} %get-tuple-element.9), channel_id=1, source_target_pairs={{2,0},{4,2},{6,4},{8,6},{10,8},{12,10},{14,12},{16,14},{18,16},{20... | collective-permute-start | bytes 196616 | tf_op jit(solution)/shard_map/ppermute | solution.py:353

commit v5 on v4

--- a/solution.py
+++ b/solution.py
@@ -140,7 +140,7 @@
         return self.weight(a, b) if a == b else self.weight(a, b) + self.weight(b, a)
 
 
-def brick_kernel(prev0, prev1, own0, own1, dens, ready, placed):
+def fill_brick(prev0, prev1, own0, own1, dens, ready, placed):
     core = lax.axis_index("bricks")
     side = dens.shape[0]
     groups = LANES // side
@@ -199,31 +199,11 @@
             dens[x, side : 2 * side] = high
 
 
-def box_kernel(
-    offs_hbm,
-    prev0,
-    prev1,
-    own0,
-    own1,
-    next0,
-    next1,
-    cut_own,
-    cut_next,
-    dens,
-    dens_hbm,
-    out,
-    offs,
-    grads,
-    sems,
+def mid_kernel(
+    prev0, prev1, own0, own1, next0, next1, dens, mixed, bend, ready, placed
 ):
-    copy = pltpu.make_async_copy(offs_hbm, offs, sems.at[0])
-    copy.start()
-    whole = pltpu.make_async_copy(dens, dens_hbm, sems.at[1])
-    whole.start()
-    core = lax.axis_index("bricks")
-    side = out.shape[1]
-    groups = LANES // side
-    per = side // groups
+    side, per = own0.shape[1], own0.shape[0] - 1
+    fill_brick(prev0, prev1, own0, own1, dens, ready, placed)
     packets = (prev0, prev1, own0, own1, next0, next1)
     tables = Tables(packets, ((0, 0), (0, 1), (1, 0), (1, 1), (2, 0), (2, 1)))
     me, mate = 2, 3
@@ -277,13 +257,29 @@
         for b in range(4):
             term = pick(mine[b], b, me) * fields[b]
             mix = term if mix is None else mix + term
-        bend = rho * lax.rsqrt(1.0 + rho * rho)
+        mixed[i] = mix
+        bend[i] = rho * lax.rsqrt(1.0 + rho * rho)
+
+
+def last_kernel(own, cut_own, cut_next, mixed, bend, dens, dens_hbm, out_hbm, out, sems):
+    copies = [
+        pltpu.make_async_copy(dens, dens_hbm, sems.at[0]),
+        pltpu.make_async_copy(out, out_hbm, sems.at[1]),
+    ]
+    copies[0].start()
+    side = out.shape[1]
+    groups = LANES // side
+    per = side // groups
+    corner = own[per, 0:SUB].astype(F32).astype(I32)
+    s0, s1, s2 = [corner[axis, 0] for axis in range(3)]
+    lane = iota((1, LANES), 1)
+    planes = []
+    for i in range(per):
+        spill = (lane // side) * per + i < s0
         outer = jnp.where(spill, cut_next[i].astype(F32), cut_own[i].astype(F32))
-        potential = (outer + bend).astype(BF16).astype(F32)
-        grads[i] = 2.0 * potential * mix
-    copy.wait()
-    s0, s1, s2 = offs[core, 0], offs[core, 1], offs[core, 2]
-    planes = [pltpu.roll(grads[i], (side - s1) & (side - 1), 0).astype(BF16) for i in range(per)]
+        potential = (outer + bend[i]).astype(BF16).astype(F32)
+        grad = 2.0 * potential * mixed[i]
+        planes.append(pltpu.roll(grad, (side - s1) & (side - 1), 0).astype(BF16))
     stacked = jnp.concatenate(planes, 0)
     from_lane, to = iota((LANES, side), 0), iota((LANES, side), 1)
     turned = (from_lane & (side - 1)) == ((to + s2) & (side - 1))
@@ -292,7 +288,9 @@
         part = jnp.dot(stacked, gather, preferred_element_type=F32).astype(BF16)
         for i in range(per):
             out[0, (g * per + i - s0) & (side - 1)] = part[i * side : (i + 1) * side]
-    whole.wait()
+    copies[1].start()
+    for copy in copies:
+        copy.wait()
 
 
 def call(kernel, outs, out_specs, ins, args, scratch, moved=2000000):
@@ -353,35 +351,24 @@
     cut_next = lax.ppermute(cut_prev, "atoms", down)
     prev_mate = lax.ppermute(prev, "bricks", swap)
     following_mate = lax.ppermute(following, "bricks", swap)
-    dens = call(
-        brick_kernel,
-        shape((side, depth, width), F32),
-        VMEM,
-        [VMEM] * 4,
-        (prev, prev_mate, own, own_mate),
+    dens, mixed, bend = call(
+        mid_kernel,
+        (shape((side, depth, width), F32),) + (shape((per, side, LANES), F32),) * 2,
+        (VMEM,) * 3,
+        [VMEM] * 6,
+        (prev, prev_mate, own, own_mate, following, following_mate),
         [
             pltpu.VMEM((2 * count, per * side, 2 * LANES), BF16),
             pltpu.VMEM((2 * count, per * side, groups * LANES), F32),
         ],
     )
     density, gradient = call(
-        box_kernel,
+        last_kernel,
         (shape((side, depth, width), F32), shape((1, side, side, side), BF16)),
-        (HBM, VMEM),
-        [HBM] + [VMEM] * 9,
-        (
-            offsets,
-            prev,
-            prev_mate,
-            own,
-            own_mate,
-            following,
-            following_mate,
-            cut_own,
-            cut_next,
-            dens,
-        ),
-        [pltpu.SMEM(offsets.shape, I32), pltpu.VMEM((per, side, LANES), F32), dma((2,))],
+        (HBM,) * 2,
+        [VMEM] * 6,
+        (own, cut_own, cut_next, mixed, bend, dens),
+        [pltpu.VMEM((1, side, side, side), BF16), dma((2,))],
     )
     return density, gradient
 

time: 26.4 us -> 30.3 us (1.15)
  waiting for transfers between devices: 12.1 us -> 18.1 us
  starting transfers between devices: 9.23 us -> 7.38 us
    ppermute x1, waiting for transfers between devices: 2.65 us -> 5.79 us  [step(): prev = lax.ppermute(own, 'atoms', up)]
    ppermute x1, starting transfers between devices: 2.55 us -> 0.01 us  [step(): prev = lax.ppermute(own, 'atoms', up)]
    ppermute x1, starting transfers between devices: 4.06 us -> 6.54 us  [step(): following = lax.ppermute(own, 'atoms', down)]
    ppermute x1, waiting for transfers between devices: 0.01 us -> 1.97 us  [step(): following = lax.ppermute(own, 'atoms', down)]
    ppermute x1, starting transfers between devices: 1.34 us -> 0.06 us  [step(): cut_next = lax.ppermute(cut_prev, 'atoms', down)]
    ppermute x1, waiting for transfers between devices: 2.23 us -> 3.19 us  [step(): cut_next = lax.ppermute(cut_prev, 'atoms', down)]
    ppermute x1, starting transfers between devices: 0.51 us -> 0.01 us  [step(): following_mate = lax.ppermute(following, 'bricks', swap)]
  transfers between devices with their start and end apart: 8 -> 8, of which waited for: 3 -> 4; matrix products, arithmetic and copies ran while one was open for 0% -> 0% of each run, Pallas kernels for 10% -> 9%
where the time goes in v5:
time: 30.3 us; the launch traced here: 30.2 us
  waiting for transfers between devices  18.1 us (60%)
  starting transfers between devices  7.38 us (24%)
  Pallas kernels  3.97 us (13%)
  between operations  0.7 us (2%)
    ppermute x1, waiting for transfers between devices, step(): offsets_prev = lax.ppermute(offsets, 'atoms', up)  7.16 us
    ppermute x1, starting transfers between devices, step(): following = lax.ppermute(own, 'atoms', down)  6.54 us
    ppermute x1, waiting for transfers between devices, step(): prev = lax.ppermute(own, 'atoms', up)  5.79 us
    pallas_call x4, Pallas kernels, call(): pl.pallas_call(kernel, out_shape=outs, in_specs=ins, out_specs=out_specs,...  3.97 us
    ppermute x1, waiting for transfers between devices, step(): cut_next = lax.ppermute(cut_prev, 'atoms', down)  3.19 us
    ppermute x1, waiting for transfers between devices, step(): following = lax.ppermute(own, 'atoms', down)  1.97 us
  transfers between devices with their start and end apart: 8, of which 4 were waited for; matrix products, arithmetic and copies ran while one was open for 0% of the time, Pallas kernels for 9%

profile of v5, /device:TPU:0, one launch (start us, length us, event | category | flops | bytes accessed | tf_op | source)
XLA Modules:
  0.0 30.2 jit_solution(15964386907731815151)
XLA Ops:
  0.6 0.6 %collective-permute-start.1 = (f32[32,64,128]{2,1,0:T(8,128)}, f32[32,64,128]{2,1,0:T(8,128)S(1)}, u32[]{:S(2)}, u32[]{:S(2)}) collective-permute-start(f32[32,64,128]{2,1,0:T(8,128)} %v_hbm.1), channel_id=1, source_target_pairs={{0,1},{1,0},{2,3},{3,2},{4,5},{5,4},{6,7},{7,6},{8,9},{9,8},{10,11... | collective-permute-start | bytes 3145736 | tf_op jit(solution)/shard_map/ppermute | solution.py:341
  1.2 1.4 %shard_map.68 = (bf16[9,32,128]{2,1,0:T(8,128)(2,1)S(1)}, f32[32,64,128]{2,1,0:T(8,128)S(1)}) custom-call(s32[2,3]{1,0:T(2,128)} %offs_hbm.1, f32[1,6]{1,0:T(1,128)} %kern_hbm.1, s32[1,6]{1,0:T(1,128)} %pat_hbm.1, bf16[2,32,32,32]{3,2,1,0:T(8,128)(2,1)} %orbs_hbm.1, f32[32,64,128]{2,1,0:T(8,128)} %v_hbm.1), custom_call_target="tpu_custom_call" | custom-call | flops 1000000 | bytes 2000000 | tf_op jit(solution)/shard_map/pallas_call | solution.py:297
  2.6 0.0 copy-start
  2.6 6.5 %collective-permute-start.6 = (bf16[9,32,128]{2,1,0:T(8,128)(2,1)S(1)}, bf16[9,32,128]{2,1,0:T(8,128)(2,1)S(1)}, u32[]{:S(2)}, u32[]{:S(2)}) collective-permute-start(bf16[9,32,128]{2,1,0:T(8,128)(2,1)S(1)} %get-tuple-element.9.packet.own0.own), channel_id=1, source_target_pairs={{2,0},{4,2},{6,4},{8,6},{10,8},{12,10},{14,12},{16,14},{18,16},{20... | collective-permute-start | bytes 221192 | tf_op jit(solution)/shard_map/ppermute | solution.py:340
  9.1 0.0 collective-permute-start.3
  9.1 0.2 collective-permute-start.5
  9.3 2.0 %collective-permute-done.6.next0 = bf16[9,32,128]{2,1,0:T(8,128)(2,1)S(1)} collective-permute-done((bf16[9,32,128]{2,1,0:T(8,128)(2,1)S(1)}, bf16[9,32,128]{2,1,0:T(8,128)(2,1)S(1)}, u32[]{:S(2)}, u32[]{:S(2)}) %collective-permute-start.6) | collective-permute-done | bytes 73760 | tf_op jit(solution)/shard_map/ppermute | solution.py:340
  11.3 0.0 collective-permute-start.7
  11.3 5.8 %collective-permute-done.3.prev0 = bf16[9,32,128]{2,1,0:T(8,128)(2,1)S(1)} collective-permute-done((bf16[9,32,128]{2,1,0:T(8,128)(2,1)S(1)}, bf16[9,32,128]{2,1,0:T(8,128)(2,1)S(1)}, u32[]{:S(2)}, u32[]{:S(2)}) %collective-permute-start.3) | collective-permute-done | bytes 73760 | tf_op jit(solution)/shard_map/ppermute | solution.py:339
  17.1 0.0 collective-permute-start.4
  17.1 0.0 copy-done
  17.1 0.0 collective-permute-start
  17.1 7.2 %collective-permute-done.offs_prev = s32[2,3]{1,0:T(2,128)S(1)} collective-permute-done((s32[2,3]{1,0:T(2,128)S(1)}, s32[2,3]{1,0:T(2,128)S(1)}, u32[]{:S(2)}, u32[]{:S(2)}) %collective-permute-start) | collective-permute-done | bytes 56 | tf_op jit(solution)/shard_map/ppermute | solution.py:324
  24.3 0.0 collective-permute-done.1.v_other
  24.3 0.4 %shard_map.69 = (bf16[8,32,128]{2,1,0:T(8,128)(2,1)S(1)}, bf16[8,32,128]{2,1,0:T(8,128)(2,1)S(1)}) custom-call(bf16[9,32,128]{2,1,0:T(8,128)(2,1)S(1)} %get-tuple-element.9.packet.own0.own, s32[2,3]{1,0:T(2,128)S(1)} %collective-permute-done.offs_prev, f32[32,64,128]{2,1,0:T(8,128)S(1)} %get-tuple-element.10.v_own, ...), custom_call_target="tpu_custom_call" | custom-call | flops 1000000 | bytes 2000000 | tf_op jit(solution)/shard_map/pallas_call | solution.py:297
  24.7 0.1 collective-permute-start.2
  24.8 0.0 collective-permute-done.5.own1
  24.8 0.0 collective-permute-done.7.next1
  24.8 0.0 collective-permute-done.4.prev1
  24.8 1.0 %shard_map.70 = (f32[32,64,128]{2,1,0:T(8,128)S(1)}, f32[8,32,128]{2,1,0:T(8,128)S(1)}, f32[8,32,128]{2,1,0:T(8,128)S(1)}) custom-call(bf16[9,32,128]{2,1,0:T(8,128)(2,1)S(1)} %collective-permute-done.3.prev0, bf16[9,32,128]{2,1,0:T(8,128)(2,1)S(1)} %collective-permute-done.4.prev1, bf16[9,32,128]{2,1,0:T(8,128)(2,1)S(1)} %get-tuple-element.9.packet.own0.own, ...), custom_call_target="tpu_custom_call" | custom-call | flops 1000000 | bytes 2000000 | tf_op jit(solution)/shard_map/pallas_call | solution.py:297
  25.9 3.2 %collective-permute-done.2.cut_next = bf16[8,32,128]{2,1,0:T(8,128)(2,1)S(1)} collective-permute-done((bf16[8,32,128]{2,1,0:T(8,128)(2,1)S(1)}, bf16[8,32,128]{2,1,0:T(8,128)(2,1)S(1)}, u32[]{:S(2)}, u32[]{:S(2)}) %collective-permute-start.2) | collective-permute-done | bytes 65568 | tf_op jit(solution)/shard_map/ppermute | solution.py:351
  29.1 1.1 %shard_map.71 = (f32[32,64,128]{2,1,0:T(8,128)}, bf16[1,32,32,32]{3,2,1,0:T(8,128)(2,1)}) custom-call(bf16[9,32,128]{2,1,0:T(8,128)(2,1)S(1)} %get-tuple-element.9.packet.own0.own, bf16[8,32,128]{2,1,0:T(8,128)(2,1)S(1)} %get-tuple-element.11.cut_own, bf16[8,32,128]{2,1,0:T(8,128)(2,1)S(1)} %collective-permute-done.2.cut_next, ...), custom_call_target="tpu_custom_call" | custom-call | flops 1000000 | bytes 2000000 | tf_op jit(solution)/shard_map/pallas_call | solution.py:297
Async XLA Ops:
  0.6 23.7 %collective-permute-start.1 = (f32[32,64,128]{2,1,0:T(8,128)}, f32[32,64,128]{2,1,0:T(8,128)S(1)}, u32[]{:S(2)}, u32[]{:S(2)}) collective-permute-start(f32[32,64,128]{2,1,0:T(8,128)} %v_hbm.1), channel_id=1, source_target_pairs={{0,1},{1,0},{2,3},{3,2},{4,5},{5,4},{6,7},{7,6},{8,9},{9,8},{10,11... | collective-permute-start | bytes 3145736 | tf_op jit(solution)/shard_map/ppermute | solution.py:341
  2.6 14.5 %copy-start = (s32[2,3]{1,0:T(2,128)S(1)}, s32[2,3]{1,0:T(2,128)}, u32[]{:S(2)}) copy-start(s32[2,3]{1,0:T(2,128)} %offs_hbm.1) | copy-start | bytes 76
  2.6 8.7 %collective-permute-start.6 = (bf16[9,32,128]{2,1,0:T(8,128)(2,1)S(1)}, bf16[9,32,128]{2,1,0:T(8,128)(2,1)S(1)}, u32[]{:S(2)}, u32[]{:S(2)}) collective-permute-start(bf16[9,32,128]{2,1,0:T(8,128)(2,1)S(1)} %get-tuple-element.9.packet.own0.own), channel_id=1, source_target_pairs={{2,0},{4,2},{6,4},{8,6},{10,8},{12,10},{14,12},{16,14},{18,16},{20... | collective-permute-start | bytes 221192 | tf_op jit(solution)/shard_map/ppermute | solution.py:340
  9.1 8.0 %collective-permute-start.3 = (bf16[9,32,128]{2,1,0:T(8,128)(2,1)S(1)}, bf16[9,32,128]{2,1,0:T(8,128)(2,1)S(1)}, u32[]{:S(2)}, u32[]{:S(2)}) collective-permute-start(bf16[9,32,128]{2,1,0:T(8,128)(2,1)S(1)} %get-tuple-element.9.packet.own0.own), channel_id=1, source_target_pairs={{0,2},{2,4},{4,6},{6,8},{8,10},{10,12},{12,14},{14,16},{16,18},{18... | collective-permute-start | bytes 221192 | tf_op jit(solution)/shard_map/ppermute | solution.py:339
  9.1 15.7 %collective-permute-start.5 = (bf16[9,32,128]{2,1,0:T(8,128)(2,1)S(1)}, bf16[9,32,128]{2,1,0:T(8,128)(2,1)S(1)}, u32[]{:S(2)}, u32[]{:S(2)}) collective-permute-start(bf16[9,32,128]{2,1,0:T(8,128)(2,1)S(1)} %get-tuple-element.9.packet.own0.own), channel_id=1, source_target_pairs={{0,1},{1,0},{2,3},{3,2},{4,5},{5,4},{6,7},{7,6},{8,9},{9,8},{10,11... | collective-permute-start | bytes 221192 | tf_op jit(solution)/shard_map/ppermute | solution.py:342
  11.3 13.5 %collective-permute-start.7 = (bf16[9,32,128]{2,1,0:T(8,128)(2,1)S(1)}, bf16[9,32,128]{2,1,0:T(8,128)(2,1)S(1)}, u32[]{:S(2)}, u32[]{:S(2)}) collective-permute-start(bf16[9,32,128]{2,1,0:T(8,128)(2,1)S(1)} %collective-permute-done.6.next0), channel_id=1, source_target_pairs={{0,1},{1,0},{2,3},{3,2},{4,5},{5,4},{6,7},{7,6},{8,9},{9,8},{10,11... | collective-permute-start | bytes 221192 | tf_op jit(solution)/shard_map/ppermute | solution.py:353
  17.1 7.7 %collective-permute-start.4 = (bf16[9,32,128]{2,1,0:T(8,128)(2,1)S(1)}, bf16[9,32,128]{2,1,0:T(8,128)(2,1)S(1)}, u32[]{:S(2)}, u32[]{:S(2)}) collective-permute-start(bf16[9,32,128]{2,1,0:T(8,128)(2,1)S(1)} %collective-permute-done.3.prev0), channel_id=1, source_target_pairs={{0,1},{1,0},{2,3},{3,2},{4,5},{5,4},{6,7},{7,6},{8,9},{9,8},{10,11... | collective-permute-start | bytes 221192 | tf_op jit(solution)/shard_map/ppermute | solution.py:352
  17.1 7.2 %collective-permute-start = (s32[2,3]{1,0:T(2,128)S(1)}, s32[2,3]{1,0:T(2,128)S(1)}, u32[]{:S(2)}, u32[]{:S(2)}) collective-permute-start(s32[2,3]{1,0:T(2,128)S(1)} %copy-done), channel_id=1, source_target_pairs={{0,2},{2,4},{4,6},{6,8},{8,10},{10,12},{12,14},{14,16},{16,18},{18... | collective-permute-start | bytes 80 | tf_op jit(solution)/shard_map/ppermute | solution.py:324
  24.7 4.3 %collective-permute-start.2 = (bf16[8,32,128]{2,1,0:T(8,128)(2,1)S(1)}, bf16[8,32,128]{2,1,0:T(8,128)(2,1)S(1)}, u32[]{:S(2)}, u32[]{:S(2)}) collective-permute-start(bf16[8,32,128]{2,1,0:T(8,128)(2,1)S(1)} %get-tuple-element.12), channel_id=1, source_target_pairs={{2,0},{4,2},{6,4},{8,6},{10,8},{12,10},{14,12},{16,14},{18,16},{20... | collective-permute-start | bytes 196616 | tf_op jit(solution)/shard_map/ppermute | solution.py:351

commit v6 on v5

--- a/solution.py
+++ b/solution.py
@@ -53,28 +53,32 @@
     groups = LANES // side
     per = side // groups
     k_at, lane = iota((side, LANES), 0), iota((side, LANES), 1)
-    for copy in copies[:-1]:
+    for copy in copies[:3]:
         copy.wait()
-    corner = [offs[core, axis] for axis in range(3)]
+    table = offs[...]
+    corner = [jnp.where(core == 0, table[0, axis], table[1, axis]) for axis in range(3)]
     o0, o1, o2 = corner
-    turned = (lane & (side - 1)) == ((k_at + o2) & (side - 1))
+    turned = jnp.where((lane & (side - 1)) == ((k_at + o2) & (side - 1)), 1.0, 0.0)
+    spreads = [jnp.where((lane // side) == g, turned, 0.0).astype(BF16) for g in range(groups)]
+    values = [jnp.full((1, LANES), m, I32).astype(F32) for m in corner] + [None] * (SUB - 3)
+    line = kern[...] * pat[...].astype(F32)
+    wide = [jnp.broadcast_to(line[:, c : c + 1], (1, LANES)) for c in range(3 * count)]
+    for c in range(3 * count):
+        w = jnp.where(core == 0, wide[c], wide[c ^ 1])
+        high = w.astype(BF16).astype(F32)
+        values += [high, w - high]
+    out[per] = rows_splat(values, side).astype(BF16)
+    copies[3].wait()
     total = jnp.zeros((per * side, LANES), F32)
     for g in range(groups):
-        spread = jnp.where(turned & ((lane // side) == g), 1.0, 0.0).astype(BF16)
         planes = [orb[(g * per + i - o0) & (side - 1)] for i in range(per)]
-        total = total + jnp.dot(jnp.concatenate(planes, 0), spread, preferred_element_type=F32)
+        total = total + jnp.dot(
+            jnp.concatenate(planes, 0), spreads[g], preferred_element_type=F32
+        )
     for i in range(per):
         plane = pltpu.roll(total[i * side : (i + 1) * side], o1 & (side - 1), 0)
         out[i] = plane.astype(BF16)
-    values = [jnp.full((1, LANES), m, I32).astype(F32) for m in corner] + [None] * (SUB - 3)
-    line = kern[...] * pat[...].astype(F32)
-    spread = [jnp.broadcast_to(line[:, c : c + 1], (1, LANES)) for c in range(3 * count)]
-    for c in range(3 * count):
-        w = jnp.where(core == 0, spread[c], spread[c ^ 1])
-        high = w.astype(BF16).astype(F32)
-        values += [high, w - high]
-    out[per] = rows_splat(values, side).astype(BF16)
-    copies[-1].wait()
+    copies[4].wait()
 
 
 def cut_kernel(packet, offs_prev, v_own, v_other, cut_own, cut_prev):
@@ -102,21 +106,21 @@
         start = o2 + ((lane - o2) & (LANES - 1))
         own = mine & ((start // LANES) == core)
         other = mine & ((start // LANES) != core)
-        masks = [
-            jnp.where(a & b, 1.0, 0.0).astype(BF16)
-            for a in (own, other)
-            for b in (~upper, upper)
+        high, left, right = [
+            jnp.where(m, 1.0, 0.0).astype(BF16) > 0 for m in (upper, own, other)
         ]
+        zero = jnp.zeros((side, LANES), BF16)
         parts = []
         for g in range(groups):
             planes = []
             for x in range(g * per, (g + 1) * per):
-                plane = None
-                for n, (v, at) in enumerate(
-                    ((v_own, 0), (v_own, depth - side), (v_other, 0), (v_other, depth - side))
-                ):
-                    term = v[x, at : at + side].astype(BF16) * masks[n]
-                    plane = term if plane is None else plane + term
+                one, two = [
+                    jnp.where(
+                        high, v[x, depth - side :].astype(BF16), v[x, 0:side].astype(BF16)
+                    )
+                    for v in (v_own, v_other)
+                ]
+                plane = jnp.where(left, one, jnp.where(right, two, zero))
                 planes.append(plane)
             parts.append(jnp.concatenate(planes, 0))
         out = jnp.dot(jnp.concatenate(parts, 1), folds, preferred_element_type=F32)
@@ -329,7 +333,7 @@
         [HBM] * 5,
         (offsets, kernel, pattern, orbitals, local_potential),
         [
-            pltpu.SMEM(offsets.shape, I32),
+            pltpu.VMEM(offsets.shape, I32),
             pltpu.VMEM(kernel.shape, F32),
             pltpu.VMEM(pattern.shape, I32),
             pltpu.VMEM(orbitals.shape[1:], BF16),

time: 30.3 us -> 30.3 us (level)
  no operation moved by 1% of the time
where the time goes in v6:
time: 30.3 us; the launch traced here: 30.2 us
  waiting for transfers between devices  18.1 us (60%)
  starting transfers between devices  7.38 us (24%)
  Pallas kernels  3.97 us (13%)
  between operations  0.71 us (2%)
    ppermute x1, waiting for transfers between devices, step(): offsets_prev = lax.ppermute(offsets, 'atoms', up)  7.16 us
    ppermute x1, starting transfers between devices, step(): following = lax.ppermute(own, 'atoms', down)  6.54 us
    ppermute x1, waiting for transfers between devices, step(): prev = lax.ppermute(own, 'atoms', up)  5.79 us
    pallas_call x4, Pallas kernels, call(): pl.pallas_call(kernel, out_shape=outs, in_specs=ins, out_specs=out_specs,...  3.97 us
    ppermute x1, waiting for transfers between devices, step(): cut_next = lax.ppermute(cut_prev, 'atoms', down)  3.19 us
    ppermute x1, waiting for transfers between devices, step(): following = lax.ppermute(own, 'atoms', down)  1.97 us
  transfers between devices with their start and end apart: 8, of which 4 were waited for; matrix products, arithmetic and copies ran while one was open for 0% of the time, Pallas kernels for 9%

profile of v6, /device:TPU:0, one launch (start us, length us, event | category | flops | bytes accessed | tf_op | source)
XLA Modules:
  0.0 30.2 jit_solution(14308297121830476283)
XLA Ops:
  0.6 0.6 %collective-permute-start.1 = (f32[32,64,128]{2,1,0:T(8,128)}, f32[32,64,128]{2,1,0:T(8,128)S(1)}, u32[]{:S(2)}, u32[]{:S(2)}) collective-permute-start(f32[32,64,128]{2,1,0:T(8,128)} %v_hbm.1), channel_id=1, source_target_pairs={{0,1},{1,0},{2,3},{3,2},{4,5},{5,4},{6,7},{7,6},{8,9},{9,8},{10,11... | collective-permute-start | bytes 3145736 | tf_op jit(solution)/shard_map/ppermute | solution.py:345
  1.2 1.4 %shard_map.68 = (bf16[9,32,128]{2,1,0:T(8,128)(2,1)S(1)}, f32[32,64,128]{2,1,0:T(8,128)S(1)}) custom-call(s32[2,3]{1,0:T(2,128)} %offs_hbm.1, f32[1,6]{1,0:T(1,128)} %kern_hbm.1, s32[1,6]{1,0:T(1,128)} %pat_hbm.1, bf16[2,32,32,32]{3,2,1,0:T(8,128)(2,1)} %orbs_hbm.1, f32[32,64,128]{2,1,0:T(8,128)} %v_hbm.1), custom_call_target="tpu_custom_call" | custom-call | flops 1000000 | bytes 2000000 | tf_op jit(solution)/shard_map/pallas_call | solution.py:301
  2.6 0.0 copy-start
  2.6 6.5 %collective-permute-start.6 = (bf16[9,32,128]{2,1,0:T(8,128)(2,1)S(1)}, bf16[9,32,128]{2,1,0:T(8,128)(2,1)S(1)}, u32[]{:S(2)}, u32[]{:S(2)}) collective-permute-start(bf16[9,32,128]{2,1,0:T(8,128)(2,1)S(1)} %get-tuple-element.9.packet.own0.own), channel_id=1, source_target_pairs={{2,0},{4,2},{6,4},{8,6},{10,8},{12,10},{14,12},{16,14},{18,16},{20... | collective-permute-start | bytes 221192 | tf_op jit(solution)/shard_map/ppermute | solution.py:344
  9.1 0.0 collective-permute-start.3
  9.1 0.2 collective-permute-start.5
  9.4 2.0 %collective-permute-done.6.next0 = bf16[9,32,128]{2,1,0:T(8,128)(2,1)S(1)} collective-permute-done((bf16[9,32,128]{2,1,0:T(8,128)(2,1)S(1)}, bf16[9,32,128]{2,1,0:T(8,128)(2,1)S(1)}, u32[]{:S(2)}, u32[]{:S(2)}) %collective-permute-start.6) | collective-permute-done | bytes 73760 | tf_op jit(solution)/shard_map/ppermute | solution.py:344
  11.3 0.0 collective-permute-start.7
  11.3 5.8 %collective-permute-done.3.prev0 = bf16[9,32,128]{2,1,0:T(8,128)(2,1)S(1)} collective-permute-done((bf16[9,32,128]{2,1,0:T(8,128)(2,1)S(1)}, bf16[9,32,128]{2,1,0:T(8,128)(2,1)S(1)}, u32[]{:S(2)}, u32[]{:S(2)}) %collective-permute-start.3) | collective-permute-done | bytes 73760 | tf_op jit(solution)/shard_map/ppermute | solution.py:343
  17.1 0.0 collective-permute-start.4
  17.1 0.0 copy-done
  17.1 0.0 collective-permute-start
  17.1 7.2 %collective-permute-done.offs_prev = s32[2,3]{1,0:T(2,128)S(1)} collective-permute-done((s32[2,3]{1,0:T(2,128)S(1)}, s32[2,3]{1,0:T(2,128)S(1)}, u32[]{:S(2)}, u32[]{:S(2)}) %collective-permute-start) | collective-permute-done | bytes 56 | tf_op jit(solution)/shard_map/ppermute | solution.py:328
  24.3 0.0 collective-permute-done.1.v_other
  24.3 0.4 %shard_map.69 = (bf16[8,32,128]{2,1,0:T(8,128)(2,1)S(1)}, bf16[8,32,128]{2,1,0:T(8,128)(2,1)S(1)}) custom-call(bf16[9,32,128]{2,1,0:T(8,128)(2,1)S(1)} %get-tuple-element.9.packet.own0.own, s32[2,3]{1,0:T(2,128)S(1)} %collective-permute-done.offs_prev, f32[32,64,128]{2,1,0:T(8,128)S(1)} %get-tuple-element.10.v_own, ...), custom_call_target="tpu_custom_call" | custom-call | flops 1000000 | bytes 2000000 | tf_op jit(solution)/shard_map/pallas_call | solution.py:301
  24.7 0.1 collective-permute-start.2
  24.8 0.0 collective-permute-done.5.own1
  24.8 0.0 collective-permute-done.7.next1
  24.8 0.0 collective-permute-done.4.prev1
  24.8 1.0 %shard_map.70 = (f32[32,64,128]{2,1,0:T(8,128)S(1)}, f32[8,32,128]{2,1,0:T(8,128)S(1)}, f32[8,32,128]{2,1,0:T(8,128)S(1)}) custom-call(bf16[9,32,128]{2,1,0:T(8,128)(2,1)S(1)} %collective-permute-done.3.prev0, bf16[9,32,128]{2,1,0:T(8,128)(2,1)S(1)} %collective-permute-done.4.prev1, bf16[9,32,128]{2,1,0:T(8,128)(2,1)S(1)} %get-tuple-element.9.packet.own0.own, ...), custom_call_target="tpu_custom_call" | custom-call | flops 1000000 | bytes 2000000 | tf_op jit(solution)/shard_map/pallas_call | solution.py:301
  25.9 3.2 %collective-permute-done.2.cut_next = bf16[8,32,128]{2,1,0:T(8,128)(2,1)S(1)} collective-permute-done((bf16[8,32,128]{2,1,0:T(8,128)(2,1)S(1)}, bf16[8,32,128]{2,1,0:T(8,128)(2,1)S(1)}, u32[]{:S(2)}, u32[]{:S(2)}) %collective-permute-start.2) | collective-permute-done | bytes 65568 | tf_op jit(solution)/shard_map/ppermute | solution.py:355
  29.1 1.1 %shard_map.71 = (f32[32,64,128]{2,1,0:T(8,128)}, bf16[1,32,32,32]{3,2,1,0:T(8,128)(2,1)}) custom-call(bf16[9,32,128]{2,1,0:T(8,128)(2,1)S(1)} %get-tuple-element.9.packet.own0.own, bf16[8,32,128]{2,1,0:T(8,128)(2,1)S(1)} %get-tuple-element.11.cut_own, bf16[8,32,128]{2,1,0:T(8,128)(2,1)S(1)} %collective-permute-done.2.cut_next, ...), custom_call_target="tpu_custom_call" | custom-call | flops 1000000 | bytes 2000000 | tf_op jit(solution)/shard_map/pallas_call | solution.py:301
Async XLA Ops:
  0.6 23.7 %collective-permute-start.1 = (f32[32,64,128]{2,1,0:T(8,128)}, f32[32,64,128]{2,1,0:T(8,128)S(1)}, u32[]{:S(2)}, u32[]{:S(2)}) collective-permute-start(f32[32,64,128]{2,1,0:T(8,128)} %v_hbm.1), channel_id=1, source_target_pairs={{0,1},{1,0},{2,3},{3,2},{4,5},{5,4},{6,7},{7,6},{8,9},{9,8},{10,11... | collective-permute-start | bytes 3145736 | tf_op jit(solution)/shard_map/ppermute | solution.py:345
  2.6 14.5 %copy-start = (s32[2,3]{1,0:T(2,128)S(1)}, s32[2,3]{1,0:T(2,128)}, u32[]{:S(2)}) copy-start(s32[2,3]{1,0:T(2,128)} %offs_hbm.1) | copy-start | bytes 76
  2.6 8.7 %collective-permute-start.6 = (bf16[9,32,128]{2,1,0:T(8,128)(2,1)S(1)}, bf16[9,32,128]{2,1,0:T(8,128)(2,1)S(1)}, u32[]{:S(2)}, u32[]{:S(2)}) collective-permute-start(bf16[9,32,128]{2,1,0:T(8,128)(2,1)S(1)} %get-tuple-element.9.packet.own0.own), channel_id=1, source_target_pairs={{2,0},{4,2},{6,4},{8,6},{10,8},{12,10},{14,12},{16,14},{18,16},{20... | collective-permute-start | bytes 221192 | tf_op jit(solution)/shard_map/ppermute | solution.py:344
  9.1 8.0 %collective-permute-start.3 = (bf16[9,32,128]{2,1,0:T(8,128)(2,1)S(1)}, bf16[9,32,128]{2,1,0:T(8,128)(2,1)S(1)}, u32[]{:S(2)}, u32[]{:S(2)}) collective-permute-start(bf16[9,32,128]{2,1,0:T(8,128)(2,1)S(1)} %get-tuple-element.9.packet.own0.own), channel_id=1, source_target_pairs={{0,2},{2,4},{4,6},{6,8},{8,10},{10,12},{12,14},{14,16},{16,18},{18... | collective-permute-start | bytes 221192 | tf_op jit(solution)/shard_map/ppermute | solution.py:343
  9.1 15.7 %collective-permute-start.5 = (bf16[9,32,128]{2,1,0:T(8,128)(2,1)S(1)}, bf16[9,32,128]{2,1,0:T(8,128)(2,1)S(1)}, u32[]{:S(2)}, u32[]{:S(2)}) collective-permute-start(bf16[9,32,128]{2,1,0:T(8,128)(2,1)S(1)} %get-tuple-element.9.packet.own0.own), channel_id=1, source_target_pairs={{0,1},{1,0},{2,3},{3,2},{4,5},{5,4},{6,7},{7,6},{8,9},{9,8},{10,11... | collective-permute-start | bytes 221192 | tf_op jit(solution)/shard_map/ppermute | solution.py:346
  11.3 13.5 %collective-permute-start.7 = (bf16[9,32,128]{2,1,0:T(8,128)(2,1)S(1)}, bf16[9,32,128]{2,1,0:T(8,128)(2,1)S(1)}, u32[]{:S(2)}, u32[]{:S(2)}) collective-permute-start(bf16[9,32,128]{2,1,0:T(8,128)(2,1)S(1)} %collective-permute-done.6.next0), channel_id=1, source_target_pairs={{0,1},{1,0},{2,3},{3,2},{4,5},{5,4},{6,7},{7,6},{8,9},{9,8},{10,11... | collective-permute-start | bytes 221192 | tf_op jit(solution)/shard_map/ppermute | solution.py:357
  17.1 7.7 %collective-permute-start.4 = (bf16[9,32,128]{2,1,0:T(8,128)(2,1)S(1)}, bf16[9,32,128]{2,1,0:T(8,128)(2,1)S(1)}, u32[]{:S(2)}, u32[]{:S(2)}) collective-permute-start(bf16[9,32,128]{2,1,0:T(8,128)(2,1)S(1)} %collective-permute-done.3.prev0), channel_id=1, source_target_pairs={{0,1},{1,0},{2,3},{3,2},{4,5},{5,4},{6,7},{7,6},{8,9},{9,8},{10,11... | collective-permute-start | bytes 221192 | tf_op jit(solution)/shard_map/ppermute | solution.py:356
  17.1 7.2 %collective-permute-start = (s32[2,3]{1,0:T(2,128)S(1)}, s32[2,3]{1,0:T(2,128)S(1)}, u32[]{:S(2)}, u32[]{:S(2)}) collective-permute-start(s32[2,3]{1,0:T(2,128)S(1)} %copy-done), channel_id=1, source_target_pairs={{0,2},{2,4},{4,6},{6,8},{8,10},{10,12},{12,14},{14,16},{16,18},{18... | collective-permute-start | bytes 80 | tf_op jit(solution)/shard_map/ppermute | solution.py:328
  24.7 4.3 %collective-permute-start.2 = (bf16[8,32,128]{2,1,0:T(8,128)(2,1)S(1)}, bf16[8,32,128]{2,1,0:T(8,128)(2,1)S(1)}, u32[]{:S(2)}, u32[]{:S(2)}) collective-permute-start(bf16[8,32,128]{2,1,0:T(8,128)(2,1)S(1)} %get-tuple-element.12), channel_id=1, source_target_pairs={{2,0},{4,2},{6,4},{8,6},{10,8},{12,10},{14,12},{16,14},{18,16},{20... | collective-permute-start | bytes 196616 | tf_op jit(solution)/shard_map/ppermute | solution.py:355

commit v7 on v6

--- a/solution.py
+++ b/solution.py
@@ -81,17 +81,12 @@
     copies[4].wait()
 
 
-def cut_kernel(packet, offs_prev, v_own, v_other, cut_own, cut_prev):
+def cut_window(corner, v_own, v_other, cut):
     side, depth = v_own.shape[0], v_own.shape[1]
     groups = LANES // side
     per = side // groups
     core = lax.axis_index("bricks")
-    meta = packet[packet.shape[0] - 1].astype(F32)
-    line = jnp.where(core == 0, offs_prev[0:1, :], offs_prev[1:2, :])
-    corners = [
-        [meta[axis : axis + 1].astype(I32) for axis in range(3)],
-        [jnp.broadcast_to(line[:, axis : axis + 1], (1, LANES)) for axis in range(3)],
-    ]
+    _, o1, o2 = corner
     lane = iota((side, LANES), 1)
     row = iota((side, LANES), 0)
     fold = jnp.where((lane & (side - 1)) == row, 1.0, 0.0).astype(BF16)
@@ -99,32 +94,41 @@
     for g in range(groups):
         block = fold * jnp.where((lane // side) == g, 1.0, 0.0).astype(BF16)
         folds += [block] * groups
-    folds = jnp.concatenate(folds, 0)
-    for (_, o1, o2), cut in zip(corners, (cut_own, cut_prev)):
-        upper = row < o1
-        mine = ((lane - o2) & (LANES - 1)) < side
-        start = o2 + ((lane - o2) & (LANES - 1))
-        own = mine & ((start // LANES) == core)
-        other = mine & ((start // LANES) != core)
-        high, left, right = [
-            jnp.where(m, 1.0, 0.0).astype(BF16) > 0 for m in (upper, own, other)
-        ]
-        zero = jnp.zeros((side, LANES), BF16)
-        parts = []
-        for g in range(groups):
-            planes = []
-            for x in range(g * per, (g + 1) * per):
-                one, two = [
-                    jnp.where(
-                        high, v[x, depth - side :].astype(BF16), v[x, 0:side].astype(BF16)
-                    )
-                    for v in (v_own, v_other)
-                ]
-                plane = jnp.where(left, one, jnp.where(right, two, zero))
-                planes.append(plane)
-            parts.append(jnp.concatenate(planes, 0))
-        out = jnp.dot(jnp.concatenate(parts, 1), folds, preferred_element_type=F32)
-        cut[...] = out.astype(BF16).reshape(per, side, LANES)
+    start = o2 + ((lane - o2) & (LANES - 1))
+    inside = start - o2 < side
+    own = inside & ((start // LANES) == core)
+    other = inside & ((start // LANES) != core)
+    high, left, right = [
+        jnp.where(m, 1.0, 0.0).astype(BF16) > 0 for m in (row < o1, own, other)
+    ]
+    zero = jnp.zeros((side, LANES), BF16)
+    parts = []
+    for g in range(groups):
+        planes = []
+        for x in range(g * per, (g + 1) * per):
+            one, two = [
+                jnp.where(high, v[x, depth - side :].astype(BF16), v[x, 0:side].astype(BF16))
+                for v in (v_own, v_other)
+            ]
+            planes.append(jnp.where(left, one, jnp.where(right, two, zero)))
+        parts.append(jnp.concatenate(planes, 0))
+    out = jnp.dot(
+        jnp.concatenate(parts, 1), jnp.concatenate(folds, 0), preferred_element_type=F32
+    )
+    cut[...] = out.astype(BF16).reshape(per, side, LANES)
+
+
+def cut_prev_kernel(offs_prev, v_own, v_other, cut):
+    core = lax.axis_index("bricks")
+    line = jnp.where(core == 0, offs_prev[0:1, :], offs_prev[1:2, :])
+    corner = [jnp.broadcast_to(line[:, axis : axis + 1], (1, LANES)) for axis in range(3)]
+    cut_window(corner, v_own, v_other, cut)
+
+
+def cut_own_kernel(packet, v_own, v_other, cut):
+    meta = packet[packet.shape[0] - 1].astype(F32)
+    corner = [meta[axis : axis + 1].astype(I32) for axis in range(3)]
+    cut_window(corner, v_own, v_other, cut)
 
 
 class Tables:
@@ -180,15 +184,21 @@
             high = product.astype(BF16)
             ready[a, i * side : (i + 1) * side, 0:LANES] = high
             ready[a, i * side : (i + 1) * side, LANES:] = (product - high.astype(F32)).astype(BF16)
-    wide = groups * LANES
-    to = iota((LANES, wide), 1)
-    from_lane = iota((LANES, wide), 0)
-    spread = jnp.where(from_lane == (to // LANES) * side + (to & (side - 1)), 1.0, 0.0).astype(BF16)
+    from_lane = iota((side, LANES), 0)
+    fold = jnp.where(from_lane == (iota((side, LANES), 1) & (side - 1)), 1.0, 0.0)
+    empty = jnp.zeros((side, LANES), BF16)
     for a in range(many):
-        inside = jnp.where(z_at[a] == core * LANES + lane, 1.0, 0.0).astype(BF16)
-        place = spread * jnp.concatenate([inside] * groups, 1)
-        out = jnp.dot(ready[a], jnp.concatenate([place] * 2, 0), preferred_element_type=F32)
-        placed[a] = out
+        inside = z_at[a] == core * LANES + lane
+        block = jnp.where(inside, fold, 0.0).astype(BF16)
+        place = jnp.concatenate(
+            [
+                jnp.concatenate([block if h == g else empty for h in range(groups)], 1)
+                for g in range(groups)
+            ]
+            * 2,
+            0,
+        )
+        placed[a] = jnp.dot(ready[a], place, preferred_element_type=F32)
     for g in range(groups):
         for i in range(per):
             x = g * per + i
@@ -344,15 +354,18 @@
     following = lax.ppermute(own, "atoms", down)
     other = lax.ppermute(local_potential, "bricks", swap)
     own_mate = lax.ppermute(own, "bricks", swap)
-    cut_own, cut_prev = call(
-        cut_kernel,
-        (shape((per, side, LANES), BF16),) * 2,
-        (VMEM,) * 2,
-        [VMEM] * 4,
-        (own, offsets_prev, mine, other),
+    cut_prev = call(
+        cut_prev_kernel,
+        shape((per, side, LANES), BF16),
+        VMEM,
+        [VMEM] * 3,
+        (offsets_prev, mine, other),
         [],
     )
     cut_next = lax.ppermute(cut_prev, "atoms", down)
+    cut_own = call(
+        cut_own_kernel, shape((per, side, LANES), BF16), VMEM, [VMEM] * 3, (own, mine, other), []
+    )
     prev_mate = lax.ppermute(prev, "bricks", swap)
     following_mate = lax.ppermute(following, "bricks", swap)
     dens, mixed, bend = call(

time: 30.3 us -> 30.3 us (level)
    pallas_call x4 -> x5, Pallas kernels: 3.97 us -> 4.1 us  [call(): pl.pallas_call(kernel, out_shape=outs, in_specs=ins, out_specs=out_specs,...]
  transfers between devices with their start and end apart: 8 -> 8, of which waited for: 4 -> 4; matrix products, arithmetic and copies ran while one was open for 0% -> 0% of each run, Pallas kernels for 9% -> 10%
where the time goes in v7:
time: 30.3 us; the launch traced here: 30.1 us
  waiting for transfers between devices  18 us (59%)
  starting transfers between devices  7.38 us (24%)
  Pallas kernels  4.1 us (14%)
  between operations  0.71 us (2%)
    ppermute x1, waiting for transfers between devices, step(): offsets_prev = lax.ppermute(offsets, 'atoms', up)  7.16 us
    ppermute x1, starting transfers between devices, step(): following = lax.ppermute(own, 'atoms', down)  6.54 us
    ppermute x1, waiting for transfers between devices, step(): prev = lax.ppermute(own, 'atoms', up)  5.79 us
    pallas_call x5, Pallas kernels, call(): pl.pallas_call(kernel, out_shape=outs, in_specs=ins, out_specs=out_specs,...  4.1 us
    ppermute x1, waiting for transfers between devices, step(): cut_next = lax.ppermute(cut_prev, 'atoms', down)  3.02 us
    ppermute x1, waiting for transfers between devices, step(): following = lax.ppermute(own, 'atoms', down)  1.97 us
  transfers between devices with their start and end apart: 8, of which 4 were waited for; matrix products, arithmetic and copies ran while one was open for 0% of the time, Pallas kernels for 10%

profile of v7, /device:TPU:0, one launch (start us, length us, event | category | flops | bytes accessed | tf_op | source)
XLA Modules:
  0.0 30.1 jit_solution(15720707252306038013)
XLA Ops:
  0.6 0.6 %collective-permute-start = (f32[32,64,128]{2,1,0:T(8,128)}, f32[32,64,128]{2,1,0:T(8,128)S(1)}, u32[]{:S(2)}, u32[]{:S(2)}) collective-permute-start(f32[32,64,128]{2,1,0:T(8,128)} %v_hbm.1), channel_id=1, source_target_pairs={{0,1},{1,0},{2,3},{3,2},{4,5},{5,4},{6,7},{7,6},{8,9},{9,8},{10,11... | collective-permute-start | bytes 3145736 | tf_op jit(solution)/shard_map/ppermute | solution.py:355
  1.2 1.4 %shard_map.68 = (bf16[9,32,128]{2,1,0:T(8,128)(2,1)S(1)}, f32[32,64,128]{2,1,0:T(8,128)S(1)}) custom-call(s32[2,3]{1,0:T(2,128)} %offs_hbm.1, f32[1,6]{1,0:T(1,128)} %kern_hbm.1, s32[1,6]{1,0:T(1,128)} %pat_hbm.1, bf16[2,32,32,32]{3,2,1,0:T(8,128)(2,1)} %orbs_hbm.1, f32[32,64,128]{2,1,0:T(8,128)} %v_hbm.1), custom_call_target="tpu_custom_call" | custom-call | flops 1000000 | bytes 2000000 | tf_op jit(solution)/shard_map/pallas_call | solution.py:311
  2.6 0.0 copy-start
  2.6 6.5 %collective-permute-start.6 = (bf16[9,32,128]{2,1,0:T(8,128)(2,1)S(1)}, bf16[9,32,128]{2,1,0:T(8,128)(2,1)S(1)}, u32[]{:S(2)}, u32[]{:S(2)}) collective-permute-start(bf16[9,32,128]{2,1,0:T(8,128)(2,1)S(1)} %get-tuple-element.7.packet.own0.own), channel_id=1, source_target_pairs={{2,0},{4,2},{6,4},{8,6},{10,8},{12,10},{14,12},{16,14},{18,16},{20... | collective-permute-start | bytes 221192 | tf_op jit(solution)/shard_map/ppermute | solution.py:354
  9.1 0.0 collective-permute-start.3
  9.1 0.2 collective-permute-start.5
  9.4 2.0 %collective-permute-done.6.next0 = bf16[9,32,128]{2,1,0:T(8,128)(2,1)S(1)} collective-permute-done((bf16[9,32,128]{2,1,0:T(8,128)(2,1)S(1)}, bf16[9,32,128]{2,1,0:T(8,128)(2,1)S(1)}, u32[]{:S(2)}, u32[]{:S(2)}) %collective-permute-start.6) | collective-permute-done | bytes 73760 | tf_op jit(solution)/shard_map/ppermute | solution.py:354
  11.3 0.0 collective-permute-start.7
  11.3 5.8 %collective-permute-done.3.prev0 = bf16[9,32,128]{2,1,0:T(8,128)(2,1)S(1)} collective-permute-done((bf16[9,32,128]{2,1,0:T(8,128)(2,1)S(1)}, bf16[9,32,128]{2,1,0:T(8,128)(2,1)S(1)}, u32[]{:S(2)}, u32[]{:S(2)}) %collective-permute-start.3) | collective-permute-done | bytes 73760 | tf_op jit(solution)/shard_map/ppermute | solution.py:353
  17.1 0.0 collective-permute-start.4
  17.1 0.0 copy-done
  17.1 0.0 collective-permute-start.1
  17.1 7.2 %collective-permute-done.1.offs_prev = s32[2,3]{1,0:T(2,128)S(1)} collective-permute-done((s32[2,3]{1,0:T(2,128)S(1)}, s32[2,3]{1,0:T(2,128)S(1)}, u32[]{:S(2)}, u32[]{:S(2)}) %collective-permute-start.1) | collective-permute-done | bytes 56 | tf_op jit(solution)/shard_map/ppermute | solution.py:338
  24.3 0.0 collective-permute-done.v_other
  24.3 0.4 %shard_map.70 = bf16[8,32,128]{2,1,0:T(8,128)(2,1)S(1)} custom-call(s32[2,3]{1,0:T(2,128)S(1)} %collective-permute-done.1.offs_prev, f32[32,64,128]{2,1,0:T(8,128)S(1)} %get-tuple-element.8.v_own, f32[32,64,128]{2,1,0:T(8,128)S(1)} %collective-permute-done.v_other), custom_call_target="tpu_custom_call" | custom-call | flops 1000000 | bytes 2000000 | tf_op jit(solution)/shard_map/pallas_call | solution.py:311
  24.7 0.1 collective-permute-start.2
  24.8 0.0 collective-permute-done.5.own1
  24.8 0.0 collective-permute-done.7.next1
  24.8 0.0 collective-permute-done.4.prev1
  24.8 0.9 %shard_map.71 = (f32[32,64,128]{2,1,0:T(8,128)S(1)}, f32[8,32,128]{2,1,0:T(8,128)S(1)}, f32[8,32,128]{2,1,0:T(8,128)S(1)}) custom-call(bf16[9,32,128]{2,1,0:T(8,128)(2,1)S(1)} %collective-permute-done.3.prev0, bf16[9,32,128]{2,1,0:T(8,128)(2,1)S(1)} %collective-permute-done.4.prev1, bf16[9,32,128]{2,1,0:T(8,128)(2,1)S(1)} %get-tuple-element.7.packet.own0.own, ...), custom_call_target="tpu_custom_call" | custom-call | flops 1000000 | bytes 2000000 | tf_op jit(solution)/shard_map/pallas_call | solution.py:311
  25.7 0.2 shard_map.69.cut_own
  26.0 3.0 %collective-permute-done.2.cut_next = bf16[8,32,128]{2,1,0:T(8,128)(2,1)S(1)} collective-permute-done((bf16[8,32,128]{2,1,0:T(8,128)(2,1)S(1)}, bf16[8,32,128]{2,1,0:T(8,128)(2,1)S(1)}, u32[]{:S(2)}, u32[]{:S(2)}) %collective-permute-start.2) | collective-permute-done | bytes 65568 | tf_op jit(solution)/shard_map/ppermute | solution.py:365
  29.0 1.1 %shard_map.72 = (f32[32,64,128]{2,1,0:T(8,128)}, bf16[1,32,32,32]{3,2,1,0:T(8,128)(2,1)}) custom-call(bf16[9,32,128]{2,1,0:T(8,128)(2,1)S(1)} %get-tuple-element.7.packet.own0.own, bf16[8,32,128]{2,1,0:T(8,128)(2,1)S(1)} %shard_map.69.cut_own, bf16[8,32,128]{2,1,0:T(8,128)(2,1)S(1)} %collective-permute-done.2.cut_next, ...), custom_call_target="tpu_custom_call" | custom-call | flops 1000000 | bytes 2000000 | tf_op jit(solution)/shard_map/pallas_call | solution.py:311
Async XLA Ops:
  0.6 23.7 %collective-permute-start = (f32[32,64,128]{2,1,0:T(8,128)}, f32[32,64,128]{2,1,0:T(8,128)S(1)}, u32[]{:S(2)}, u32[]{:S(2)}) collective-permute-start(f32[32,64,128]{2,1,0:T(8,128)} %v_hbm.1), channel_id=1, source_target_pairs={{0,1},{1,0},{2,3},{3,2},{4,5},{5,4},{6,7},{7,6},{8,9},{9,8},{10,11... | collective-permute-start | bytes 3145736 | tf_op jit(solution)/shard_map/ppermute | solution.py:355
  2.6 14.5 %copy-start = (s32[2,3]{1,0:T(2,128)S(1)}, s32[2,3]{1,0:T(2,128)}, u32[]{:S(2)}) copy-start(s32[2,3]{1,0:T(2,128)} %offs_hbm.1) | copy-start | bytes 76
  2.6 8.7 %collective-permute-start.6 = (bf16[9,32,128]{2,1,0:T(8,128)(2,1)S(1)}, bf16[9,32,128]{2,1,0:T(8,128)(2,1)S(1)}, u32[]{:S(2)}, u32[]{:S(2)}) collective-permute-start(bf16[9,32,128]{2,1,0:T(8,128)(2,1)S(1)} %get-tuple-element.7.packet.own0.own), channel_id=1, source_target_pairs={{2,0},{4,2},{6,4},{8,6},{10,8},{12,10},{14,12},{16,14},{18,16},{20... | collective-permute-start | bytes 221192 | tf_op jit(solution)/shard_map/ppermute | solution.py:354
  9.1 8.0 %collective-permute-start.3 = (bf16[9,32,128]{2,1,0:T(8,128)(2,1)S(1)}, bf16[9,32,128]{2,1,0:T(8,128)(2,1)S(1)}, u32[]{:S(2)}, u32[]{:S(2)}) collective-permute-start(bf16[9,32,128]{2,1,0:T(8,128)(2,1)S(1)} %get-tuple-element.7.packet.own0.own), channel_id=1, source_target_pairs={{0,2},{2,4},{4,6},{6,8},{8,10},{10,12},{12,14},{14,16},{16,18},{18... | collective-permute-start | bytes 221192 | tf_op jit(solution)/shard_map/ppermute | solution.py:353
  9.1 15.6 %collective-permute-start.5 = (bf16[9,32,128]{2,1,0:T(8,128)(2,1)S(1)}, bf16[9,32,128]{2,1,0:T(8,128)(2,1)S(1)}, u32[]{:S(2)}, u32[]{:S(2)}) collective-permute-start(bf16[9,32,128]{2,1,0:T(8,128)(2,1)S(1)} %get-tuple-element.7.packet.own0.own), channel_id=1, source_target_pairs={{0,1},{1,0},{2,3},{3,2},{4,5},{5,4},{6,7},{7,6},{8,9},{9,8},{10,11... | collective-permute-start | bytes 221192 | tf_op jit(solution)/shard_map/ppermute | solution.py:356
  11.3 13.4 %collective-permute-start.7 = (bf16[9,32,128]{2,1,0:T(8,128)(2,1)S(1)}, bf16[9,32,128]{2,1,0:T(8,128)(2,1)S(1)}, u32[]{:S(2)}, u32[]{:S(2)}) collective-permute-start(bf16[9,32,128]{2,1,0:T(8,128)(2,1)S(1)} %collective-permute-done.6.next0), channel_id=1, source_target_pairs={{0,1},{1,0},{2,3},{3,2},{4,5},{5,4},{6,7},{7,6},{8,9},{9,8},{10,11... | collective-permute-start | bytes 221192 | tf_op jit(solution)/shard_map/ppermute | solution.py:370
  17.1 7.7 %collective-permute-start.4 = (bf16[9,32,128]{2,1,0:T(8,128)(2,1)S(1)}, bf16[9,32,128]{2,1,0:T(8,128)(2,1)S(1)}, u32[]{:S(2)}, u32[]{:S(2)}) collective-permute-start(bf16[9,32,128]{2,1,0:T(8,128)(2,1)S(1)} %collective-permute-done.3.prev0), channel_id=1, source_target_pairs={{0,1},{1,0},{2,3},{3,2},{4,5},{5,4},{6,7},{7,6},{8,9},{9,8},{10,11... | collective-permute-start | bytes 221192 | tf_op jit(solution)/shard_map/ppermute | solution.py:369
  17.1 7.2 %collective-permute-start.1 = (s32[2,3]{1,0:T(2,128)S(1)}, s32[2,3]{1,0:T(2,128)S(1)}, u32[]{:S(2)}, u32[]{:S(2)}) collective-permute-start(s32[2,3]{1,0:T(2,128)S(1)} %copy-done), channel_id=1, source_target_pairs={{0,2},{2,4},{4,6},{6,8},{8,10},{10,12},{12,14},{14,16},{16,18},{18... | collective-permute-start | bytes 80 | tf_op jit(solution)/shard_map/ppermute | solution.py:338
  24.7 4.3 %collective-permute-start.2 = (bf16[8,32,128]{2,1,0:T(8,128)(2,1)S(1)}, bf16[8,32,128]{2,1,0:T(8,128)(2,1)S(1)}, u32[]{:S(2)}, u32[]{:S(2)}) collective-permute-start(bf16[8,32,128]{2,1,0:T(8,128)(2,1)S(1)} %shard_map.70), channel_id=1, source_target_pairs={{2,0},{4,2},{6,4},{8,6},{10,8},{12,10},{14,12},{16,14},{18,16},{20... | collective-permute-start | bytes 196616 | tf_op jit(solution)/shard_map/ppermute | solution.py:365
